TPU v7x, 128 devices: a whole 4x4x4 slice. The times are simulated.
128 devices in a mesh: lon: 16 (over z_hi, y, core), lat: 8 (over x, z_lo).
Axes of the slice: x: 4, y: 4, z: 4 (z_hi: 2, z_lo: 2; z = z_hi * 2 + z_lo), core: 2. Of those that a mesh axis runs over, the one named last changes fastest.
Arguments:
- temp: float32 [4, 512, 12288], P(None, 'lat', 'lon'), may hold values from -6 to 6
- salt: float32 [4, 512, 12288], P(None, 'lat', 'lon'), may hold values from -6 to 6
- uvel: float32 [4, 512, 12288], P(None, 'lat', 'lon'), may hold values from -6 to 6
- vvel: float32 [4, 512, 12288], P(None, 'lat', 'lon'), may hold values from -6 to 6
- thick: float32 [4, 512, 12288], P(None, 'lat', 'lon'), may hold values from 0.5 to 2
- land: int32 [4, 512, 12288], P(None, 'lat', 'lon'), may hold values 0 or 1
- east_width: float32 [512, 12288], P('lat', 'lon'), may hold values from 0.5 to 2
- north_width: float32 [512, 12288], P('lat', 'lon'), may hold values from 0.5 to 2
- coriolis: float32 [512, 12288], P('lat', 'lon'), may hold values from 0.5 to 1.5
Outputs:
- temp_next: float32 [4, 512, 12288], P(None, 'lat', 'lon')
- salt_next: float32 [4, 512, 12288], P(None, 'lat', 'lon')
- uvel_next: float32 [4, 512, 12288], P(None, 'lat', 'lon')
- vvel_next: float32 [4, 512, 12288], P(None, 'lat', 'lon')
All inputs are finite; a program needn't handle non-finite values. No bound on the sum of `land` on one device may be relied on, other than what follows from the above.
Results may differ from a plain program's by a relative error of at most 0.00002.
Values sent between devices are 32-bit elements; how exact they have to be, the bound alone decides.
No kernel may reach another device: no remote copies, remote signals or barrier semaphores. Data moves between devices by JAX's collectives and lax.ppermute only.
A program may use at most 128 MiB of HBM per device.

v0:
```python
import jax
import jax.numpy as jnp
from jax import lax
from jax.sharding import PartitionSpec as P

time_step = 0.2
biharm_coef = 0.02
alpha_temp = 0.2
beta_salt = 0.8
thin_floor = 0.25


def with_halo(cells, sides, width, closed):
    for axis, dim in sides:
        count = lax.axis_size(axis)
        ends = count if closed else count - 1
        head = lax.slice_in_dim(cells, 0, width, axis=dim)
        tail = lax.slice_in_dim(cells, cells.shape[dim] - width, cells.shape[dim], axis=dim)
        cells = jnp.concatenate(
            [
                lax.ppermute(tail, axis, [(i, (i + 1) % count) for i in range(ends)]),
                cells,
                lax.ppermute(head, axis, [((i + 1) % count, i) for i in range(ends)]),
            ],
            axis=dim,
        )
    return cells


def partner(shard, axis, bit):
    return lax.ppermute(shard, axis, [(i, i ^ 1 << bit) for i in range(lax.axis_size(axis))])


def laplace(field, east_coef, north_coef, volume):
    east_diff = east_coef * (field[..., 1:] - field[..., :-1])
    north_diff = north_coef * (field[..., 1:, :] - field[..., :-1, :])
    return (
        east_diff[..., 1:-1, 1:]
        - east_diff[..., 1:-1, :-1]
        + north_diff[..., 1:, 1:-1]
        - north_diff[..., :-1, 1:-1]
    ) / volume


def advance_level(
    fields, depth_ext, east_ext, north_ext, overhead, wet_cells, coriolis, east_width, north_width
):
    lon_thick = jnp.minimum(depth_ext[:, :-1], depth_ext[:, 1:])
    lat_thick = jnp.minimum(depth_ext[:-1], depth_ext[1:])
    east_coef = (
        lon_thick * (north_ext[:, :-1] + north_ext[:, 1:]) / (east_ext[:, :-1] + east_ext[:, 1:])
    )
    north_coef = lat_thick * (east_ext[:-1] + east_ext[1:]) / (north_ext[:-1] + north_ext[1:])
    volume = east_ext * north_ext * jnp.maximum(depth_ext, thin_floor)
    cycle_lap = laplace(fields, east_coef, north_coef, volume[1:-1, 1:-1])
    biharmonic = laplace(
        cycle_lap, east_coef[1:-1, 1:-1], north_coef[1:-1, 1:-1], volume[2:-2, 2:-2]
    )
    transport_east = (
        lon_thick
        * (north_ext[:, :-1] + north_ext[:, 1:])
        * (fields[2][:, :-1] + fields[2][:, 1:])
        / 4.0
    )
    transport_north = (
        lat_thick * (east_ext[:-1] + east_ext[1:]) * (fields[3][:-1] + fields[3][1:]) / 4.0
    )
    tracers = fields[:2]
    flux_east = transport_east * (tracers[..., :-1] + tracers[..., 1:]) / 2.0
    flux_north = transport_north * (tracers[..., :-1, :] + tracers[..., 1:, :]) / 2.0
    advect = (
        flux_east[..., 2:-2, 2:-1]
        - flux_east[..., 2:-2, 1:-2]
        + flux_north[..., 2:-1, 2:-2]
        - flux_north[..., 1:-2, 2:-2]
    ) / volume[2:-2, 2:-2]
    buoyancy = (beta_salt * fields[1] - alpha_temp * fields[0]) * depth_ext
    pressure = overhead + 0.5 * buoyancy
    overhead = overhead + buoyancy
    grad_east = (pressure[2:-2, 3:-1] - pressure[2:-2, 1:-3]) / (2.0 * east_width)
    grad_north = (pressure[3:-1, 2:-2] - pressure[1:-3, 2:-2]) / (2.0 * north_width)
    interior = fields[:, 2:-2, 2:-2]
    temp_out = wet_cells * (interior[0] - time_step * advect[0] - biharm_coef * biharmonic[0])
    salt_out = wet_cells * (interior[1] - time_step * advect[1] - biharm_coef * biharmonic[1])
    uvel_out = wet_cells * (
        interior[2] + time_step * (coriolis * interior[3] - grad_east) - biharm_coef * biharmonic[2]
    )
    vvel_out = wet_cells * (
        interior[3]
        + time_step * (-coriolis * interior[2] - grad_north)
        - biharm_coef * biharmonic[3]
    )
    return ((temp_out, salt_out, uvel_out, vvel_out), overhead)


def lat_rim(stacked):
    return with_halo(stacked, (("lat", 1),), 2, False)


def lon_rim(stacked):
    return with_halo(stacked, (("lon", 2),), 2, True)


def fold_ghost(top_rows, sign_list):
    mirror = top_rows
    for bit_number in range(lax.axis_size("lon").bit_length() - 1):
        mirror = partner(mirror, "lon", bit_number)
    mirror = mirror[..., ::-1]
    mirror = mirror * sign_list[:, None, None]
    return jnp.stack([mirror[:, 1], mirror[:, 0]], axis=1)


def extend_local(stacked, sign_list):
    on_top = lax.axis_index("lat") == lax.axis_size("lat") - 1
    tall_stack = lat_rim(stacked)
    ghost_rows = fold_ghost(stacked[:, -3:, :], sign_list)
    north_rows = jnp.where(on_top, ghost_rows, tall_stack[:, -2:, :])
    tall_stack = jnp.concatenate([tall_stack[:, :-2, :], north_rows], axis=1)
    return lon_rim(tall_stack)


def shards(temp, salt, uvel, vvel, thick, land, east_width, north_width, coriolis):
    level_count = temp.shape[0]
    depth = land.astype(jnp.float32) * thick
    stacked = jnp.concatenate(
        [temp, salt, uvel, vvel, depth, east_width[None], north_width[None]], axis=0
    )
    sign_list = jnp.concatenate(
        [
            jnp.ones((2 * level_count,), jnp.float32),
            -jnp.ones((2 * level_count,), jnp.float32),
            jnp.ones((level_count + 2,), jnp.float32),
        ]
    )
    extended = extend_local(stacked, sign_list)
    row_ids = lax.broadcasted_iota(jnp.int32, extended[0].shape, 0)
    southern = jnp.logical_and(lax.axis_index("lat") == 0, row_ids < 2)
    east_ext = jnp.where(southern, 1.0, extended[5 * level_count])
    north_ext = jnp.where(southern, 1.0, extended[5 * level_count + 1])
    overhead = jnp.zeros_like(east_ext)
    results = []
    for level_index in range(level_count):
        fields = jnp.stack(
            [
                extended[level_index],
                extended[level_count + level_index],
                extended[2 * level_count + level_index],
                extended[3 * level_count + level_index],
            ]
        )
        outputs, overhead = advance_level(
            fields,
            extended[4 * level_count + level_index],
            east_ext,
            north_ext,
            overhead,
            land[level_index].astype(jnp.float32),
            coriolis,
            east_width,
            north_width,
        )
        results.append(outputs)
    return (
        jnp.stack([r[0] for r in results]),
        jnp.stack([r[1] for r in results]),
        jnp.stack([r[2] for r in results]),
        jnp.stack([r[3] for r in results]),
    )


def solution(mesh):
    in_specs = (
        P(None, "lat", "lon"),
        P(None, "lat", "lon"),
        P(None, "lat", "lon"),
        P(None, "lat", "lon"),
        P(None, "lat", "lon"),
        P(None, "lat", "lon"),
        P("lat", "lon"),
        P("lat", "lon"),
        P("lat", "lon"),
    )
    out_specs = (
        P(None, "lat", "lon"),
        P(None, "lat", "lon"),
        P(None, "lat", "lon"),
        P(None, "lat", "lon"),
    )
    return jax.shard_map(shards, mesh=mesh, in_specs=in_specs, out_specs=out_specs, check_vma=False)
```

profile of v0, /device:TPU:2, one launch (start us, length us, event | category | flops | bytes accessed | tf_op | source)
XLA Modules:
  0.0 79.5 jit_solution(11693046833762361849)
XLA Ops:
  0.7 1.3 %constant_dynamic-update-slice_fusion.3 = f32[22,64,768]{2,1,0:T(8,128)S(1)} fusion(f32[4,64,768]{2,1,0:T(8,128)} %param.9), kind=kLoop, calls=%fused_computation.365 | loop fusion | bytes 1572864
  2.0 1.2 %constant_dynamic-update-slice_fusion.2 = f32[22,64,768]{2,1,0:T(8,128)S(1)} fusion(f32[22,64,768]{2,1,0:T(8,128)S(1)} %constant_dynamic-update-slice_fusion.3, f32[4,64,768]{2,1,0:T(8,128)} %param.10), kind=kLoop, calls=%fused_computation.364 | loop fusion | bytes 1572864
  3.3 1.2 %constant_dynamic-update-slice_fusion.1 = f32[22,64,768]{2,1,0:T(8,128)S(1)} fusion(f32[22,64,768]{2,1,0:T(8,128)S(1)} %constant_dynamic-update-slice_fusion.2, f32[4,64,768]{2,1,0:T(8,128)} %param.11), kind=kLoop, calls=%fused_computation.363 | loop fusion | bytes 1572864
  4.9 1.5 %collective-permute-done.1 = f32[22,3,768]{2,0,1:T(8,128)S(1)} collective-permute-done((f32[22,3,768]{2,0,1:T(8,128)S(1)}, f32[22,3,768]{2,0,1:T(8,128)S(1)}, u32[]{:S(2)}, u32[]{:S(2)}) %collective-permute-start.1) | collective-permute-done | bytes 202784 | tf_op jit(solution)/shard_map/ppermute | solution.py:31
  6.4 1.6 %collective-permute-start.2 = (f32[22,3,768]{2,0,1:T(8,128)S(1)}, f32[22,3,768]{2,0,1:T(8,128)S(1)}, u32[]{:S(2)}, u32[]{:S(2)}) collective-permute-start(f32[22,3,768]{2,0,1:T(8,128)S(1)} %collective-permute-done.1), channel_id=1, source_target_pairs={{0,16},{8,24},{16,0},{24,8},{32,48},{40,56},{48,32},{56,40},{64,80... | collective-permute-start | bytes 608264 | tf_op jit(solution)/shard_map/ppermute | solution.py:31
  8.0 5.9 %collective-permute-done.2 = f32[22,3,768]{2,0,1:T(8,128)S(1)} collective-permute-done((f32[22,3,768]{2,0,1:T(8,128)S(1)}, f32[22,3,768]{2,0,1:T(8,128)S(1)}, u32[]{:S(2)}, u32[]{:S(2)}) %collective-permute-start.2) | collective-permute-done | bytes 202784 | tf_op jit(solution)/shard_map/ppermute | solution.py:31
  13.9 3.2 %collective-permute-start.3 = (f32[22,3,768]{2,0,1:T(8,128)S(1)}, f32[22,3,768]{2,0,1:T(8,128)S(1)}, u32[]{:S(2)}, u32[]{:S(2)}) collective-permute-start(f32[22,3,768]{2,0,1:T(8,128)S(1)} %collective-permute-done.2), channel_id=1, source_target_pairs={{0,32},{8,40},{16,48},{24,56},{32,0},{40,8},{48,16},{56,24},{64,96... | collective-permute-start | bytes 608264 | tf_op jit(solution)/shard_map/ppermute | solution.py:31
  17.1 5.0 %collective-permute-done.3 = f32[22,3,768]{2,0,1:T(8,128)S(1)} collective-permute-done((f32[22,3,768]{2,0,1:T(8,128)S(1)}, f32[22,3,768]{2,0,1:T(8,128)S(1)}, u32[]{:S(2)}, u32[]{:S(2)}) %collective-permute-start.3) | collective-permute-done | bytes 202784 | tf_op jit(solution)/shard_map/ppermute | solution.py:31
  22.0 3.9 %collective-permute-start.4 = (f32[22,3,768]{2,0,1:T(8,128)S(1)}, f32[22,3,768]{2,0,1:T(8,128)S(1)}, u32[]{:S(2)}, u32[]{:S(2)}) collective-permute-start(f32[22,3,768]{2,0,1:T(8,128)S(1)} %collective-permute-done.3), channel_id=1, source_target_pairs={{0,64},{8,72},{16,80},{24,88},{32,96},{40,104},{48,112},{56,120},{... | collective-permute-start | bytes 608264 | tf_op jit(solution)/shard_map/ppermute | solution.py:31
  26.0 2.9 %collective-permute-start = (f32[22,2,768]{2,1,0:T(2,128)S(1)}, f32[22,2,768]{2,1,0:T(2,128)S(1)}, u32[]{:S(2)}, u32[]{:S(2)}) collective-permute-start(f32[22,2,768]{2,1,0:T(2,128)S(1)} %get-tuple-element.70), channel_id=1, source_target_pairs={{0,1},{1,2},{2,3},{3,4},{4,5},{5,6},{6,7},{8,9},{9,10},{10,11},{11... | collective-permute-start | bytes 405512 | tf_op jit(solution)/shard_map/ppermute | solution.py:21
  28.9 3.8 %collective-permute-start.5 = (f32[22,2,768]{2,1,0:T(2,128)S(1)}, f32[22,2,768]{2,1,0:T(2,128)S(1)}, u32[]{:S(2)}, u32[]{:S(2)}) collective-permute-start(f32[22,2,768]{2,1,0:T(2,128)S(1)} %get-tuple-element.71), channel_id=1, source_target_pairs={{1,0},{2,1},{3,2},{4,3},{5,4},{6,5},{7,6},{9,8},{10,9},{11,10},{12... | collective-permute-start | bytes 405512 | tf_op jit(solution)/shard_map/ppermute | solution.py:23
  32.8 0.5 rev.3
  33.5 3.1 %collective-permute-done.5 = f32[22,2,768]{2,1,0:T(2,128)S(1)} collective-permute-done((f32[22,2,768]{2,1,0:T(2,128)S(1)}, f32[22,2,768]{2,1,0:T(2,128)S(1)}, u32[]{:S(2)}, u32[]{:S(2)}) %collective-permute-start.5) | collective-permute-done | bytes 135200 | tf_op jit(solution)/shard_map/ppermute | solution.py:23
  36.8 1.7 %pad_maximum_fusion.7 = (f32[22,68,2]{2,1,0:T(8,128)S(1)}, f32[22,68,2]{2,1,0:T(8,128)S(1)}) fusion(f32[22,2,768]{2,1,0:T(2,128)S(1)} %maximum_select_fusion, f32[22,64,768]{2,1,0:T(8,128)} %copy-done, f32[22,2,768]{2,1,0:T(2,128)S(1)} %collective-permute-done), kind=kLoop, calls=%fused_computation.55 | loop fusion | flops 11968 | bytes 4619648 | tf_op jit(solution)/shard_map/slice | solution.py:18
  39.1 2.4 %collective-permute-start.7 = (f32[22,68,2]{1,2,0:T(2,128)S(1)}, f32[22,68,2]{1,2,0:T(2,128)S(1)}, u32[]{:S(2)}, u32[]{:S(2)}) collective-permute-start(f32[22,68,2]{1,2,0:T(2,128)S(1)} %copy.56), channel_id=1, source_target_pairs={{8,0},{16,8},{24,16},{32,24},{40,32},{48,40},{56,48},{64,56},{72,6... | collective-permute-start | bytes 35912 | tf_op jit(solution)/shard_map/ppermute | solution.py:23
  41.6 6.8 %collective-permute-done.6 = f32[22,68,2]{1,2,0:T(2,128)S(1)} collective-permute-done((f32[22,68,2]{1,2,0:T(2,128)S(1)}, f32[22,68,2]{1,2,0:T(2,128)S(1)}, u32[]{:S(2)}, u32[]{:S(2)}) %collective-permute-start.6) | collective-permute-done | bytes 12000 | tf_op jit(solution)/shard_map/ppermute | solution.py:21
  48.4 0.4 copy.57
  48.8 0.4 copy.58
  49.2 5.5 %pad_maximum_fusion = f32[22,68,772]{2,1,0:T(8,128)S(1)} fusion(f32[22,68,2]{2,1,0:T(8,128)S(1)} %copy.58, f32[22,2,768]{2,1,0:T(2,128)S(1)} %maximum_select_fusion, f32[22,64,768]{2,1,0:T(8,128)} %copy-done, f32[22,2,768]{2,1,0:T(2,128)S(1)} %collective-permute-done, f32[22,68,2]{2,1,0:T(8,128)S(1)} %copy.57), kind=kLoop, calls=%fused_computation | loop fusion | flops 4619648 | bytes 9239296 | tf_op jit(solution)/shard_map/concatenate | solution.py:19
  57.4 0.4 fusion.188
  58.7 0.4 fusion.86
  59.4 0.4 fusion.14
  60.4 0.3 fusion.9
  61.6 1.0 %fusion.17 = f32[4,66,770]{2,1,0:T(8,128)S(1)} fusion(f32[4,67,772]{2,1,0:T(8,128)S(1)} %fusion.18, f32[4,68,771]{2,1,0:T(8,128)S(1)} %fusion.19, f32[66,770]{1,0:T(8,128)S(1)} %slice.1209), kind=kLoop, calls=%fused_computation.42 | loop fusion | flops 813120 | bytes 4268880 | tf_op jit(solution)/shard_map/div | solution.py:37
  62.6 0.3 fusion.16
  63.1 1.0 %fusion.12 = f32[4,66,770]{2,1,0:T(8,128)S(1)} fusion(f32[4,67,772]{2,1,0:T(8,128)S(1)} %fusion.13, f32[4,68,771]{2,1,0:T(8,128)S(1)} %fusion.14, f32[66,770]{1,0:T(8,128)S(1)} %slice.1254), kind=kLoop, calls=%fused_computation.30 | loop fusion | flops 813120 | bytes 4268880 | tf_op jit(solution)/shard_map/div | solution.py:37
  64.1 0.3 fusion.11
  64.6 1.0 %fusion.7 = f32[4,66,770]{2,1,0:T(8,128)S(1)} fusion(f32[4,67,772]{2,1,0:T(8,128)S(1)} %fusion.8, f32[4,68,771]{2,1,0:T(8,128)S(1)} %fusion.9, f32[66,770]{1,0:T(8,128)S(1)} %slice.1299), kind=kLoop, calls=%fused_computation.18 | loop fusion | flops 813120 | bytes 4268880 | tf_op jit(solution)/shard_map/div | solution.py:37
  66.0 1.0 %fusion.2 = f32[4,66,770]{2,1,0:T(8,128)S(1)} fusion(f32[4,67,772]{2,1,0:T(8,128)S(1)} %fusion.3, f32[4,68,771]{2,1,0:T(8,128)S(1)} %fusion.4, f32[66,770]{1,0:T(8,128)S(1)} %slice.1344), kind=kLoop, calls=%fused_computation.6 | loop fusion | flops 813120 | bytes 4268880 | tf_op jit(solution)/shard_map/div | solution.py:37
  67.0 0.3 fusion.1
  67.5 0.6 fusion.49
  68.5 0.5 fusion.63
  69.0 0.7 fusion.23
  69.8 0.5 fusion.62
  70.3 0.7 fusion.22
  71.1 0.3 fusion.127
  71.4 0.4 fusion.119
  72.0 0.4 fusion.31
  72.3 0.5 fusion.61
  72.8 0.7 fusion.21
  73.6 0.4 fusion.111
  73.9 0.5 fusion.60
  74.4 0.7 fusion.20
  75.2 0.3 fusion.103
  75.7 0.9 %pad_maximum_fusion.11 = f32[4,64,768]{2,1,0:T(8,128)} fusion(f32[1,64,768]{2,1,0:T(8,128)S(1)} %get-tuple-element.78, f32[1,64,768]{2,1,0:T(8,128)S(1)} %get-tuple-element.76, f32[1,64,768]{2,1,0:T(8,128)S(1)} %get-tuple-element.74, f32[1,64,768]{2,1,0:T(8,128)S(1)} %get-tuple-element.72), kind=kLoop, calls=%fused_computation.75 | loop fusion | flops 589824 | bytes 1572864 | tf_op jit(solution)/shard_map/stack | solution.py:167
  76.7 0.9 %pad_maximum_fusion.9 = f32[4,64,768]{2,1,0:T(8,128)} fusion(f32[1,64,768]{2,1,0:T(8,128)S(1)} %get-tuple-element.88, f32[1,64,768]{2,1,0:T(8,128)S(1)} %get-tuple-element.91, f32[1,64,768]{2,1,0:T(8,128)S(1)} %get-tuple-element.82, f32[1,64,768]{2,1,0:T(8,128)S(1)} %get-tuple-element.85), kind=kLoop, calls=%fused_computation.73 | loop fusion | flops 589824 | bytes 1572864 | tf_op jit(solution)/shard_map/stack | solution.py:165
  77.6 0.9 %pad_maximum_fusion.10 = f32[4,64,768]{2,1,0:T(8,128)} fusion(f32[1,64,768]{2,1,0:T(8,128)S(1)} %get-tuple-element.79, f32[1,64,768]{2,1,0:T(8,128)S(1)} %get-tuple-element.77, f32[1,64,768]{2,1,0:T(8,128)S(1)} %get-tuple-element.75, f32[1,64,768]{2,1,0:T(8,128)S(1)} %get-tuple-element.73), kind=kLoop, calls=%fused_computation.74 | loop fusion | flops 589824 | bytes 1572864 | tf_op jit(solution)/shard_map/stack | solution.py:166
  78.5 0.9 %pad_maximum_fusion.8 = f32[4,64,768]{2,1,0:T(8,128)} fusion(f32[1,64,768]{2,1,0:T(8,128)S(1)} %get-tuple-element.89, f32[1,64,768]{2,1,0:T(8,128)S(1)} %get-tuple-element.90, f32[1,64,768]{2,1,0:T(8,128)S(1)} %get-tuple-element.83, f32[1,64,768]{2,1,0:T(8,128)S(1)} %get-tuple-element.84), kind=kLoop, calls=%fused_computation.72 | loop fusion | flops 589824 | bytes 1572864 | tf_op jit(solution)/shard_map/stack | solution.py:164
  (86 shorter events, 8.6 us)
Async XLA Ops:
  0.6 3.8 %copy-start.7 = (f32[4,64,768]{2,1,0:T(8,128)S(1)}, f32[4,64,768]{2,1,0:T(8,128)}, u32[]{:S(2)}) copy-start(f32[4,64,768]{2,1,0:T(8,128)} %param.12) | copy-start | bytes 2359300
  0.6 3.9 %copy-start.1 = (s32[4,64,768]{2,1,0:T(8,128)S(1)}, s32[4,64,768]{2,1,0:T(8,128)}, u32[]{:S(2)}) copy-start(s32[4,64,768]{2,1,0:T(8,128)} %param.14) | copy-start | bytes 2359300
  0.7 3.9 %copy-start.10 = (f32[4,64,768]{2,1,0:T(8,128)S(1)}, f32[4,64,768]{2,1,0:T(8,128)}, u32[]{:S(2)}) copy-start(f32[4,64,768]{2,1,0:T(8,128)} %param.13) | copy-start | bytes 2359300
  0.7 4.0 %copy-start.2 = (f32[64,768]{1,0:T(8,128)S(1)}, f32[64,768]{1,0:T(8,128)}, u32[]{:S(2)}) copy-start(f32[64,768]{1,0:T(8,128)} %param.15) | copy-start | bytes 589828
  0.7 4.0 %copy-start.3 = (f32[64,768]{1,0:T(8,128)S(1)}, f32[64,768]{1,0:T(8,128)}, u32[]{:S(2)}) copy-start(f32[64,768]{1,0:T(8,128)} %param.16) | copy-start | bytes 589828
  3.2 30.0 %copy-start.11 = (f32[22]{0:T(128)S(1)}, f32[22]{0:T(128)}, u32[]{:S(2)}) copy-start(f32[22]{0:T(128)} %constant.38.clone.1) | copy-start | bytes 268
  4.7 21.2 %copy-start = (f32[22,64,768]{2,1,0:T(8,128)}, f32[22,64,768]{2,1,0:T(8,128)S(1)}, u32[]{:S(2)}) copy-start(f32[22,64,768]{2,1,0:T(8,128)S(1)} %bitcast_dynamic-update-slice_fusion) | copy-start | bytes 12976132
  4.8 1.6 %collective-permute-start.1 = (f32[22,3,768]{2,0,1:T(8,128)S(1)}, f32[22,3,768]{2,0,1:T(8,128)S(1)}, u32[]{:S(2)}, u32[]{:S(2)}) collective-permute-start(f32[22,3,768]{2,0,1:T(8,128)S(1)} %copy.52), channel_id=1, source_target_pairs={{0,8},{8,0},{16,24},{24,16},{32,40},{40,32},{48,56},{56,48},{64,72... | collective-permute-start | bytes 608264 | tf_op jit(solution)/shard_map/ppermute | solution.py:31
  6.4 7.5 %collective-permute-start.2 = (f32[22,3,768]{2,0,1:T(8,128)S(1)}, f32[22,3,768]{2,0,1:T(8,128)S(1)}, u32[]{:S(2)}, u32[]{:S(2)}) collective-permute-start(f32[22,3,768]{2,0,1:T(8,128)S(1)} %collective-permute-done.1), channel_id=1, source_target_pairs={{0,16},{8,24},{16,0},{24,8},{32,48},{40,56},{48,32},{56,40},{64,80... | collective-permute-start | bytes 608264 | tf_op jit(solution)/shard_map/ppermute | solution.py:31
  13.9 8.1 %collective-permute-start.3 = (f32[22,3,768]{2,0,1:T(8,128)S(1)}, f32[22,3,768]{2,0,1:T(8,128)S(1)}, u32[]{:S(2)}, u32[]{:S(2)}) collective-permute-start(f32[22,3,768]{2,0,1:T(8,128)S(1)} %collective-permute-done.2), channel_id=1, source_target_pairs={{0,32},{8,40},{16,48},{24,56},{32,0},{40,8},{48,16},{56,24},{64,96... | collective-permute-start | bytes 608264 | tf_op jit(solution)/shard_map/ppermute | solution.py:31
  22.0 10.7 %collective-permute-start.4 = (f32[22,3,768]{2,0,1:T(8,128)S(1)}, f32[22,3,768]{2,0,1:T(8,128)S(1)}, u32[]{:S(2)}, u32[]{:S(2)}) collective-permute-start(f32[22,3,768]{2,0,1:T(8,128)S(1)} %collective-permute-done.3), channel_id=1, source_target_pairs={{0,64},{8,72},{16,80},{24,88},{32,96},{40,104},{48,112},{56,120},{... | collective-permute-start | bytes 608264 | tf_op jit(solution)/shard_map/ppermute | solution.py:31
  26.0 10.8 %collective-permute-start = (f32[22,2,768]{2,1,0:T(2,128)S(1)}, f32[22,2,768]{2,1,0:T(2,128)S(1)}, u32[]{:S(2)}, u32[]{:S(2)}) collective-permute-start(f32[22,2,768]{2,1,0:T(2,128)S(1)} %get-tuple-element.70), channel_id=1, source_target_pairs={{0,1},{1,2},{2,3},{3,4},{4,5},{5,6},{6,7},{8,9},{9,10},{10,11},{11... | collective-permute-start | bytes 405512 | tf_op jit(solution)/shard_map/ppermute | solution.py:21
  28.9 7.7 %collective-permute-start.5 = (f32[22,2,768]{2,1,0:T(2,128)S(1)}, f32[22,2,768]{2,1,0:T(2,128)S(1)}, u32[]{:S(2)}, u32[]{:S(2)}) collective-permute-start(f32[22,2,768]{2,1,0:T(2,128)S(1)} %get-tuple-element.71), channel_id=1, source_target_pairs={{1,0},{2,1},{3,2},{4,3},{5,4},{6,5},{7,6},{9,8},{10,9},{11,10},{12... | collective-permute-start | bytes 405512 | tf_op jit(solution)/shard_map/ppermute | solution.py:23
  39.1 9.7 %collective-permute-start.7 = (f32[22,68,2]{1,2,0:T(2,128)S(1)}, f32[22,68,2]{1,2,0:T(2,128)S(1)}, u32[]{:S(2)}, u32[]{:S(2)}) collective-permute-start(f32[22,68,2]{1,2,0:T(2,128)S(1)} %copy.56), channel_id=1, source_target_pairs={{8,0},{16,8},{24,16},{32,24},{40,32},{48,40},{56,48},{64,56},{72,6... | collective-permute-start | bytes 35912 | tf_op jit(solution)/shard_map/ppermute | solution.py:23
  41.5 6.8 %collective-permute-start.6 = (f32[22,68,2]{1,2,0:T(2,128)S(1)}, f32[22,68,2]{1,2,0:T(2,128)S(1)}, u32[]{:S(2)}, u32[]{:S(2)}) collective-permute-start(f32[22,68,2]{1,2,0:T(2,128)S(1)} %copy.55), channel_id=1, source_target_pairs={{0,8},{8,16},{16,24},{24,32},{32,40},{40,48},{48,56},{56,64},{64,7... | collective-permute-start | bytes 35912 | tf_op jit(solution)/shard_map/ppermute | solution.py:21
  69.0 2.0 %copy-start.6 = (f32[4,64,768]{2,1,0:T(8,128)S(1)}, f32[4,64,768]{2,1,0:T(8,128)}, u32[]{:S(2)}) copy-start(f32[4,64,768]{2,1,0:T(8,128)} %param.11) | copy-start | bytes 2359300
  69.0 2.0 %copy-start.8 = (f32[4,64,768]{2,1,0:T(8,128)S(1)}, f32[4,64,768]{2,1,0:T(8,128)}, u32[]{:S(2)}) copy-start(f32[4,64,768]{2,1,0:T(8,128)} %param.12) | copy-start | bytes 2359300
  69.0 2.0 %copy-start.9 = (f32[64,768]{1,0:T(8,128)S(1)}, f32[64,768]{1,0:T(8,128)}, u32[]{:S(2)}) copy-start(f32[64,768]{1,0:T(8,128)} %param.17) | copy-start | bytes 589828
  70.3 1.5 %copy-start.4 = (f32[4,64,768]{2,1,0:T(8,128)S(1)}, f32[4,64,768]{2,1,0:T(8,128)}, u32[]{:S(2)}) copy-start(f32[4,64,768]{2,1,0:T(8,128)} %param.9) | copy-start | bytes 2359300
  70.3 1.5 %copy-start.5 = (f32[4,64,768]{2,1,0:T(8,128)S(1)}, f32[4,64,768]{2,1,0:T(8,128)}, u32[]{:S(2)}) copy-start(f32[4,64,768]{2,1,0:T(8,128)} %param.10) | copy-start | bytes 2359300
where the time goes:
time: 79.7 us; the launch traced here: 79.5 us
  other arithmetic  29.4 us (37%)
  waiting for transfers between devices  22.2 us (28%)
  starting transfers between devices  17.9 us (22%)
  local copies, waits for them, and re-layouts  8.61 us (11%)
  between operations  1.37 us (2%)
    ppermute x4, waiting for transfers between devices, partner(): lax.ppermute(shard, axis, [(i, i ^ 1 << bit) for i in range(lax.axis_size...  12.3 us
    ppermute x4, starting transfers between devices, partner(): lax.ppermute(shard, axis, [(i, i ^ 1 << bit) for i in range(lax.axis_size...  8.73 us
    ppermute x2, waiting for transfers between devices, with_halo(): lax.ppermute(tail, axis, [(i, (i + 1) % count) for i in range(ends)])  6.84 us
    div x8, other arithmetic, laplace(): (east_diff[..., 1:-1, 1:] - east_diff[..., 1:-1, :-1] + north_diff[..., 1...  6.82 us
    ppermute x2, starting transfers between devices, with_halo(): lax.ppermute(head, axis, [((i + 1) % count, i) for i in range(ends)])  6.23 us
    concatenate x1, other arithmetic, with_halo(): jnp.concatenate([lax.ppermute(tail, axis, [(i, (i + 1) % count) for i in...  5.46 us
    unnamed x29, local copies, waits for them, and re-layouts  3.87 us
    ppermute x2, waiting for transfers between devices, with_halo(): lax.ppermute(head, axis, [((i + 1) % count, i) for i in range(ends)])  3.07 us
  transfers between devices with their start and end apart: 8, of which 5 were waited for; matrix products, arithmetic and copies ran while one was open for 2% of the time, Pallas kernels for 0%

commit v1 on v0

v1 whole, which is shorter than its diff:
```python
import jax
import jax.numpy as jnp
from jax import lax
from jax.experimental import pallas as pl
from jax.experimental.pallas import tpu as pltpu
from jax.sharding import PartitionSpec as P

time_step = 0.2
biharm_coef = 0.02
alpha_temp = 0.2
beta_salt = 0.8
thin_floor = 0.25

LEVELS = 4
ROWS = 64
COLS = 768
TILE = 128
WIDE = COLS + TILE
TALL = ROWS + 16
FIELDS = 22
F32 = jnp.float32
PARAMS = pltpu.CompilerParams(vmem_limit_bytes=56 * 1024 * 1024)
AXES = ("lon", "lat")


def place(lat, lon, lats, lons):
    return (lon % lons) * lats + lat


def both(pairs):
    return [p for a, b in pairs for p in ((a, b), (b, a))]


def lat_pairs(lats, lons, bit):
    pairs = [
        (place(i, j, lats, lons), place(i + 1, j, lats, lons))
        for i in range(bit, lats - 1, 2)
        for j in range(lons)
    ]
    if bit:
        pairs += [
            (place(lats - 1, j, lats, lons), place(lats - 1, lons - 1 - j, lats, lons))
            for j in range(lons // 2)
        ]
    return both(pairs)


def lon_pairs(lats, lons, bit):
    return both(
        [
            (place(i, j, lats, lons), place(i, j + 1, lats, lons))
            for i in range(lats)
            for j in range(bit, lons, 2)
        ]
    )


def rows_kernel(*refs):
    low, high, (near_ref, far_ref), stage = refs[:8], refs[8:16], refs[16:18], refs[18]
    lat = lax.axis_index("lat")
    odd = lat % 2 == 1
    top = lat == lax.axis_size("lat") - 1

    def gather(group, take, dst):
        for kind in range(5):
            for level in range(LEVELS):
                if kind < 4:
                    cells = group[kind][level]
                else:
                    cells = group[4][level] * group[5][level].astype(F32)
                for k, row in enumerate(take):
                    dst[k, kind * LEVELS + level : kind * LEVELS + level + 1, :] = cells[row : row + 1]
        for k, row in enumerate(take):
            dst[k, 20:21, :] = group[6][row : row + 1, :]
            dst[k, 21:22, :] = group[7][row : row + 1, :]

    @pl.when(odd)
    def _():
        gather(low, (0, 1), near_ref)

        @pl.when(jnp.logical_not(top))
        def _():
            gather(high, (6, 7), far_ref)

        @pl.when(top)
        def _():
            gather(high, (6, 5), stage)
            kind_row = lax.broadcasted_iota(jnp.int32, (24, TILE), 0)
            turned = jnp.logical_and(kind_row >= 2 * LEVELS, kind_row < 4 * LEVELS)
            sign = jnp.where(turned, -1.0, 1.0).astype(F32)
            flip = TILE - 1 - lax.broadcasted_iota(jnp.int32, (24, TILE), 1)
            for k in range(2):
                for t in range(COLS // TILE):
                    src = stage[k, :, COLS - TILE * (t + 1) : COLS - TILE * t]
                    rev = jnp.take_along_axis(src, flip, axis=1, mode="promise_in_bounds")
                    far_ref[k, :, TILE * t : TILE * (t + 1)] = rev * sign

    @pl.when(jnp.logical_not(odd))
    def _():
        gather(high, (6, 7), near_ref)
        gather(low, (0, 1), far_ref)


def pack_rows(arrays):
    def spec(a, at):
        if a.ndim == 3:
            return pl.BlockSpec((LEVELS, 8, COLS), lambda i: (0, at, 0))
        return pl.BlockSpec((8, COLS), lambda i: (at, 0))

    whole = pl.BlockSpec((2, 24, COLS), lambda i: (0, 0, 0))
    shape = jax.ShapeDtypeStruct((2, 24, COLS), F32)
    return pl.pallas_call(
        rows_kernel,
        grid=(1,),
        in_specs=[spec(a, 0) for a in arrays] + [spec(a, ROWS // 8 - 1) for a in arrays],
        out_specs=[whole, whole],
        out_shape=[shape, shape],
        scratch_shapes=[pltpu.VMEM((2, 24, COLS), F32)],
        compiler_params=PARAMS,
        name="pack_rows",
    )(*arrays, *arrays)


def ghost_rows(near, far, odd, at_south):
    south = jnp.where(odd, near, far)
    north = jnp.where(odd, far, near)
    kind_row = lax.broadcasted_iota(jnp.int32, south.shape, south.ndim - 2)
    south = jnp.where(jnp.logical_and(at_south, kind_row >= 20), 1.0, south)
    return south, north


def columns_kernel(*refs):
    west, east, near_ref, far_ref, out_ref = refs[:8], refs[8:16], refs[16], refs[17], refs[18]
    lat = lax.axis_index("lat")
    lane = lax.broadcasted_iota(jnp.int32, (ROWS, TILE), 1)
    packed = jnp.zeros((ROWS, TILE), F32)

    def edge(group, kind, level):
        if kind < 4:
            return group[kind][level]
        if kind == 4:
            return group[4][level] * group[5][level].astype(F32)
        return group[6 + level][...]

    for f in range(FIELDS):
        kind, level = divmod(f, LEVELS)
        cells = jnp.where(lane < TILE // 2, edge(west, kind, level), edge(east, kind, level))
        if f:
            cells = pltpu.roll(cells, 4 * f, 1)
        mine = ((lane + 2) & (TILE - 1)) >> 2 == f
        packed = jnp.where(mine, cells, packed)
    out_ref[0:ROWS, :] = packed

    small = lax.broadcasted_iota(jnp.int32, (24, TILE), 1)
    kind_row = lax.broadcasted_iota(jnp.int32, (24, TILE), 0)
    mine = ((small + 2) & (TILE - 1)) >> 2 == kind_row
    for side in range(2):
        for k in range(2):
            parts = []
            for cut in (slice(0, TILE), slice(COLS - TILE, COLS)):
                parts.append(
                    ghost_rows(near_ref[k, :, cut], far_ref[k, :, cut], lat % 2 == 1, lat == 0)[1 - side]
                )
            cells = jnp.where(small < TILE // 2, parts[0], parts[1])
            cells = pltpu.roll(cells, 0, 1, stride=4, stride_axis=0)
            row = jnp.sum(jnp.where(mine, cells, 0.0), axis=0, keepdims=True)
            at = ROWS + 2 * side + k
            out_ref[at : at + 1, :] = row
    out_ref[ROWS + 4 : ROWS + 8, :] = jnp.zeros((4, TILE), F32)


def pack_columns(arrays, near, far):
    def spec(a, at):
        if a.ndim == 3:
            return pl.BlockSpec((LEVELS, ROWS, TILE), lambda i: (0, 0, at))
        return pl.BlockSpec((ROWS, TILE), lambda i: (0, at))

    whole = pl.BlockSpec((2, 24, COLS), lambda i: (0, 0, 0))
    return pl.pallas_call(
        columns_kernel,
        grid=(1,),
        in_specs=[spec(a, 0) for a in arrays]
        + [spec(a, COLS // TILE - 1) for a in arrays]
        + [whole, whole],
        out_specs=pl.BlockSpec((ROWS + 8, TILE), lambda i: (0, 0)),
        out_shape=jax.ShapeDtypeStruct((ROWS + 8, TILE), F32),
        compiler_params=PARAMS,
        name="pack_columns",
    )(*arrays, *arrays, near, far)


def to_east(x):
    return pltpu.roll(x, x.shape[1] - 1, 1)


def to_west(x, by=1):
    return pltpu.roll(x, by, 1)


def step_kernel(
    temp, salt, uvel, vvel, thick, land, ewid, nwid, cori, near, far, lon_even, lon_odd,
    temp_out, salt_out, uvel_out, vvel_out,
    ext, wid, side, ratio_e, ratio_n, span_e, span_n, inv_area,
    coef_e, coef_n, inv_vol, move_n, flux_t, flux_s, lap, pres, slope, over, over_e,
):
    level = pl.program_id(0)
    lat, lon = lax.axis_index("lat"), lax.axis_index("lon")
    lat_odd, lon_is_odd = lat % 2 == 1, lon % 2 == 1

    def fill(dst, f, load):
        shift = (TILE - 4 * f) % TILE if isinstance(f, int) else (TILE - 4 * f) & (TILE - 1)
        for c in range(ROWS // 8):
            dst[8 + 8 * c : 16 + 8 * c, 0:COLS] = load(8 * c)
            dst[8 + 8 * c : 16 + 8 * c, COLS:WIDE] = pltpu.roll(side[8 * c : 8 * c + 8, :], shift, 1)
        south, north = [], []
        for k in range(2):
            a = near[k, pl.ds(f, 1), :]
            b = far[k, pl.ds(f, 1), :]
            s = jnp.where(lat_odd, a, b)
            if isinstance(f, int) and f >= 20:
                s = jnp.where(lat == 0, 1.0, s)
            south.append(s)
            north.append(jnp.where(lat_odd, b, a))
        corner = pltpu.roll(side[ROWS : ROWS + 8, :], shift, 1)
        dst[72:74, 0:COLS] = jnp.concatenate(north, axis=0)
        dst[6:8, 0:COLS] = jnp.concatenate(south, axis=0)
        dst[72:74, COLS:WIDE] = corner[0:2]
        dst[6:8, COLS:WIDE] = corner[2:4]

    @pl.when(level == 0)
    def _():
        lane = lax.broadcasted_iota(jnp.int32, (ROWS + 8, TILE), 1)
        a, b = lon_even[...], lon_odd[...]
        from_east = jnp.where(lon_is_odd, b, a)
        from_west = jnp.where(lon_is_odd, a, b)
        side[...] = jnp.where((lane & 3) < 2, from_east, from_west)
        fill(wid.at[0], 20, lambda r: ewid[r : r + 8, :])
        fill(wid.at[1], 21, lambda r: nwid[r : r + 8, :])
        for c in range(10):
            r = 6 + 8 * c if c < 9 else 71
            e, n = wid[0, r : r + 8, :], wid[1, r : r + 8, :]
            ee, ne = to_east(e), to_east(n)
            en, nn = wid[0, r + 1 : r + 9, :], wid[1, r + 1 : r + 9, :]
            ratio_e[r : r + 8, :] = (n + ne) / (e + ee)
            ratio_n[r : r + 8, :] = (e + en) / (n + nn)
            span_e[r : r + 8, :] = (1.25 * time_step / 0.2 * 0.02 / biharm_coef) * (n + ne)
            span_n[r : r + 8, :] = (1.25 * time_step / 0.2 * 0.02 / biharm_coef) * (e + en)
            inv_area[r : r + 8, :] = 1.0 / (e * n)
            over[r : r + 8, :] = jnp.zeros((8, WIDE), F32)
            over_e[r : r + 8, :] = jnp.zeros((8, WIDE), F32)

    fill(ext.at[0], level, lambda r: temp[0, r : r + 8, :])
    fill(ext.at[1], LEVELS + level, lambda r: salt[0, r : r + 8, :])
    fill(ext.at[2], 2 * LEVELS + level, lambda r: uvel[0, r : r + 8, :])
    fill(ext.at[3], 3 * LEVELS + level, lambda r: vvel[0, r : r + 8, :])
    fill(ext.at[4], 4 * LEVELS + level, lambda r: thick[0, r : r + 8, :] * land[0, r : r + 8, :].astype(F32))

    for c in range(9):
        r = 7 + 8 * c
        here, above, below = slice(r, r + 8), slice(r + 1, r + 9), slice(r - 1, r + 7)
        d, dn, ds = ext[4, here, :], ext[4, above, :], ext[4, below, :]
        de = to_east(d)
        lon_thick = jnp.minimum(d, de)
        lat_thick = jnp.minimum(d, dn)
        ce = lon_thick * ratio_e[here, :]
        cn = lat_thick * ratio_n[here, :]
        cs = jnp.minimum(ds, d) * ratio_n[below, :]
        iv = inv_area[here, :] / jnp.maximum(d, thin_floor)
        coef_e[here, :] = ce
        coef_n[here, :] = cn
        inv_vol[here, :] = iv
        east = []
        for f in range(4):
            q, qn, qs = ext[f, here, :], ext[f, above, :], ext[f, below, :]
            qe = to_east(q)
            fe = ce * (qe - q)
            lap[f, here, :] = (fe - to_west(fe) + cn * (qn - q) - cs * (q - qs)) * iv
            if f < 3:
                east.append(qe)
            if f == 2:
                te = lon_thick * span_e[here, :] * (q + qe)
                flux_t[here, :] = te * (ext[0, here, :] + east[0])
                flux_s[here, :] = te * (ext[1, here, :] + east[1])
                be = (beta_salt * east[1] - alpha_temp * east[0]) * de
                pe = over_e[here, :] + 0.5 * be
                over_e[here, :] = over_e[here, :] + be
                slope[here, :] = pe - to_west(pe, 2)
            if f == 3:
                move_n[here, :] = lat_thick * span_n[here, :] * (q + qn)
        b = (beta_salt * ext[1, here, :] - alpha_temp * ext[0, here, :]) * d
        pres[here, :] = over[here, :] + 0.5 * b
        over[here, :] = over[here, :] + b

    for c in range(ROWS // 8):
        r = 8 + 8 * c
        here, above, below = slice(r, r + 8), slice(r + 1, r + 9), slice(r - 1, r + 7)
        own = slice(8 * c, 8 * c + 8)
        ce, cn, cs = coef_e[here, :], coef_n[here, 0:COLS], coef_n[below, 0:COLS]
        iv = biharm_coef * inv_vol[here, 0:COLS]
        wet = land[0, own, :].astype(F32)

        def tendency(f, extra=None):
            m = lap[f, here, :]
            fe = ce * (to_east(m) - m)
            if extra is not None:
                fe = fe + extra[here, :]
            zonal = (fe - to_west(fe))[:, 0:COLS]
            m = m[:, 0:COLS]
            return zonal + cn * (lap[f, above, 0:COLS] - m) - cs * (m - lap[f, below, 0:COLS])

        gn, gs = move_n[here, 0:COLS], move_n[below, 0:COLS]
        for f, extra, out in ((0, flux_t, temp_out), (1, flux_s, salt_out)):
            q, qn, qs = ext[f, here, 0:COLS], ext[f, above, 0:COLS], ext[f, below, 0:COLS]
            total = tendency(f, extra) + gn * (q + qn) - gs * (qs + q)
            out[0, own, :] = wet * (q - total * iv)
        u, v = ext[2, here, 0:COLS], ext[3, here, 0:COLS]
        turn = time_step * cori[own, :]
        ge = slope[here, 0:COLS] * (0.5 * time_step) / ewid[own, :]
        gn = (pres[above, 0:COLS] - pres[below, 0:COLS]) * (0.5 * time_step) / nwid[own, :]
        uvel_out[0, own, :] = wet * (u + turn * v - ge - tendency(2) * iv)
        vvel_out[0, own, :] = wet * (v - turn * u - gn - tendency(3) * iv)


def advance(arrays, coriolis, near, far, lon_even, lon_odd):
    by_level = pl.BlockSpec((1, ROWS, COLS), lambda i: (i, 0, 0))
    flat = pl.BlockSpec((ROWS, COLS), lambda i: (0, 0))
    rows = pl.BlockSpec((2, 24, COLS), lambda i: (0, 0, 0))
    cols = pl.BlockSpec((ROWS + 8, TILE), lambda i: (0, 0))
    plane = pltpu.VMEM((TALL, WIDE), F32)
    return pl.pallas_call(
        step_kernel,
        grid=(LEVELS,),
        in_specs=[by_level] * 6 + [flat] * 3 + [rows] * 2 + [cols] * 2,
        out_specs=[by_level] * 4,
        out_shape=[jax.ShapeDtypeStruct((LEVELS, ROWS, COLS), F32)] * 4,
        scratch_shapes=[
            pltpu.VMEM((5, TALL, WIDE), F32),
            pltpu.VMEM((2, TALL, WIDE), F32),
            pltpu.VMEM((ROWS + 8, TILE), F32),
        ]
        + [plane] * 5
        + [plane] * 6
        + [pltpu.VMEM((4, TALL, WIDE), F32)]
        + [plane] * 4,
        compiler_params=PARAMS,
        name="advance",
    )(*arrays, coriolis, near, far, lon_even, lon_odd)


def shards(temp, salt, uvel, vvel, thick, land, east_width, north_width, coriolis):
    lats, lons = lax.axis_size("lat"), lax.axis_size("lon")
    arrays = (temp, salt, uvel, vvel, thick, land, east_width, north_width)
    near, far = pack_rows(arrays)
    near = lax.ppermute(near, AXES, lat_pairs(lats, lons, 0))
    far = lax.ppermute(far, AXES, lat_pairs(lats, lons, 1))
    packed = pack_columns(arrays, near, far)
    lon_even = lax.ppermute(packed, AXES, lon_pairs(lats, lons, 0))
    lon_odd = lax.ppermute(packed, AXES, lon_pairs(lats, lons, 1))
    return tuple(advance(arrays, coriolis, near, far, lon_even, lon_odd))


def solution(mesh):
    deep, flat = P(None, "lat", "lon"), P("lat", "lon")
    return jax.shard_map(
        shards,
        mesh=mesh,
        in_specs=(deep,) * 6 + (flat,) * 3,
        out_specs=(deep,) * 4,
        check_vma=False,
    )
```

time: 79.7 us -> 54.5 us (0.68)
  the two profiles are of different devices: /device:TPU:2 before, /device:TPU:63 now
where the time goes in v1:
time: 54.5 us; the launch traced here: 54.3 us
  Pallas kernels  30.4 us (56%)
  waiting for transfers between devices  15.5 us (28%)
  starting transfers between devices  5.85 us (11%)
  local copies, waits for them, and re-layouts  1.89 us (3%)
  between operations  0.66 us (1%)
    pallas_call x1, Pallas kernels, advance(): pl.pallas_call(step_kernel, grid=(LEVELS,), in_specs=[by_level] * 6 + [fl...  25.6 us
    ppermute x1, waiting for transfers between devices, shards(): far = lax.ppermute(far, AXES, lat_pairs(lats, lons, 1))  9.08 us
    ppermute x1, waiting for transfers between devices, shards(): lon_odd = lax.ppermute(packed, AXES, lon_pairs(lats, lons, 1))  6.46 us
    ppermute x1, starting transfers between devices, shards(): far = lax.ppermute(far, AXES, lat_pairs(lats, lons, 1))  5.1 us
    pallas_call x1, Pallas kernels, pack_columns(): pl.pallas_call(columns_kernel, grid=(1,), in_specs=[spec(a, 0) for a in a...  2.49 us
    pallas_call x1, Pallas kernels, pack_rows(): pl.pallas_call(rows_kernel, grid=(1,), in_specs=[spec(a, 0) for a in arra...  2.31 us
    unnamed x8, local copies, waits for them, and re-layouts  1.89 us
  transfers between devices with their start and end apart: 4, of which 2 were waited for; matrix products, arithmetic and copies ran while one was open for 0% of the time, Pallas kernels for 0%

profile of v1, /device:TPU:63, one launch (start us, length us, event | category | flops | bytes accessed | tf_op | source)
XLA Modules:
  0.0 54.3 jit_solution(17665936135929528311)
XLA Ops:
  0.6 2.3 %pack_rows.1 = (f32[2,24,768]{2,1,0:T(8,128)}, f32[2,24,768]{2,1,0:T(8,128)}) custom-call(f32[4,64,768]{2,1,0:T(8,128)} %temp.1, f32[4,64,768]{2,1,0:T(8,128)} %salt.1, f32[4,64,768]{2,1,0:T(8,128)} %uvel.1, f32[4,64,768]{2,1,0:T(8,128)} %vvel.1, f32[4,64,768]{2,1,0:T(8,128)} %thick.1, s32[4,64,768]{2,1,0:T(8,128)} %land.1, f32[64,768]{1,0:T(8,128)} %ewid.1, ...), custom_call_target="tpu_custom_call" | custom-call | tf_op jit(solution)/shard_map/pack_rows/pallas_call | solution.py:112
  2.9 0.0 collective-permute-start
  2.9 5.1 %collective-permute-start.1 = (f32[2,24,768]{2,1,0:T(8,128)}, f32[2,24,768]{2,1,0:T(8,128)S(1)}, u32[]{:S(2)}, u32[]{:S(2)}) collective-permute-start(f32[2,24,768]{2,1,0:T(8,128)} %get-tuple-element.7), channel_id=1, source_target_pairs={{1,2},{2,1},{9,10},{10,9},{17,18},{18,17},{25,26},{26,25},{33,34},... | collective-permute-start | bytes 442376 | tf_op jit(solution)/shard_map/ppermute | solution.py:355
  8.1 0.0 collective-permute-done.refs_16_.near
  8.1 0.0 copy-start
  8.1 9.1 %collective-permute-done.1.refs_17_.far = f32[2,24,768]{2,1,0:T(8,128)S(1)} collective-permute-done((f32[2,24,768]{2,1,0:T(8,128)}, f32[2,24,768]{2,1,0:T(8,128)S(1)}, u32[]{:S(2)}, u32[]{:S(2)}) %collective-permute-start.1) | collective-permute-done | bytes 147488 | tf_op jit(solution)/shard_map/ppermute | solution.py:355
  17.2 0.0 copy-done
  17.2 0.0 copy-start.1
  17.2 0.7 %copy-done.1 = f32[2,24,768]{2,1,0:T(8,128)} copy-done((f32[2,24,768]{2,1,0:T(8,128)}, f32[2,24,768]{2,1,0:T(8,128)S(1)}, u32[]{:S(2)}) %copy-start.1) | copy-done | bytes 147480
  17.8 2.5 %pack_columns.1 = f32[72,128]{1,0:T(8,128)} custom-call(f32[4,64,768]{2,1,0:T(8,128)} %temp.1, f32[4,64,768]{2,1,0:T(8,128)} %salt.1, f32[4,64,768]{2,1,0:T(8,128)} %uvel.1, f32[4,64,768]{2,1,0:T(8,128)} %vvel.1, f32[4,64,768]{2,1,0:T(8,128)} %thick.1, s32[4,64,768]{2,1,0:T(8,128)} %land.1, f32[64,768]{1,0:T(8,128)} %ewid.1, f32[64,768]{1,0:T(8,128)} %nwid.1, ...), custom_call_target="tpu_custom_call" | custom-call | tf_op jit(solution)/shard_map/pack_columns/pallas_call | solution.py:179
  20.3 0.7 %collective-permute-start.3 = (f32[72,128]{1,0:T(8,128)}, f32[72,128]{1,0:T(8,128)S(1)}, u32[]{:S(2)}, u32[]{:S(2)}) collective-permute-start(f32[72,128]{1,0:T(8,128)} %pack_columns.1), channel_id=1, source_target_pairs={{8,16},{16,8},{24,32},{32,24},{40,48},{48,40},{56,64},{64,56},{72,... | collective-permute-start | bytes 110600 | tf_op jit(solution)/shard_map/ppermute | solution.py:358
  21.0 0.0 collective-permute-start.2
  21.1 6.5 %collective-permute-done.3.lon_odd = f32[72,128]{1,0:T(8,128)S(1)} collective-permute-done((f32[72,128]{1,0:T(8,128)}, f32[72,128]{1,0:T(8,128)S(1)}, u32[]{:S(2)}, u32[]{:S(2)}) %collective-permute-start.3) | collective-permute-done | bytes 36896 | tf_op jit(solution)/shard_map/ppermute | solution.py:358
  27.5 0.0 copy-start.2
  27.5 0.0 collective-permute-done.2.lon_even
  27.5 0.6 %copy-done.2 = f32[72,128]{1,0:T(8,128)} copy-done((f32[72,128]{1,0:T(8,128)}, f32[72,128]{1,0:T(8,128)S(1)}, u32[]{:S(2)}) %copy-start.2) | copy-done | bytes 36888
  28.1 0.0 copy-start.3
  28.1 0.6 %copy-done.3 = f32[72,128]{1,0:T(8,128)} copy-done((f32[72,128]{1,0:T(8,128)}, f32[72,128]{1,0:T(8,128)S(1)}, u32[]{:S(2)}) %copy-start.3) | copy-done | bytes 36888
  28.7 25.6 %advance.1 = (f32[4,64,768]{2,1,0:T(8,128)}, f32[4,64,768]{2,1,0:T(8,128)}, f32[4,64,768]{2,1,0:T(8,128)}, f32[4,64,768]{2,1,0:T(8,128)}) custom-call(f32[4,64,768]{2,1,0:T(8,128)} %temp.1, f32[4,64,768]{2,1,0:T(8,128)} %salt.1, f32[4,64,768]{2,1,0:T(8,128)} %uvel.1, f32[4,64,768]{2,1,0:T(8,128)} %vvel.1, f32[4,64,768]{2,1,0:T(8,128)} %thick.1, ...), custom_call_target="tpu_custom_call" | custom-call | tf_op jit(solution)/shard_map/advance/pallas_call | solution.py:330
Async XLA Ops:
  2.9 5.1 %collective-permute-start = (f32[2,24,768]{2,1,0:T(8,128)}, f32[2,24,768]{2,1,0:T(8,128)S(1)}, u32[]{:S(2)}, u32[]{:S(2)}) collective-permute-start(f32[2,24,768]{2,1,0:T(8,128)} %get-tuple-element.6), channel_id=1, source_target_pairs={{0,1},{1,0},{8,9},{9,8},{16,17},{17,16},{24,25},{25,24},{32,33},{3... | collective-permute-start | bytes 442376 | tf_op jit(solution)/shard_map/ppermute | solution.py:354
  2.9 14.2 %collective-permute-start.1 = (f32[2,24,768]{2,1,0:T(8,128)}, f32[2,24,768]{2,1,0:T(8,128)S(1)}, u32[]{:S(2)}, u32[]{:S(2)}) collective-permute-start(f32[2,24,768]{2,1,0:T(8,128)} %get-tuple-element.7), channel_id=1, source_target_pairs={{1,2},{2,1},{9,10},{10,9},{17,18},{18,17},{25,26},{26,25},{33,34},... | collective-permute-start | bytes 442376 | tf_op jit(solution)/shard_map/ppermute | solution.py:355
  8.1 9.1 %copy-start = (f32[2,24,768]{2,1,0:T(8,128)}, f32[2,24,768]{2,1,0:T(8,128)S(1)}, u32[]{:S(2)}) copy-start(f32[2,24,768]{2,1,0:T(8,128)S(1)} %collective-permute-done.refs_16_.near) | copy-start | bytes 442372
  17.2 0.7 %copy-start.1 = (f32[2,24,768]{2,1,0:T(8,128)}, f32[2,24,768]{2,1,0:T(8,128)S(1)}, u32[]{:S(2)}) copy-start(f32[2,24,768]{2,1,0:T(8,128)S(1)} %collective-permute-done.1.refs_17_.far) | copy-start | bytes 442372
  20.3 7.2 %collective-permute-start.3 = (f32[72,128]{1,0:T(8,128)}, f32[72,128]{1,0:T(8,128)S(1)}, u32[]{:S(2)}, u32[]{:S(2)}) collective-permute-start(f32[72,128]{1,0:T(8,128)} %pack_columns.1), channel_id=1, source_target_pairs={{8,16},{16,8},{24,32},{32,24},{40,48},{48,40},{56,64},{64,56},{72,... | collective-permute-start | bytes 110600 | tf_op jit(solution)/shard_map/ppermute | solution.py:358
  21.0 6.5 %collective-permute-start.2 = (f32[72,128]{1,0:T(8,128)}, f32[72,128]{1,0:T(8,128)S(1)}, u32[]{:S(2)}, u32[]{:S(2)}) collective-permute-start(f32[72,128]{1,0:T(8,128)} %pack_columns.1), channel_id=1, source_target_pairs={{0,8},{8,0},{16,24},{24,16},{32,40},{40,32},{48,56},{56,48},{64,72... | collective-permute-start | bytes 110600 | tf_op jit(solution)/shard_map/ppermute | solution.py:357
  27.5 0.6 %copy-start.2 = (f32[72,128]{1,0:T(8,128)}, f32[72,128]{1,0:T(8,128)S(1)}, u32[]{:S(2)}) copy-start(f32[72,128]{1,0:T(8,128)S(1)} %collective-permute-done.3.lon_odd) | copy-start | bytes 110596
  28.1 0.6 %copy-start.3 = (f32[72,128]{1,0:T(8,128)}, f32[72,128]{1,0:T(8,128)S(1)}, u32[]{:S(2)}) copy-start(f32[72,128]{1,0:T(8,128)S(1)} %collective-permute-done.2.lon_even) | copy-start | bytes 110596

commit v2 on v1

--- a/solution.py
+++ b/solution.py
@@ -10,16 +10,19 @@
 alpha_temp = 0.2
 beta_salt = 0.8
 thin_floor = 0.25
+flux_scale = time_step / 8.0 / biharm_coef
 
 LEVELS = 4
 ROWS = 64
 COLS = 768
 TILE = 128
 WIDE = COLS + TILE
-TALL = ROWS + 16
+MAIN = 16
+TALL = ROWS + 2 * MAIN
 FIELDS = 22
 F32 = jnp.float32
-PARAMS = pltpu.CompilerParams(vmem_limit_bytes=56 * 1024 * 1024)
+PARAMS = pltpu.CompilerParams(vmem_limit_bytes=12 * 1024 * 1024)
+BIG = pltpu.CompilerParams(vmem_limit_bytes=24 * 1024 * 1024)
 AXES = ("lon", "lat")
 
 
@@ -55,6 +58,14 @@
     )
 
 
+def onto_chip(x):
+    return pltpu.with_memory_space_constraint(x, pltpu.VMEM)
+
+
+def off_chip(x):
+    return pltpu.with_memory_space_constraint(x, pltpu.HBM)
+
+
 def rows_kernel(*refs):
     low, high, (near_ref, far_ref), stage = refs[:8], refs[8:16], refs[16:18], refs[18]
     lat = lax.axis_index("lat")
@@ -108,17 +119,17 @@
         return pl.BlockSpec((8, COLS), lambda i: (at, 0))
 
     whole = pl.BlockSpec((2, 24, COLS), lambda i: (0, 0, 0))
-    shape = jax.ShapeDtypeStruct((2, 24, COLS), F32)
+    shape = pltpu.VMEM((2, 24, COLS), F32)
     return pl.pallas_call(
         rows_kernel,
         grid=(1,),
         in_specs=[spec(a, 0) for a in arrays] + [spec(a, ROWS // 8 - 1) for a in arrays],
-        out_specs=[whole, whole],
+        out_specs=[pl.BlockSpec(memory_space=pltpu.VMEM)] * 2,
         out_shape=[shape, shape],
         scratch_shapes=[pltpu.VMEM((2, 24, COLS), F32)],
         compiler_params=PARAMS,
         name="pack_rows",
-    )(*arrays, *arrays)
+    )(*[off_chip(x) for x in (*arrays, *arrays)])
 
 
 def ghost_rows(near, far, odd, at_south):
@@ -181,20 +192,22 @@
         grid=(1,),
         in_specs=[spec(a, 0) for a in arrays]
         + [spec(a, COLS // TILE - 1) for a in arrays]
-        + [whole, whole],
-        out_specs=pl.BlockSpec((ROWS + 8, TILE), lambda i: (0, 0)),
-        out_shape=jax.ShapeDtypeStruct((ROWS + 8, TILE), F32),
+        + [pl.BlockSpec(memory_space=pltpu.VMEM)] * 2,
+        out_specs=pl.BlockSpec(memory_space=pltpu.VMEM),
+        out_shape=pltpu.VMEM((ROWS + 8, TILE), F32),
         compiler_params=PARAMS,
         name="pack_columns",
-    )(*arrays, *arrays, near, far)
-
-
-def to_east(x):
-    return pltpu.roll(x, x.shape[1] - 1, 1)
-
-
-def to_west(x, by=1):
-    return pltpu.roll(x, by, 1)
+    )(*[onto_chip(x) for x in (*arrays, *arrays, near, far)])
+
+
+def north_of(here, above):
+    sub = lax.broadcasted_iota(jnp.int32, here.shape, 0)
+    return pltpu.roll(jnp.where(sub == 0, above, here), 7, 0)
+
+
+def south_of(here, below):
+    sub = lax.broadcasted_iota(jnp.int32, here.shape, 0)
+    return pltpu.roll(jnp.where(sub == 7, below, here), 1, 0)
 
 
 def step_kernel(
@@ -206,12 +219,24 @@
     level = pl.program_id(0)
     lat, lon = lax.axis_index("lat"), lax.axis_index("lon")
     lat_odd, lon_is_odd = lat % 2 == 1, lon % 2 == 1
+    lane = lax.broadcasted_iota(jnp.int32, (8, TILE), 1)
+    first, last = lane == 0, lane == TILE - 1
+
+    def tile(t):
+        return slice(TILE * t, TILE * t + TILE)
+
+    def turn_e(x):
+        return pltpu.roll(x, TILE - 1, 1)
+
+    def turn_w(x):
+        return pltpu.roll(x, 1, 1)
 
     def fill(dst, f, load):
-        shift = (TILE - 4 * f) % TILE if isinstance(f, int) else (TILE - 4 * f) & (TILE - 1)
-        for c in range(ROWS // 8):
-            dst[8 + 8 * c : 16 + 8 * c, 0:COLS] = load(8 * c)
-            dst[8 + 8 * c : 16 + 8 * c, COLS:WIDE] = pltpu.roll(side[8 * c : 8 * c + 8, :], shift, 1)
+        shift = (TILE - 4 * f) & (TILE - 1)
+
+        for r in range(0, ROWS, 8):
+            dst[MAIN + r : MAIN + r + 8, 0:COLS] = load(r)
+            dst[MAIN + r : MAIN + r + 8, COLS:WIDE] = pltpu.roll(side[r : r + 8, :], shift, 1)
         south, north = [], []
         for k in range(2):
             a = near[k, pl.ds(f, 1), :]
@@ -222,115 +247,181 @@
             south.append(s)
             north.append(jnp.where(lat_odd, b, a))
         corner = pltpu.roll(side[ROWS : ROWS + 8, :], shift, 1)
-        dst[72:74, 0:COLS] = jnp.concatenate(north, axis=0)
-        dst[6:8, 0:COLS] = jnp.concatenate(south, axis=0)
-        dst[72:74, COLS:WIDE] = corner[0:2]
-        dst[6:8, COLS:WIDE] = corner[2:4]
+        top, low = MAIN + ROWS, MAIN - 2
+        dst[top : top + 2, 0:COLS] = jnp.concatenate(north, axis=0)
+        dst[low : low + 2, 0:COLS] = jnp.concatenate(south, axis=0)
+        dst[top : top + 2, COLS:WIDE] = corner[0:2]
+        dst[low : low + 2, COLS:WIDE] = corner[2:4]
 
     @pl.when(level == 0)
     def _():
-        lane = lax.broadcasted_iota(jnp.int32, (ROWS + 8, TILE), 1)
+        wide_lane = lax.broadcasted_iota(jnp.int32, (ROWS + 8, TILE), 1)
         a, b = lon_even[...], lon_odd[...]
         from_east = jnp.where(lon_is_odd, b, a)
         from_west = jnp.where(lon_is_odd, a, b)
-        side[...] = jnp.where((lane & 3) < 2, from_east, from_west)
+        side[...] = jnp.where((wide_lane & 3) < 2, from_east, from_west)
         fill(wid.at[0], 20, lambda r: ewid[r : r + 8, :])
         fill(wid.at[1], 21, lambda r: nwid[r : r + 8, :])
-        for c in range(10):
-            r = 6 + 8 * c if c < 9 else 71
-            e, n = wid[0, r : r + 8, :], wid[1, r : r + 8, :]
-            ee, ne = to_east(e), to_east(n)
-            en, nn = wid[0, r + 1 : r + 9, :], wid[1, r + 1 : r + 9, :]
-            ratio_e[r : r + 8, :] = (n + ne) / (e + ee)
-            ratio_n[r : r + 8, :] = (e + en) / (n + nn)
-            span_e[r : r + 8, :] = (1.25 * time_step / 0.2 * 0.02 / biharm_coef) * (n + ne)
-            span_n[r : r + 8, :] = (1.25 * time_step / 0.2 * 0.02 / biharm_coef) * (e + en)
-            inv_area[r : r + 8, :] = 1.0 / (e * n)
-            over[r : r + 8, :] = jnp.zeros((8, WIDE), F32)
-            over_e[r : r + 8, :] = jnp.zeros((8, WIDE), F32)
-
-    fill(ext.at[0], level, lambda r: temp[0, r : r + 8, :])
-    fill(ext.at[1], LEVELS + level, lambda r: salt[0, r : r + 8, :])
-    fill(ext.at[2], 2 * LEVELS + level, lambda r: uvel[0, r : r + 8, :])
-    fill(ext.at[3], 3 * LEVELS + level, lambda r: vvel[0, r : r + 8, :])
-    fill(ext.at[4], 4 * LEVELS + level, lambda r: thick[0, r : r + 8, :] * land[0, r : r + 8, :].astype(F32))
-
-    for c in range(9):
-        r = 7 + 8 * c
-        here, above, below = slice(r, r + 8), slice(r + 1, r + 9), slice(r - 1, r + 7)
-        d, dn, ds = ext[4, here, :], ext[4, above, :], ext[4, below, :]
-        de = to_east(d)
-        lon_thick = jnp.minimum(d, de)
-        lat_thick = jnp.minimum(d, dn)
-        ce = lon_thick * ratio_e[here, :]
-        cn = lat_thick * ratio_n[here, :]
-        cs = jnp.minimum(ds, d) * ratio_n[below, :]
-        iv = inv_area[here, :] / jnp.maximum(d, thin_floor)
-        coef_e[here, :] = ce
-        coef_n[here, :] = cn
-        inv_vol[here, :] = iv
-        east = []
-        for f in range(4):
-            q, qn, qs = ext[f, here, :], ext[f, above, :], ext[f, below, :]
-            qe = to_east(q)
-            fe = ce * (qe - q)
-            lap[f, here, :] = (fe - to_west(fe) + cn * (qn - q) - cs * (q - qs)) * iv
-            if f < 3:
-                east.append(qe)
-            if f == 2:
-                te = lon_thick * span_e[here, :] * (q + qe)
-                flux_t[here, :] = te * (ext[0, here, :] + east[0])
-                flux_s[here, :] = te * (ext[1, here, :] + east[1])
-                be = (beta_salt * east[1] - alpha_temp * east[0]) * de
-                pe = over_e[here, :] + 0.5 * be
-                over_e[here, :] = over_e[here, :] + be
-                slope[here, :] = pe - to_west(pe, 2)
-            if f == 3:
-                move_n[here, :] = lat_thick * span_n[here, :] * (q + qn)
-        b = (beta_salt * ext[1, here, :] - alpha_temp * ext[0, here, :]) * d
-        pres[here, :] = over[here, :] + 0.5 * b
-        over[here, :] = over[here, :] + b
-
-    for c in range(ROWS // 8):
-        r = 8 + 8 * c
-        here, above, below = slice(r, r + 8), slice(r + 1, r + 9), slice(r - 1, r + 7)
-        own = slice(8 * c, 8 * c + 8)
-        ce, cn, cs = coef_e[here, :], coef_n[here, 0:COLS], coef_n[below, 0:COLS]
-        iv = biharm_coef * inv_vol[here, 0:COLS]
-        wet = land[0, own, :].astype(F32)
-
-        def tendency(f, extra=None):
-            m = lap[f, here, :]
-            fe = ce * (to_east(m) - m)
-            if extra is not None:
-                fe = fe + extra[here, :]
-            zonal = (fe - to_west(fe))[:, 0:COLS]
-            m = m[:, 0:COLS]
-            return zonal + cn * (lap[f, above, 0:COLS] - m) - cs * (m - lap[f, below, 0:COLS])
-
-        gn, gs = move_n[here, 0:COLS], move_n[below, 0:COLS]
-        for f, extra, out in ((0, flux_t, temp_out), (1, flux_s, salt_out)):
-            q, qn, qs = ext[f, here, 0:COLS], ext[f, above, 0:COLS], ext[f, below, 0:COLS]
-            total = tendency(f, extra) + gn * (q + qn) - gs * (qs + q)
-            out[0, own, :] = wet * (q - total * iv)
-        u, v = ext[2, here, 0:COLS], ext[3, here, 0:COLS]
-        turn = time_step * cori[own, :]
-        ge = slope[here, 0:COLS] * (0.5 * time_step) / ewid[own, :]
-        gn = (pres[above, 0:COLS] - pres[below, 0:COLS]) * (0.5 * time_step) / nwid[own, :]
-        uvel_out[0, own, :] = wet * (u + turn * v - ge - tendency(2) * iv)
-        vvel_out[0, own, :] = wet * (v - turn * u - gn - tendency(3) * iv)
+
+        def chunk(c, _):
+            r = pl.multiple_of(8 * c + 8, 8)
+            here, above = pl.ds(r, 8), pl.ds(r + 8, 8)
+            for t in range(7):
+                e, n = wid[0, here, tile(t)], wid[1, here, tile(t)]
+                u = (t + 1) % 7
+                ee = jnp.where(last, turn_e(wid[0, here, tile(u)]), turn_e(e))
+                ne = jnp.where(last, turn_e(wid[1, here, tile(u)]), turn_e(n))
+                en = north_of(e, wid[0, above, tile(t)])
+                nn = north_of(n, wid[1, above, tile(t)])
+                ratio_e[here, tile(t)] = (n + ne) / (e + ee)
+                ratio_n[here, tile(t)] = (e + en) / (n + nn)
+                span_e[here, tile(t)] = flux_scale * (n + ne)
+                span_n[here, tile(t)] = flux_scale * (e + en)
+                inv_area[here, tile(t)] = 1.0 / (e * n)
+                over[here, tile(t)] = jnp.zeros((8, TILE), F32)
+                over_e[here, tile(t)] = jnp.zeros((8, TILE), F32)
+            return 0
+
+        lax.fori_loop(0, ROWS // 8 + 2, chunk, 0)
+
+    fill(ext.at[0], level, lambda r: temp[level, r : r + 8, :])
+    fill(ext.at[1], LEVELS + level, lambda r: salt[level, r : r + 8, :])
+    fill(ext.at[2], 2 * LEVELS + level, lambda r: uvel[level, r : r + 8, :])
+    fill(ext.at[3], 3 * LEVELS + level, lambda r: vvel[level, r : r + 8, :])
+    fill(ext.at[4], 4 * LEVELS + level, lambda r: thick[level, r : r + 8, :] * land[level, r : r + 8, :].astype(F32))
+
+    def laps(c, _):
+        r = pl.multiple_of(8 * c + 8, 8)
+        here, above, below = pl.ds(r, 8), pl.ds(r + 8, 8), pl.ds(r - 8, 8)
+
+        def zonal(t, turned):
+            d, rd = turned[4]
+            de_next = ext[4, here, tile((t + 1) % 7)]
+            ahead = [(ext[f, here, tile((t + 1) % 7)],) for f in range(4)] + [(de_next,)]
+            ahead = [(x[0], turn_e(x[0])) for x in ahead]
+            de = jnp.where(last, ahead[4][1], rd)
+            lon_thick = jnp.minimum(d, de)
+            ce = lon_thick * ratio_e[here, tile(t)]
+            east = [jnp.where(last, ahead[f][1], turned[f][1]) for f in range(4)]
+            flux = [ce * (east[f] - turned[f][0]) for f in range(4)]
+            te = lon_thick * span_e[here, tile(t)] * (turned[2][0] + east[2])
+            be = (beta_salt * east[1] - alpha_temp * east[0]) * de
+            return ahead, ce, flux, te, be, east
+
+        start = [(x, turn_e(x)) for x in (ext[f, here, tile(6)] for f in range(5))]
+        at_zero, _, flux6, _, be6, _ = zonal(6, start)
+        pe6 = over_e[here, tile(6)] + 0.5 * be6
+        wrap_flux = [turn_w(x) for x in flux6]
+        wrap_pe = pltpu.roll(pe6, 2, 1)
+        behind, behind_pe, turned = wrap_flux, wrap_pe, at_zero
+        for t in range(7):
+            ahead, ce, flux, te, be, east = zonal(t, turned)
+            if t < 6:
+                turned_flux = [turn_w(x) for x in flux]
+            else:
+                turned_flux = wrap_flux
+            coef_e[here, tile(t)] = ce
+            d = turned[4][0]
+            dn = north_of(d, ext[4, above, tile(t)])
+            ds = south_of(d, ext[4, below, tile(t)])
+            lat_thick = jnp.minimum(d, dn)
+            rn = ratio_n[here, tile(t)]
+            cn = lat_thick * rn
+            cs = jnp.minimum(ds, d) * south_of(rn, ratio_n[below, tile(t)])
+            iv = inv_area[here, tile(t)] / jnp.maximum(d, thin_floor)
+            coef_n[here, tile(t)] = cn
+            inv_vol[here, tile(t)] = iv
+            for f in range(4):
+                q = turned[f][0]
+                qn = north_of(q, ext[f, above, tile(t)])
+                qs = south_of(q, ext[f, below, tile(t)])
+                west = jnp.where(first, behind[f], turned_flux[f])
+                lap[f, here, tile(t)] = (flux[f] - west + cn * (qn - q) - cs * (q - qs)) * iv
+                if f == 3:
+                    move_n[here, tile(t)] = lat_thick * span_n[here, tile(t)] * (q + qn)
+            q0, q1 = turned[0][0], turned[1][0]
+            flux_t[here, tile(t)] = te * (q0 + east[0])
+            flux_s[here, tile(t)] = te * (q1 + east[1])
+            b = (beta_salt * q1 - alpha_temp * q0) * d
+            before = over[here, tile(t)]
+            pres[here, tile(t)] = before + 0.5 * b
+            over[here, tile(t)] = before + b
+            before = over_e[here, tile(t)]
+            over_e[here, tile(t)] = before + be
+            if t < 6:
+                pe = before + 0.5 * be
+                turned_pe = pltpu.roll(pe, 2, 1)
+                slope[here, tile(t)] = pe - jnp.where(lane < 2, behind_pe, turned_pe)
+                behind_pe = turned_pe
+            behind, turned = turned_flux, ahead
+        return 0
+
+    lax.fori_loop(0, ROWS // 8 + 2, laps, 0)
+
+    def finish(c, _):
+        r = pl.multiple_of(MAIN + 8 * c, 8)
+        here, above, below = pl.ds(r, 8), pl.ds(r + 8, 8), pl.ds(r - 8, 8)
+        own = pl.ds(pl.multiple_of(8 * c, 8), 8)
+
+        def zonal(t, turned):
+            ahead = [lap[f, here, tile((t + 1) % 7)] for f in range(4)]
+            ahead = [(x, turn_e(x)) for x in ahead]
+            ce = coef_e[here, tile(t)]
+            flux = [ce * (jnp.where(last, ahead[f][1], turned[f][1]) - turned[f][0]) for f in range(4)]
+            flux[0] = flux[0] + flux_t[here, tile(t)]
+            flux[1] = flux[1] + flux_s[here, tile(t)]
+            return ahead, flux
+
+        start = [(x, turn_e(x)) for x in (lap[f, here, tile(6)] for f in range(4))]
+        turned, flux6 = zonal(6, start)
+        behind = [turn_w(x) for x in flux6]
+        outs = (temp_out, salt_out, uvel_out, vvel_out)
+        for t in range(6):
+            ahead, flux = zonal(t, turned)
+            turned_flux = [turn_w(x) for x in flux]
+            cn = coef_n[here, tile(t)]
+            cs = south_of(cn, coef_n[below, tile(t)])
+            iv = biharm_coef * inv_vol[here, tile(t)]
+            gn = move_n[here, tile(t)]
+            gs = south_of(gn, move_n[below, tile(t)])
+            wet = land[level, own, tile(t)].astype(F32)
+            u, v = ext[2, here, tile(t)], ext[3, here, tile(t)]
+            turning = time_step * cori[own, tile(t)]
+            for f in range(4):
+                m = turned[f][0]
+                mn = north_of(m, lap[f, above, tile(t)])
+                ms = south_of(m, lap[f, below, tile(t)])
+                west = jnp.where(first, behind[f], turned_flux[f])
+                total = flux[f] - west + cn * (mn - m) - cs * (m - ms)
+                if f < 2:
+                    q = ext[f, here, tile(t)]
+                    qn = north_of(q, ext[f, above, tile(t)])
+                    qs = south_of(q, ext[f, below, tile(t)])
+                    total = total + gn * (q + qn) - gs * (qs + q)
+                    outs[f][0, own, tile(t)] = wet * (q - total * iv)
+                elif f == 2:
+                    ge = slope[here, tile(t)] * (0.5 * time_step) / ewid[own, tile(t)]
+                    outs[f][0, own, tile(t)] = wet * (u + turning * v - ge - total * iv)
+                else:
+                    p = pres[here, tile(t)]
+                    pn = north_of(p, pres[above, tile(t)])
+                    ps = south_of(p, pres[below, tile(t)])
+                    gp = (pn - ps) * (0.5 * time_step) / nwid[own, tile(t)]
+                    outs[f][0, own, tile(t)] = wet * (v - turning * u - gp - total * iv)
+            behind, turned = turned_flux, ahead
+        return 0
+
+    lax.fori_loop(0, ROWS // 8, finish, 0)
 
 
 def advance(arrays, coriolis, near, far, lon_even, lon_odd):
     by_level = pl.BlockSpec((1, ROWS, COLS), lambda i: (i, 0, 0))
-    flat = pl.BlockSpec((ROWS, COLS), lambda i: (0, 0))
-    rows = pl.BlockSpec((2, 24, COLS), lambda i: (0, 0, 0))
-    cols = pl.BlockSpec((ROWS + 8, TILE), lambda i: (0, 0))
+    onchip = pl.BlockSpec(memory_space=pltpu.VMEM)
     plane = pltpu.VMEM((TALL, WIDE), F32)
     return pl.pallas_call(
         step_kernel,
         grid=(LEVELS,),
-        in_specs=[by_level] * 6 + [flat] * 3 + [rows] * 2 + [cols] * 2,
+        in_specs=[onchip] * 13,
         out_specs=[by_level] * 4,
         out_shape=[jax.ShapeDtypeStruct((LEVELS, ROWS, COLS), F32)] * 4,
         scratch_shapes=[
@@ -342,9 +433,9 @@
         + [plane] * 6
         + [pltpu.VMEM((4, TALL, WIDE), F32)]
         + [plane] * 4,
-        compiler_params=PARAMS,
+        compiler_params=BIG,
         name="advance",
-    )(*arrays, coriolis, near, far, lon_even, lon_odd)
+    )(*[onto_chip(x) for x in (*arrays, coriolis, near, far, lon_even, lon_odd)])
 
 
 def shards(temp, salt, uvel, vvel, thick, land, east_width, north_width, coriolis):

time: 54.5 us -> 41.8 us (0.77)
  Pallas kernels: 30.4 us -> 19.5 us
  local copies, waits for them, and re-layouts: 1.89 us -> 0.04 us
    pallas_call x1, Pallas kernels: 25.6 us -> 17.6 us  [advance(): pl.pallas_call(step_kernel, grid=(LEVELS,), in_specs=[onchip] * 13, out_s...]
    pallas_call x1, Pallas kernels: 2.49 us -> 0.27 us  [pack_columns(): pl.pallas_call(columns_kernel, grid=(1,), in_specs=[spec(a, 0) for a in a...]
    unnamed x8 -> x18, local copies, waits for them, and re-layouts: 1.89 us -> 0.04 us
    pallas_call x1, Pallas kernels: 2.31 us -> 1.71 us  [pack_rows(): pl.pallas_call(rows_kernel, grid=(1,), in_specs=[spec(a, 0) for a in arra...]
where the time goes in v2:
time: 41.8 us; the launch traced here: 41.6 us
  Pallas kernels  19.5 us (47%)
  waiting for transfers between devices  15.1 us (36%)
  starting transfers between devices  6.14 us (15%)
  between operations  0.79 us (2%)
    pallas_call x1, Pallas kernels, advance(): pl.pallas_call(step_kernel, grid=(LEVELS,), in_specs=[onchip] * 13, out_s...  17.6 us
    ppermute x1, waiting for transfers between devices, shards(): far = lax.ppermute(far, AXES, lat_pairs(lats, lons, 1))  8.89 us
    ppermute x1, waiting for transfers between devices, shards(): lon_odd = lax.ppermute(packed, AXES, lon_pairs(lats, lons, 1))  6.24 us
    ppermute x1, starting transfers between devices, shards(): far = lax.ppermute(far, AXES, lat_pairs(lats, lons, 1))  5.22 us
    pallas_call x1, Pallas kernels, pack_rows(): pl.pallas_call(rows_kernel, grid=(1,), in_specs=[spec(a, 0) for a in arra...  1.71 us
  transfers between devices with their start and end apart: 4, of which 2 were waited for; matrix products, arithmetic and copies ran while one was open for 0% of the time, Pallas kernels for 0%

profile of v2, /device:TPU:63, one launch (start us, length us, event | category | flops | bytes accessed | tf_op | source)
XLA Modules:
  0.0 41.6 jit_solution(15744809335494063635)
XLA Ops:
  0.6 0.0 copy-start.7
  0.6 0.0 copy-start.6
  0.7 0.0 copy-start.5
  0.7 0.0 copy-start.4
  0.7 0.0 copy-start.3
  0.7 0.0 copy-start.2
  0.7 0.0 copy-start.1
  0.7 0.0 copy-start
  0.7 1.7 %pack_rows.1 = (f32[2,24,768]{2,1,0:T(8,128)S(1)}, f32[2,24,768]{2,1,0:T(8,128)S(1)}) custom-call(f32[4,64,768]{2,1,0:T(8,128)} %temp.1, f32[4,64,768]{2,1,0:T(8,128)} %salt.1, f32[4,64,768]{2,1,0:T(8,128)} %uvel.1, f32[4,64,768]{2,1,0:T(8,128)} %vvel.1, f32[4,64,768]{2,1,0:T(8,128)} %thick.1, s32[4,64,768]{2,1,0:T(8,128)} %land.1, f32[64,768]{1,0:T(8,128)} %ewid.1, ...), custom_call_target="tpu_custom_call" | custom-call | tf_op jit(solution)/shard_map/pack_rows/pallas_call | solution.py:123
  2.4 0.1 collective-permute-start
  2.5 0.0 copy-start.8
  2.5 5.2 %collective-permute-start.1 = (f32[2,24,768]{2,1,0:T(8,128)S(1)}, f32[2,24,768]{2,1,0:T(8,128)S(1)}, u32[]{:S(2)}, u32[]{:S(2)}) collective-permute-start(f32[2,24,768]{2,1,0:T(8,128)S(1)} %get-tuple-element.7), channel_id=1, source_target_pairs={{1,2},{2,1},{9,10},{10,9},{17,18},{18,17},{25,26},{26,25},{33,34},... | collective-permute-start | bytes 442376 | tf_op jit(solution)/shard_map/ppermute | solution.py:446
  7.8 0.0 collective-permute-done.refs_16_.near
  7.8 8.9 %collective-permute-done.1.refs_17_.far = f32[2,24,768]{2,1,0:T(8,128)S(1)} collective-permute-done((f32[2,24,768]{2,1,0:T(8,128)S(1)}, f32[2,24,768]{2,1,0:T(8,128)S(1)}, u32[]{:S(2)}, u32[]{:S(2)}) %collective-permute-start.1) | collective-permute-done | bytes 147488 | tf_op jit(solution)/shard_map/ppermute | solution.py:446
  16.7 0.0 copy-done.7
  16.7 0.0 copy-done.6
  16.7 0.0 copy-done.5
  16.7 0.0 copy-done.4
  16.7 0.0 copy-done.3
  16.7 0.0 copy-done.2
  16.7 0.0 copy-done.1
  16.7 0.0 copy-done
  16.7 0.3 pack_columns.1
  17.0 0.8 %collective-permute-start.3 = (f32[72,128]{1,0:T(8,128)S(1)}, f32[72,128]{1,0:T(8,128)S(1)}, u32[]{:S(2)}, u32[]{:S(2)}) collective-permute-start(f32[72,128]{1,0:T(8,128)S(1)} %pack_columns.1), channel_id=1, source_target_pairs={{8,16},{16,8},{24,32},{32,24},{40,48},{48,40},{56,64},{64,56},{72,... | collective-permute-start | bytes 110600 | tf_op jit(solution)/shard_map/ppermute | solution.py:449
  17.8 0.1 collective-permute-start.2
  17.8 6.2 %collective-permute-done.3.lon_odd = f32[72,128]{1,0:T(8,128)S(1)} collective-permute-done((f32[72,128]{1,0:T(8,128)S(1)}, f32[72,128]{1,0:T(8,128)S(1)}, u32[]{:S(2)}, u32[]{:S(2)}) %collective-permute-start.3) | collective-permute-done | bytes 36896 | tf_op jit(solution)/shard_map/ppermute | solution.py:449
  24.1 0.0 collective-permute-done.2.lon_even
  24.1 0.0 copy-done.8
  24.1 17.6 %advance.1 = (f32[4,64,768]{2,1,0:T(8,128)}, f32[4,64,768]{2,1,0:T(8,128)}, f32[4,64,768]{2,1,0:T(8,128)}, f32[4,64,768]{2,1,0:T(8,128)}) custom-call(f32[4,64,768]{2,1,0:T(8,128)S(1)} %copy-done, f32[4,64,768]{2,1,0:T(8,128)S(1)} %copy-done.1, f32[4,64,768]{2,1,0:T(8,128)S(1)} %copy-done.2, f32[4,64,768]{2,1,0:T(8,128)S(1)} %copy-done.3, ...), custom_call_target="tpu_custom_call" | custom-call | tf_op jit(solution)/shard_map/advance/pallas_call | solution.py:421
Async XLA Ops:
  0.6 16.0 %copy-start.7 = (f32[64,768]{1,0:T(8,128)S(1)}, f32[64,768]{1,0:T(8,128)}, u32[]{:S(2)}) copy-start(f32[64,768]{1,0:T(8,128)} %nwid.1) | copy-start | bytes 589828
  0.6 16.0 %copy-start.6 = (f32[64,768]{1,0:T(8,128)S(1)}, f32[64,768]{1,0:T(8,128)}, u32[]{:S(2)}) copy-start(f32[64,768]{1,0:T(8,128)} %ewid.1) | copy-start | bytes 589828
  0.7 16.0 %copy-start.5 = (s32[4,64,768]{2,1,0:T(8,128)S(1)}, s32[4,64,768]{2,1,0:T(8,128)}, u32[]{:S(2)}) copy-start(s32[4,64,768]{2,1,0:T(8,128)} %land.1) | copy-start | bytes 2359300
  0.7 16.0 %copy-start.4 = (f32[4,64,768]{2,1,0:T(8,128)S(1)}, f32[4,64,768]{2,1,0:T(8,128)}, u32[]{:S(2)}) copy-start(f32[4,64,768]{2,1,0:T(8,128)} %thick.1) | copy-start | bytes 2359300
  0.7 16.0 %copy-start.3 = (f32[4,64,768]{2,1,0:T(8,128)S(1)}, f32[4,64,768]{2,1,0:T(8,128)}, u32[]{:S(2)}) copy-start(f32[4,64,768]{2,1,0:T(8,128)} %vvel.1) | copy-start | bytes 2359300
  0.7 16.0 %copy-start.2 = (f32[4,64,768]{2,1,0:T(8,128)S(1)}, f32[4,64,768]{2,1,0:T(8,128)}, u32[]{:S(2)}) copy-start(f32[4,64,768]{2,1,0:T(8,128)} %uvel.1) | copy-start | bytes 2359300
  0.7 16.0 %copy-start.1 = (f32[4,64,768]{2,1,0:T(8,128)S(1)}, f32[4,64,768]{2,1,0:T(8,128)}, u32[]{:S(2)}) copy-start(f32[4,64,768]{2,1,0:T(8,128)} %salt.1) | copy-start | bytes 2359300
  0.7 16.0 %copy-start = (f32[4,64,768]{2,1,0:T(8,128)S(1)}, f32[4,64,768]{2,1,0:T(8,128)}, u32[]{:S(2)}) copy-start(f32[4,64,768]{2,1,0:T(8,128)} %temp.1) | copy-start | bytes 2359300
  2.4 5.3 %collective-permute-start = (f32[2,24,768]{2,1,0:T(8,128)S(1)}, f32[2,24,768]{2,1,0:T(8,128)S(1)}, u32[]{:S(2)}, u32[]{:S(2)}) collective-permute-start(f32[2,24,768]{2,1,0:T(8,128)S(1)} %get-tuple-element.6), channel_id=1, source_target_pairs={{0,1},{1,0},{8,9},{9,8},{16,17},{17,16},{24,25},{25,24},{32,33},{3... | collective-permute-start | bytes 442376 | tf_op jit(solution)/shard_map/ppermute | solution.py:445
  2.5 21.6 %copy-start.8 = (f32[64,768]{1,0:T(8,128)S(1)}, f32[64,768]{1,0:T(8,128)}, u32[]{:S(2)}) copy-start(f32[64,768]{1,0:T(8,128)} %cori.1) | copy-start | bytes 589828
  2.5 14.1 %collective-permute-start.1 = (f32[2,24,768]{2,1,0:T(8,128)S(1)}, f32[2,24,768]{2,1,0:T(8,128)S(1)}, u32[]{:S(2)}, u32[]{:S(2)}) collective-permute-start(f32[2,24,768]{2,1,0:T(8,128)S(1)} %get-tuple-element.7), channel_id=1, source_target_pairs={{1,2},{2,1},{9,10},{10,9},{17,18},{18,17},{25,26},{26,25},{33,34},... | collective-permute-start | bytes 442376 | tf_op jit(solution)/shard_map/ppermute | solution.py:446
  17.0 7.1 %collective-permute-start.3 = (f32[72,128]{1,0:T(8,128)S(1)}, f32[72,128]{1,0:T(8,128)S(1)}, u32[]{:S(2)}, u32[]{:S(2)}) collective-permute-start(f32[72,128]{1,0:T(8,128)S(1)} %pack_columns.1), channel_id=1, source_target_pairs={{8,16},{16,8},{24,32},{32,24},{40,48},{48,40},{56,64},{64,56},{72,... | collective-permute-start | bytes 110600 | tf_op jit(solution)/shard_map/ppermute | solution.py:449
  17.8 6.3 %collective-permute-start.2 = (f32[72,128]{1,0:T(8,128)S(1)}, f32[72,128]{1,0:T(8,128)S(1)}, u32[]{:S(2)}, u32[]{:S(2)}) collective-permute-start(f32[72,128]{1,0:T(8,128)S(1)} %pack_columns.1), channel_id=1, source_target_pairs={{0,8},{8,0},{16,24},{24,16},{32,40},{40,32},{48,56},{56,48},{64,72... | collective-permute-start | bytes 110600 | tf_op jit(solution)/shard_map/ppermute | solution.py:448

commit v3 on v2

v3 whole, which is shorter than its diff:
```python
import jax
import jax.numpy as jnp
from jax import lax
from jax.experimental import pallas as pl
from jax.experimental.pallas import tpu as pltpu
from jax.sharding import PartitionSpec as P

time_step = 0.2
biharm_coef = 0.02
alpha_temp = 0.2
beta_salt = 0.8
thin_floor = 0.25
flux_scale = time_step / 8.0 / biharm_coef

LEVELS = 4
ROWS = 64
COLS = 768
TILE = 128
TILES = COLS // TILE
CHUNKS = ROWS // 8
TALL = ROWS + 16
FIELDS = 22
SHOWN = FIELDS + LEVELS + 1
F32 = jnp.float32
PARAMS = pltpu.CompilerParams(vmem_limit_bytes=12 * 1024 * 1024)
AXES = ("lon", "lat")
VMEM = pl.BlockSpec(memory_space=pltpu.VMEM)


def place(lat, lon, lats, lons):
    return (lon % lons) * lats + lat


def both(pairs):
    return [p for a, b in pairs for p in ((a, b), (b, a))]


def lat_pairs(lats, lons, bit):
    pairs = [
        (place(i, j, lats, lons), place(i + 1, j, lats, lons))
        for i in range(bit, lats - 1, 2)
        for j in range(lons)
    ]
    if bit:
        pairs += [
            (place(lats - 1, j, lats, lons), place(lats - 1, lons - 1 - j, lats, lons))
            for j in range(lons // 2)
        ]
    return both(pairs)


def lon_pairs(lats, lons, bit):
    return both(
        [
            (place(i, j, lats, lons), place(i, j + 1, lats, lons))
            for i in range(lats)
            for j in range(bit, lons, 2)
        ]
    )


def onto_chip(x):
    return pltpu.with_memory_space_constraint(x, pltpu.VMEM)


def off_chip(x):
    return pltpu.with_memory_space_constraint(x, pltpu.HBM)


def rows_kernel(*refs):
    low, high, (near_ref, far_ref), stage = refs[:8], refs[8:16], refs[16:18], refs[18]
    lat = lax.axis_index("lat")
    odd = lat % 2 == 1
    top = lat == lax.axis_size("lat") - 1

    def gather(group, take, dst):
        for kind in range(5):
            for level in range(LEVELS):
                if kind < 4:
                    cells = group[kind][level]
                else:
                    cells = group[4][level] * group[5][level].astype(F32)
                for k, row in enumerate(take):
                    dst[k, kind * LEVELS + level : kind * LEVELS + level + 1, :] = cells[row : row + 1]
        for k, row in enumerate(take):
            dst[k, 20:21, :] = group[6][row : row + 1, :]
            dst[k, 21:22, :] = group[7][row : row + 1, :]

    @pl.when(odd)
    def _():
        gather(low, (0, 1), near_ref)

        @pl.when(jnp.logical_not(top))
        def _():
            gather(high, (6, 7), far_ref)

        @pl.when(top)
        def _():
            gather(high, (6, 5), stage)
            kind_row = lax.broadcasted_iota(jnp.int32, (24, TILE), 0)
            turned = jnp.logical_and(kind_row >= 2 * LEVELS, kind_row < 4 * LEVELS)
            sign = jnp.where(turned, -1.0, 1.0).astype(F32)
            flip = TILE - 1 - lax.broadcasted_iota(jnp.int32, (24, TILE), 1)
            for k in range(2):
                for t in range(COLS // TILE):
                    src = stage[k, :, COLS - TILE * (t + 1) : COLS - TILE * t]
                    rev = jnp.take_along_axis(src, flip, axis=1, mode="promise_in_bounds")
                    far_ref[k, :, TILE * t : TILE * (t + 1)] = rev * sign

    @pl.when(jnp.logical_not(odd))
    def _():
        gather(high, (6, 7), near_ref)
        gather(low, (0, 1), far_ref)


def pack_rows(arrays):
    def spec(a, at):
        if a.ndim == 3:
            return pl.BlockSpec((LEVELS, 8, COLS), lambda i: (0, at, 0))
        return pl.BlockSpec((8, COLS), lambda i: (at, 0))

    whole = pl.BlockSpec((2, 24, COLS), lambda i: (0, 0, 0))
    shape = pltpu.VMEM((2, 24, COLS), F32)
    return pl.pallas_call(
        rows_kernel,
        grid=(1,),
        in_specs=[spec(a, 0) for a in arrays] + [spec(a, ROWS // 8 - 1) for a in arrays],
        out_specs=[pl.BlockSpec(memory_space=pltpu.VMEM)] * 2,
        out_shape=[shape, shape],
        scratch_shapes=[pltpu.VMEM((2, 24, COLS), F32)],
        compiler_params=PARAMS,
        name="pack_rows",
    )(*[off_chip(x) for x in (*arrays, *arrays)])


def packed_field():
    def of(shape):
        lane = lax.broadcasted_iota(jnp.int32, shape, len(shape) - 1)
        return ((lane + 2) & (TILE - 1)) >> 1

    return of


def windows_kernel(temp, salt, uvel, vvel, thick, land, ewid, nwid, cori, win, packed):
    lane = lax.broadcasted_iota(jnp.int32, (ROWS, TILE), 1)
    field = packed_field()((ROWS, TILE))
    total = jnp.zeros((ROWS, TILE), F32)

    def edge(f, cut):
        kind, level = divmod(f, LEVELS)
        if kind < 4:
            return (temp, salt, uvel, vvel)[kind][level, :, cut]
        if kind == 4:
            return thick[level, :, cut] * land[level, :, cut].astype(F32)
        if f < FIELDS:
            return (ewid, nwid)[f - 20][:, cut]
        if f < FIELDS + LEVELS:
            return land[f - FIELDS, :, cut].astype(F32)
        return cori[:, cut]

    for f in range(SHOWN):
        low, high = edge(f, slice(0, TILE)), edge(f, slice(COLS - TILE, COLS))
        cells = jnp.where(lane < TILE // 4, low, pltpu.roll(high, TILE // 2, 1))
        win[f] = cells
        if f < FIELDS:
            mine = jnp.logical_or(field == f, field == f + 33)
            total = jnp.where(mine, pltpu.roll(cells, (TILE // 2 + 2 * f) % TILE, 1), total)
    packed[...] = total


def windows(arrays, coriolis):
    return pl.pallas_call(
        windows_kernel,
        in_specs=[VMEM] * 9,
        out_specs=[VMEM] * 2,
        out_shape=[pltpu.VMEM((SHOWN, ROWS, TILE), F32), pltpu.VMEM((ROWS, TILE), F32)],
        compiler_params=PARAMS,
        name="windows",
    )(*[onto_chip(x) for x in (*arrays, coriolis)])


def columns_kernel(packed, near, far, out, ghosts, corner):
    lat = lax.axis_index("lat")
    odd = lat % 2 == 1
    out[0:ROWS, :] = packed[...]
    row = lax.broadcasted_iota(jnp.int32, (24, COLS), 0)
    fill = jnp.logical_and(lat == 0, row >= 20)
    lane = lax.broadcasted_iota(jnp.int32, (24, TILE), 1)
    field = packed_field()((24, TILE))
    small_row = lax.broadcasted_iota(jnp.int32, (24, TILE), 0)
    mine = jnp.logical_or(field == small_row, field == small_row + 33)
    for k in range(2):
        a, b = near[k], far[k]
        for side in range(2):
            if side == 0:
                cells = jnp.where(odd, b, a)
            else:
                cells = jnp.where(fill, 1.0, jnp.where(odd, a, b))
            at = 2 * side + k
            ghosts[at] = cells
            shown = jnp.where(lane < TILE // 4, cells[:, 0:TILE], pltpu.roll(cells[:, COLS - TILE : COLS], TILE // 2, 1))
            corner[at] = shown
            spread = pltpu.roll(shown, TILE // 2, 1, stride=2, stride_axis=0)
            out[ROWS + at : ROWS + at + 1, :] = jnp.sum(jnp.where(mine, spread, 0.0), axis=0, keepdims=True)
    out[ROWS + 4 : ROWS + 8, :] = jnp.zeros((4, TILE), F32)


def pack_columns(packed, near, far):
    return pl.pallas_call(
        columns_kernel,
        in_specs=[VMEM] * 3,
        out_specs=[VMEM] * 3,
        out_shape=[
            pltpu.VMEM((ROWS + 8, TILE), F32),
            pltpu.VMEM((4, 24, COLS), F32),
            pltpu.VMEM((4, 24, TILE), F32),
        ],
        compiler_params=PARAMS,
        name="pack_columns",
    )(*[onto_chip(x) for x in (packed, near, far)])


def north_of(here, above):
    sub = lax.broadcasted_iota(jnp.int32, here.shape, 0)
    return pltpu.roll(jnp.where(sub == 0, above, here), 7, 0)


def south_of(here, below):
    sub = lax.broadcasted_iota(jnp.int32, here.shape, 0)
    return pltpu.roll(jnp.where(sub == 7, below, here), 1, 0)


def inner_kernel(
    temp, salt, uvel, vvel, thick, land, ewid, nwid, cori,
    temp_out, salt_out, uvel_out, vvel_out,
    deep, ratio_e, ratio_n, span_e, span_n, inv_area, half_e, half_n,
    coef_e, coef_n, inv_vol, move_n, flux_t, flux_s, lap, pres, slope, over, over_e,
):
    level = pl.program_id(0)
    lane = lax.broadcasted_iota(jnp.int32, (8, TILE), 1)
    first, last = lane == 0, lane == TILE - 1
    data = (temp, salt, uvel, vvel)

    def tile(t):
        return slice(TILE * t, TILE * t + TILE)

    def turn_e(x):
        return pltpu.roll(x, TILE - 1, 1)

    def turn_w(x):
        return pltpu.roll(x, 1, 1)

    def around(c):
        r = pl.multiple_of(8 * c, 8)
        up = pl.multiple_of(8 * jnp.minimum(c + 1, CHUNKS - 1), 8)
        down = pl.multiple_of(8 * jnp.maximum(c - 1, 0), 8)
        return pl.ds(r, 8), pl.ds(up, 8), pl.ds(down, 8)

    @pl.when(level == 0)
    def _():
        def chunk(c, _):
            here, above, _ = around(c)
            east = [(ewid[here, tile(0)], nwid[here, tile(0)])]
            east = [tuple((x, turn_e(x)) for x in east[0])]
            for t in range(TILES):
                (e, re), (n, rn) = east[t]
                u = (t + 1) % TILES
                if u:
                    east.append(tuple((x, turn_e(x)) for x in (ewid[here, tile(u)], nwid[here, tile(u)])))
                else:
                    east.append(east[0])
                ee = jnp.where(last, east[t + 1][0][1], re)
                ne = jnp.where(last, east[t + 1][1][1], rn)
                en = north_of(e, ewid[above, tile(t)])
                nn = north_of(n, nwid[above, tile(t)])
                ratio_e[here, tile(t)] = (n + ne) / (e + ee)
                ratio_n[here, tile(t)] = (e + en) / (n + nn)
                span_e[here, tile(t)] = flux_scale * (n + ne)
                span_n[here, tile(t)] = flux_scale * (e + en)
                inv_area[here, tile(t)] = 1.0 / (e * n)
                half_e[here, tile(t)] = (0.5 * time_step) / e
                half_n[here, tile(t)] = (0.5 * time_step) / n
                over[here, tile(t)] = jnp.zeros((8, TILE), F32)
                over_e[here, tile(t)] = jnp.zeros((8, TILE), F32)
            return 0

        lax.fori_loop(0, CHUNKS, chunk, 0)

    for r in range(0, ROWS, 8):
        deep[r : r + 8, :] = thick[level, r : r + 8, :] * land[level, r : r + 8, :].astype(F32)

    def laps(c, _):
        here, above, below = around(c)

        def turned_at(t):
            cells = [x[level, here, tile(t)] for x in data] + [deep[here, tile(t)]]
            return [(x, turn_e(x)) for x in cells]

        def zonal(t, turned, ahead):
            d, rd = turned[4]
            de = jnp.where(last, ahead[4][1], rd)
            lon_thick = jnp.minimum(d, de)
            ce = lon_thick * ratio_e[here, tile(t)]
            east = [jnp.where(last, ahead[f][1], turned[f][1]) for f in range(4)]
            flux = [ce * (east[f] - turned[f][0]) for f in range(4)]
            te = lon_thick * span_e[here, tile(t)] * (turned[2][0] + east[2])
            be = (beta_salt * east[1] - alpha_temp * east[0]) * de
            before = over_e[here, tile(t)]
            pe = before + 0.5 * be
            over_e[here, tile(t)] = before + be
            return ce, flux, te, east, pe

        end, start = turned_at(TILES - 1), turned_at(0)
        kept = zonal(TILES - 1, end, start)
        behind, behind_pe = [turn_w(x) for x in kept[1]], pltpu.roll(kept[4], 2, 1)
        kept_flux, kept_pe = behind, behind_pe
        turned = start
        for t in range(TILES):
            if t < TILES - 1:
                ahead = turned_at(t + 1) if t < TILES - 2 else end
                ce, flux, te, east, pe = zonal(t, turned, ahead)
                turned_flux, turned_pe = [turn_w(x) for x in flux], pltpu.roll(pe, 2, 1)
            else:
                ce, flux, te, east, pe = kept
                turned_flux, turned_pe = kept_flux, kept_pe
            coef_e[here, tile(t)] = ce
            d = turned[4][0]
            dn, ds = north_of(d, deep[above, tile(t)]), south_of(d, deep[below, tile(t)])
            lat_thick = jnp.minimum(d, dn)
            rn = ratio_n[here, tile(t)]
            cn = lat_thick * rn
            cs = jnp.minimum(ds, d) * south_of(rn, ratio_n[below, tile(t)])
            iv = inv_area[here, tile(t)] / jnp.maximum(d, thin_floor)
            coef_n[here, tile(t)] = cn
            inv_vol[here, tile(t)] = iv
            for f in range(4):
                q = turned[f][0]
                qn, qs = north_of(q, data[f][level, above, tile(t)]), south_of(q, data[f][level, below, tile(t)])
                west = jnp.where(first, behind[f], turned_flux[f])
                lap[f, here, tile(t)] = (flux[f] - west + cn * (qn - q) - cs * (q - qs)) * iv
                if f == 3:
                    move_n[here, tile(t)] = lat_thick * span_n[here, tile(t)] * (q + qn)
            q0, q1 = turned[0][0], turned[1][0]
            flux_t[here, tile(t)] = te * (q0 + east[0])
            flux_s[here, tile(t)] = te * (q1 + east[1])
            b = (beta_salt * q1 - alpha_temp * q0) * d
            before = over[here, tile(t)]
            pres[here, tile(t)] = before + 0.5 * b
            over[here, tile(t)] = before + b
            slope[here, tile(t)] = pe - jnp.where(lane < 2, behind_pe, turned_pe)
            behind, behind_pe, turned = turned_flux, turned_pe, ahead
        return 0

    lax.fori_loop(0, CHUNKS, laps, 0)

    def finish(c, _):
        here, above, below = around(c)

        def turned_at(t):
            return [(x, turn_e(x)) for x in (lap[f, here, tile(t)] for f in range(4))]

        def zonal(t, turned, ahead):
            ce = coef_e[here, tile(t)]
            flux = [ce * (jnp.where(last, ahead[f][1], turned[f][1]) - turned[f][0]) for f in range(4)]
            flux[0] = flux[0] + flux_t[here, tile(t)]
            flux[1] = flux[1] + flux_s[here, tile(t)]
            return flux

        end, start = turned_at(TILES - 1), turned_at(0)
        kept = zonal(TILES - 1, end, start)
        kept_turned = [turn_w(x) for x in kept]
        behind, turned = kept_turned, start
        outs = (temp_out, salt_out, uvel_out, vvel_out)
        for t in range(TILES):
            if t < TILES - 1:
                ahead = turned_at(t + 1) if t < TILES - 2 else end
                flux = zonal(t, turned, ahead)
                turned_flux = [turn_w(x) for x in flux]
            else:
                flux, turned_flux = kept, kept_turned
            cn = coef_n[here, tile(t)]
            cs = south_of(cn, coef_n[below, tile(t)])
            iv = biharm_coef * inv_vol[here, tile(t)]
            gn = move_n[here, tile(t)]
            gs = south_of(gn, move_n[below, tile(t)])
            wet = land[level, here, tile(t)].astype(F32)
            u, v = uvel[level, here, tile(t)], vvel[level, here, tile(t)]
            turning = time_step * cori[here, tile(t)]
            for f in range(4):
                m = turned[f][0]
                mn, ms = north_of(m, lap[f, above, tile(t)]), south_of(m, lap[f, below, tile(t)])
                west = jnp.where(first, behind[f], turned_flux[f])
                total = flux[f] - west + cn * (mn - m) - cs * (m - ms)
                if f < 2:
                    q = data[f][level, here, tile(t)]
                    qn, qs = north_of(q, data[f][level, above, tile(t)]), south_of(q, data[f][level, below, tile(t)])
                    total = total + gn * (q + qn) - gs * (qs + q)
                    change = wet * (q - total * iv)
                elif f == 2:
                    change = wet * (u + turning * v - slope[here, tile(t)] * half_e[here, tile(t)] - total * iv)
                else:
                    p = pres[here, tile(t)]
                    rise = north_of(p, pres[above, tile(t)]) - south_of(p, pres[below, tile(t)])
                    change = wet * (v - turning * u - rise * half_n[here, tile(t)] - total * iv)
                outs[f][level, here, tile(t)] = change
            behind, turned = turned_flux, ahead
        return 0

    lax.fori_loop(0, CHUNKS, finish, 0)


def inner(arrays, coriolis):
    plane = pltpu.VMEM((ROWS, COLS), F32)
    return pl.pallas_call(
        inner_kernel,
        grid=(LEVELS,),
        in_specs=[VMEM] * 9,
        out_specs=[VMEM] * 4,
        out_shape=[pltpu.VMEM((LEVELS, ROWS, COLS), F32)] * 4,
        scratch_shapes=[plane] * 14 + [pltpu.VMEM((4, ROWS, COLS), F32)] + [plane] * 4,
        compiler_params=PARAMS,
        name="inner",
    )(*[onto_chip(x) for x in (*arrays, coriolis)])


def metric(e, n, lanes, rows):
    ee, ne, en, nn = lanes(e, 1), lanes(n, 1), rows(e, 1), rows(n, 1)
    return (
        (n + ne) / (e + ee),
        (e + en) / (n + nn),
        flux_scale * (n + ne),
        flux_scale * (e + en),
        1.0 / (e * n),
        (0.5 * time_step) / e,
        (0.5 * time_step) / n,
    )


def patch(cells, d, wet, cori, known, over, lanes, rows):
    ratio_e, ratio_n, span_e, span_n, inv_area, half_e, half_n = known
    temp, salt, uvel, vvel = cells
    de, dn = lanes(d, 1), rows(d, 1)
    lon_thick, lat_thick = jnp.minimum(d, de), jnp.minimum(d, dn)
    ce, cn = lon_thick * ratio_e, lat_thick * ratio_n
    cs = rows(cn, -1)
    iv = inv_area / jnp.maximum(d, thin_floor)
    b = (beta_salt * salt - alpha_temp * temp) * d
    p = over + 0.5 * b
    ge = (lanes(p, 1) - lanes(p, -1)) * half_e
    gn = (rows(p, 1) - rows(p, -1)) * half_n
    outs = []
    te = tn = None
    for f in (2, 3, 0, 1):
        q = cells[f]
        qe, qn, qs = lanes(q, 1), rows(q, 1), rows(q, -1)
        if f == 2:
            te = lon_thick * span_e * (q + qe)
        if f == 3:
            tn = lat_thick * span_n * (q + qn)
            ts = rows(tn, -1)
        fe = ce * (qe - q)
        m = (fe - lanes(fe, -1) + cn * (qn - q) - cs * (q - qs)) * iv
        fe = ce * (lanes(m, 1) - m)
        if f < 2:
            fe = fe + te * (q + qe)
        total = fe - lanes(fe, -1) + cn * (rows(m, 1) - m) - cs * (m - rows(m, -1))
        if f < 2:
            total = total + tn * (q + qn) - ts * (qs + q)
        change = q - biharm_coef * iv * total
        if f == 2:
            change = change + time_step * cori * vvel - ge
        if f == 3:
            change = change - time_step * cori * uvel - gn
        outs.append(wet * change)
    return (outs[2], outs[3], outs[0], outs[1]), over + b


def rims_kernel(
    temp, salt, uvel, vvel, thick, land, ewid, nwid, cori, ghosts, temp_in, salt_in, uvel_in, vvel_in,
    temp_out, salt_out, uvel_out, vvel_out, known, spin, over,
):
    level = pl.program_id(0)
    sub = lax.broadcasted_iota(jnp.int32, (8, COLS), 0)
    low, high = slice(0, 8), slice(ROWS - 8, ROWS)

    def lanes(x, by):
        return pltpu.roll(x, COLS - 1 if by > 0 else 1, 2)

    def rows(x, by):
        return pltpu.roll(x, 7 if by > 0 else 1, 1)

    def strips(f, south, north):
        g = [ghosts[k, pl.ds(f, 1), :] for k in range(4)]
        s = jnp.where(sub == 0, g[2], jnp.where(sub == 1, g[3], pltpu.roll(south, 2, 0)))
        n = jnp.where(sub == 6, g[0], jnp.where(sub == 7, g[1], pltpu.roll(north, 6, 0)))
        return jnp.stack([s, n])

    def own(south, north):
        return jnp.stack([pltpu.roll(south, 2, 0), pltpu.roll(north, 6, 0)])

    @pl.when(level == 0)
    def _():
        e = strips(20, ewid[low, :], ewid[high, :])
        n = strips(21, nwid[low, :], nwid[high, :])
        for i, x in enumerate(metric(e, n, lanes, rows)):
            known[i] = x
        spin[...] = own(cori[low, :], cori[high, :])
        over[...] = jnp.zeros((2, 8, COLS), F32)

    cells = [
        strips(LEVELS * kind + level, x[level, low, :], x[level, high, :])
        for kind, x in enumerate((temp, salt, uvel, vvel))
    ]
    wet_low, wet_high = land[level, low, :].astype(F32), land[level, high, :].astype(F32)
    d = strips(4 * LEVELS + level, thick[level, low, :] * wet_low, thick[level, high, :] * wet_high)
    new, over[...] = patch(
        cells, d, own(wet_low, wet_high), spin[...], [known[i] for i in range(7)], over[...], lanes, rows
    )
    ins = (temp_in, salt_in, uvel_in, vvel_in)
    for x, old, out in zip(new, ins, (temp_out, salt_out, uvel_out, vvel_out)):
        out[level, low, :] = jnp.where(sub < 2, pltpu.roll(x[0], 6, 0), old[level, low, :])
        out[level, high, :] = jnp.where(sub >= 6, pltpu.roll(x[1], 2, 0), old[level, high, :])


def rims(arrays, coriolis, ghosts, outs):
    return pl.pallas_call(
        rims_kernel,
        grid=(LEVELS,),
        in_specs=[VMEM] * 14,
        out_specs=[VMEM] * 4,
        out_shape=[pltpu.VMEM((LEVELS, ROWS, COLS), F32)] * 4,
        scratch_shapes=[
            pltpu.VMEM((7, 2, 8, COLS), F32),
            pltpu.VMEM((2, 8, COLS), F32),
            pltpu.VMEM((2, 8, COLS), F32),
        ],
        input_output_aliases={10: 0, 11: 1, 12: 2, 13: 3},
        compiler_params=PARAMS,
        name="rims",
    )(*[onto_chip(x) for x in (*arrays, coriolis, ghosts, *outs)])


def sides_kernel(
    win, corner, lon_even, lon_odd, temp_in, salt_in, uvel_in, vvel_in,
    temp_out, salt_out, uvel_out, vvel_out,
    side, known, over, edges, mid_sem, low_sem, high_sem,
):
    level = pl.program_id(0)
    ins, outs = (temp_in, salt_in, uvel_in, vvel_in), (temp_out, salt_out, uvel_out, vvel_out)
    lane = lax.broadcasted_iota(jnp.int32, (TALL, TILE), 1)
    field = packed_field()((TALL, TILE))
    ghost_lane = jnp.logical_or(field == 0, field == 33)
    middle = pl.ds(TILE, COLS - 2 * TILE)

    def mid_copy(i):
        return pltpu.make_async_copy(ins[i].at[:, :, middle], outs[i].at[:, :, middle], mid_sem.at[i])

    def edge_copies(i, at):
        return (
            pltpu.make_async_copy(edges.at[0, i, at], outs[i].at[at, :, pl.ds(0, TILE)], low_sem.at[i, at]),
            pltpu.make_async_copy(edges.at[1, i, at], outs[i].at[at, :, pl.ds(COLS - TILE, TILE)], high_sem.at[i, at]),
        )

    def lanes(x, by):
        return pltpu.roll(x, TILE - 1 if by > 0 else 1, 1)

    def rows(x, by):
        return pltpu.roll(x, TALL - 1 if by > 0 else 1, 0)

    def tall(body, north, south):
        pad = jnp.zeros((6, TILE), F32)
        return jnp.concatenate([pad, south, body, north, pad], axis=0)

    def extended(f):
        shift = (TILE - 2 * f) & (TILE - 1)
        base = tall(
            win[f],
            jnp.concatenate([corner[k, pl.ds(f, 1), :] for k in (0, 1)], axis=0),
            jnp.concatenate([corner[k, pl.ds(f, 1), :] for k in (2, 3)], axis=0),
        )
        return jnp.where(ghost_lane, pltpu.roll(side[...], shift, 1), base)

    @pl.when(level == 0)
    def _():
        for i in range(4):
            mid_copy(i).start()
        odd = lax.axis_index("lon") % 2 == 1
        a, b = lon_even[...], lon_odd[...]
        got = jnp.where(packed_field()((ROWS + 8, TILE)) >= 33, jnp.where(odd, b, a), jnp.where(odd, a, b))
        side[...] = tall(got[0:ROWS], got[ROWS : ROWS + 2], got[ROWS + 2 : ROWS + 4])
        e, n = extended(20), extended(21)
        for i, x in enumerate(metric(e, n, lanes, rows)):
            known[i] = x
        over[...] = jnp.zeros((TALL, TILE), F32)

    cells = [extended(LEVELS * kind + level) for kind in range(4)]
    d = extended(4 * LEVELS + level)
    blank = jnp.zeros((2, TILE), F32)
    wet, spin = tall(win[FIELDS + level], blank, blank), tall(win[FIELDS + LEVELS], blank, blank)
    new, over[...] = patch(cells, d, wet, spin, [known[i] for i in range(7)], over[...], lanes, rows)
    own = lax.broadcasted_iota(jnp.int32, (ROWS, TILE), 1)
    for i, x in enumerate(new):
        x = x[8 : 8 + ROWS]
        edges[0, i, level] = jnp.where(own < 2, x, ins[i][level, :, 0:TILE])
        edges[1, i, level] = jnp.where(own >= TILE - 2, pltpu.roll(x, TILE // 2, 1), ins[i][level, :, COLS - TILE : COLS])
        for copy in edge_copies(i, level):
            copy.start()

    @pl.when(level == LEVELS - 1)
    def _():
        for i in range(4):
            mid_copy(i).wait()
            for at in range(LEVELS):
                for copy in edge_copies(i, at):
                    copy.wait()


def sides(win, corner, lon_even, lon_odd, outs):
    return pl.pallas_call(
        sides_kernel,
        grid=(LEVELS,),
        in_specs=[VMEM] * 8,
        out_specs=[pl.BlockSpec(memory_space=pltpu.HBM)] * 4,
        out_shape=[jax.ShapeDtypeStruct((LEVELS, ROWS, COLS), F32)] * 4,
        scratch_shapes=[
            pltpu.VMEM((TALL, TILE), F32),
            pltpu.VMEM((7, TALL, TILE), F32),
            pltpu.VMEM((TALL, TILE), F32),
            pltpu.VMEM((2, 4, LEVELS, ROWS, TILE), F32),
            pltpu.SemaphoreType.DMA((4,)),
            pltpu.SemaphoreType.DMA((4, LEVELS)),
            pltpu.SemaphoreType.DMA((4, LEVELS)),
        ],
        compiler_params=PARAMS,
        name="sides",
    )(*[onto_chip(x) for x in (win, corner, lon_even, lon_odd, *outs)])


def shards(temp, salt, uvel, vvel, thick, land, east_width, north_width, coriolis):
    lats, lons = lax.axis_size("lat"), lax.axis_size("lon")
    arrays = (temp, salt, uvel, vvel, thick, land, east_width, north_width)
    near, far = pack_rows(arrays)
    near = lax.ppermute(near, AXES, lat_pairs(lats, lons, 0))
    far = lax.ppermute(far, AXES, lat_pairs(lats, lons, 1))
    win, packed = windows(arrays, coriolis)
    outs = inner(arrays, coriolis)
    near, far, packed, *outs = lax.optimization_barrier((near, far, packed, *outs))
    packed, ghosts, corner = pack_columns(packed, near, far)
    lon_even = lax.ppermute(packed, AXES, lon_pairs(lats, lons, 0))
    lon_odd = lax.ppermute(packed, AXES, lon_pairs(lats, lons, 1))
    outs = rims(arrays, coriolis, ghosts, outs)
    return tuple(sides(win, corner, lon_even, lon_odd, outs))


def solution(mesh):
    deep, flat = P(None, "lat", "lon"), P("lat", "lon")
    return jax.shard_map(
        shards,
        mesh=mesh,
        in_specs=(deep,) * 6 + (flat,) * 3,
        out_specs=(deep,) * 4,
        check_vma=False,
    )
```

time: 41.8 us -> 35.6 us (0.85)
  the two profiles are of different devices: /device:TPU:63 before, /device:TPU:38 now
where the time goes in v3:
time: 35.6 us; the launch traced here: 35.5 us
  Pallas kernels  22.8 us (64%)
  starting transfers between devices  7.98 us (22%)
  waiting for transfers between devices  3.82 us (11%)
  between operations  0.84 us (2%)
    pallas_call x1, Pallas kernels, inner(): pl.pallas_call(inner_kernel, grid=(LEVELS,), in_specs=[VMEM] * 9, out_spe...  13.3 us
    ppermute x1, starting transfers between devices, shards(): far = lax.ppermute(far, AXES, lat_pairs(lats, lons, 1))  6.91 us
    pallas_call x1, Pallas kernels, sides(): pl.pallas_call(sides_kernel, grid=(LEVELS,), in_specs=[VMEM] * 8, out_spe...  3.87 us
    ppermute x1, waiting for transfers between devices, shards(): lon_odd = lax.ppermute(packed, AXES, lon_pairs(lats, lons, 1))  3.81 us
    pallas_call x1, Pallas kernels, rims(): pl.pallas_call(rims_kernel, grid=(LEVELS,), in_specs=[VMEM] * 14, out_spe...  2.27 us
    pallas_call x1, Pallas kernels, pack_rows(): pl.pallas_call(rows_kernel, grid=(1,), in_specs=[spec(a, 0) for a in arra...  1.71 us
    pallas_call x1, Pallas kernels, windows(): pl.pallas_call(windows_kernel, in_specs=[VMEM] * 9, out_specs=[VMEM] * 2,...  1.52 us
  transfers between devices with their start and end apart: 4, of which 1 were waited for; matrix products, arithmetic and copies ran while one was open for 0% of the time, Pallas kernels for 48%

profile of v3, /device:TPU:38, one launch (start us, length us, event | category | flops | bytes accessed | tf_op | source)
XLA Modules:
  0.0 35.5 jit_solution(12031992092991193101)
XLA Ops:
  0.6 0.0 copy-start.7
  0.6 0.0 copy-start.6
  0.7 0.0 copy-start.5
  0.7 0.0 copy-start.4
  0.7 0.0 copy-start.3
  0.7 0.0 copy-start.2
  0.7 0.0 copy-start.1
  0.7 0.0 copy-start
  0.7 0.0 copy-start.8
  0.7 1.7 %pack_rows.1 = (f32[2,24,768]{2,1,0:T(8,128)S(1)}, f32[2,24,768]{2,1,0:T(8,128)S(1)}) custom-call(f32[4,64,768]{2,1,0:T(8,128)} %temp.5, f32[4,64,768]{2,1,0:T(8,128)} %salt.5, f32[4,64,768]{2,1,0:T(8,128)} %uvel.5, f32[4,64,768]{2,1,0:T(8,128)} %vvel.5, f32[4,64,768]{2,1,0:T(8,128)} %thick.5, s32[4,64,768]{2,1,0:T(8,128)} %land.5, f32[64,768]{1,0:T(8,128)} %ewid.5, ...), custom_call_target="tpu_custom_call" | custom-call | tf_op jit(solution)/shard_map/pack_rows/pallas_call | solution.py:124
  2.4 0.1 collective-permute-start
  2.5 6.9 %collective-permute-start.1 = (f32[2,24,768]{2,1,0:T(8,128)S(1)}, f32[2,24,768]{2,1,0:T(8,128)S(1)}, u32[]{:S(2)}, u32[]{:S(2)}) collective-permute-start(f32[2,24,768]{2,1,0:T(8,128)S(1)} %get-tuple-element.28), channel_id=1, source_target_pairs={{1,2},{2,1},{9,10},{10,9},{17,18},{18,17},{25,26},{26,25},{33,34},... | collective-permute-start | bytes 442376 | tf_op jit(solution)/shard_map/ppermute | solution.py:644
  9.4 0.0 copy-done.7
  9.5 0.0 copy-done.6
  9.5 0.0 copy-done.5
  9.5 0.0 copy-done.4
  9.5 0.0 copy-done.3
  9.5 0.0 copy-done.2
  9.5 0.0 copy-done.1
  9.5 0.0 copy-done
  9.5 0.0 copy-done.8
  9.5 1.5 %windows.1 = (f32[27,64,128]{2,1,0:T(8,128)S(1)}, f32[64,128]{1,0:T(8,128)S(1)}) custom-call(f32[4,64,768]{2,1,0:T(8,128)S(1)} %copy-done, f32[4,64,768]{2,1,0:T(8,128)S(1)} %copy-done.1, f32[4,64,768]{2,1,0:T(8,128)S(1)} %copy-done.2, f32[4,64,768]{2,1,0:T(8,128)S(1)} %copy-done.3, f32[4,64,768]{2,1,0:T(8,128)S(1)} %copy-done.4, ...), custom_call_target="tpu_custom_call" | custom-call | tf_op jit(solution)/shard_map/windows/pallas_call | solution.py:172
  11.1 13.3 %inner.1 = (f32[4,64,768]{2,1,0:T(8,128)S(1)}, f32[4,64,768]{2,1,0:T(8,128)S(1)}, f32[4,64,768]{2,1,0:T(8,128)S(1)}, f32[4,64,768]{2,1,0:T(8,128)S(1)}) custom-call(f32[4,64,768]{2,1,0:T(8,128)S(1)} %copy-done, f32[4,64,768]{2,1,0:T(8,128)S(1)} %copy-done.1, f32[4,64,768]{2,1,0:T(8,128)S(1)} %copy-done.2, f32[4,64,768]{2,1,0:T(8,128)S(1)} %copy-done.3, ...), custom_call_target="tpu_custom_call" | custom-call | tf_op jit(solution)/shard_map/inner/pallas_call | solution.py:414
  24.3 0.0 collective-permute-done.near
  24.3 0.0 collective-permute-done.1.far
  24.4 0.2 pack_columns.1
  24.5 0.6 %collective-permute-start.3 = (f32[72,128]{1,0:T(8,128)S(1)}, f32[72,128]{1,0:T(8,128)S(1)}, u32[]{:S(2)}, u32[]{:S(2)}) collective-permute-start(f32[72,128]{1,0:T(8,128)S(1)} %get-tuple-element.38), channel_id=1, source_target_pairs={{8,16},{16,8},{24,32},{32,24},{40,48},{48,40},{56,64},{64,56},{72,... | collective-permute-start | bytes 110600 | tf_op jit(solution)/shard_map/ppermute | solution.py:650
  25.1 0.4 %collective-permute-start.2 = (f32[72,128]{1,0:T(8,128)S(1)}, f32[72,128]{1,0:T(8,128)S(1)}, u32[]{:S(2)}, u32[]{:S(2)}) collective-permute-start(f32[72,128]{1,0:T(8,128)S(1)} %get-tuple-element.38), channel_id=1, source_target_pairs={{0,8},{8,0},{16,24},{24,16},{32,40},{40,32},{48,56},{56,48},{64,72... | collective-permute-start | bytes 110600 | tf_op jit(solution)/shard_map/ppermute | solution.py:649
  25.5 2.3 %rims.1 = (f32[4,64,768]{2,1,0:T(8,128)S(1)}, f32[4,64,768]{2,1,0:T(8,128)S(1)}, f32[4,64,768]{2,1,0:T(8,128)S(1)}, f32[4,64,768]{2,1,0:T(8,128)S(1)}) custom-call(f32[4,64,768]{2,1,0:T(8,128)S(1)} %copy-done, f32[4,64,768]{2,1,0:T(8,128)S(1)} %copy-done.1, ...), custom_call_target="tpu_custom_call", output_to_operand_aliasing={{0}: (10, {}), {1}: (11, {}), {2}: (12, {}), {3}: (13, {})} | custom-call | tf_op jit(solution)/shard_map/rims/pallas_call | solution.py:526
  27.8 3.8 %collective-permute-done.3.lon_odd = f32[72,128]{1,0:T(8,128)S(1)} collective-permute-done((f32[72,128]{1,0:T(8,128)S(1)}, f32[72,128]{1,0:T(8,128)S(1)}, u32[]{:S(2)}, u32[]{:S(2)}) %collective-permute-start.3) | collective-permute-done | bytes 36896 | tf_op jit(solution)/shard_map/ppermute | solution.py:650
  31.6 0.0 collective-permute-done.2.lon_even
  31.6 3.9 %sides.1 = (f32[4,64,768]{2,1,0:T(8,128)}, f32[4,64,768]{2,1,0:T(8,128)}, f32[4,64,768]{2,1,0:T(8,128)}, f32[4,64,768]{2,1,0:T(8,128)}) custom-call(f32[27,64,128]{2,1,0:T(8,128)S(1)} %get-tuple-element.26.win, f32[4,24,128]{2,1,0:T(8,128)S(1)} %get-tuple-element.37.corner, f32[72,128]{1,0:T(8,128)S(1)} %collective-permute-done.2.lon_even, ...), custom_call_target="tpu_custom_call" | custom-call | tf_op jit(solution)/shard_map/sides/pallas_call | solution.py:619
Async XLA Ops:
  0.6 8.8 %copy-start.7 = (f32[64,768]{1,0:T(8,128)S(1)}, f32[64,768]{1,0:T(8,128)}, u32[]{:S(2)}) copy-start(f32[64,768]{1,0:T(8,128)} %nwid.5) | copy-start | bytes 589828
  0.6 8.8 %copy-start.6 = (f32[64,768]{1,0:T(8,128)S(1)}, f32[64,768]{1,0:T(8,128)}, u32[]{:S(2)}) copy-start(f32[64,768]{1,0:T(8,128)} %ewid.5) | copy-start | bytes 589828
  0.7 8.8 %copy-start.5 = (s32[4,64,768]{2,1,0:T(8,128)S(1)}, s32[4,64,768]{2,1,0:T(8,128)}, u32[]{:S(2)}) copy-start(s32[4,64,768]{2,1,0:T(8,128)} %land.5) | copy-start | bytes 2359300
  0.7 8.8 %copy-start.4 = (f32[4,64,768]{2,1,0:T(8,128)S(1)}, f32[4,64,768]{2,1,0:T(8,128)}, u32[]{:S(2)}) copy-start(f32[4,64,768]{2,1,0:T(8,128)} %thick.5) | copy-start | bytes 2359300
  0.7 8.8 %copy-start.3 = (f32[4,64,768]{2,1,0:T(8,128)S(1)}, f32[4,64,768]{2,1,0:T(8,128)}, u32[]{:S(2)}) copy-start(f32[4,64,768]{2,1,0:T(8,128)} %vvel.5) | copy-start | bytes 2359300
  0.7 8.8 %copy-start.2 = (f32[4,64,768]{2,1,0:T(8,128)S(1)}, f32[4,64,768]{2,1,0:T(8,128)}, u32[]{:S(2)}) copy-start(f32[4,64,768]{2,1,0:T(8,128)} %uvel.5) | copy-start | bytes 2359300
  0.7 8.8 %copy-start.1 = (f32[4,64,768]{2,1,0:T(8,128)S(1)}, f32[4,64,768]{2,1,0:T(8,128)}, u32[]{:S(2)}) copy-start(f32[4,64,768]{2,1,0:T(8,128)} %salt.5) | copy-start | bytes 2359300
  0.7 8.8 %copy-start = (f32[4,64,768]{2,1,0:T(8,128)S(1)}, f32[4,64,768]{2,1,0:T(8,128)}, u32[]{:S(2)}) copy-start(f32[4,64,768]{2,1,0:T(8,128)} %temp.5) | copy-start | bytes 2359300
  0.7 8.8 %copy-start.8 = (f32[64,768]{1,0:T(8,128)S(1)}, f32[64,768]{1,0:T(8,128)}, u32[]{:S(2)}) copy-start(f32[64,768]{1,0:T(8,128)} %cori.5) | copy-start | bytes 589828
  2.4 21.9 %collective-permute-start = (f32[2,24,768]{2,1,0:T(8,128)S(1)}, f32[2,24,768]{2,1,0:T(8,128)S(1)}, u32[]{:S(2)}, u32[]{:S(2)}) collective-permute-start(f32[2,24,768]{2,1,0:T(8,128)S(1)} %get-tuple-element.27), channel_id=1, source_target_pairs={{0,1},{1,0},{8,9},{9,8},{16,17},{17,16},{24,25},{25,24},{32,33},{3... | collective-permute-start | bytes 442376 | tf_op jit(solution)/shard_map/ppermute | solution.py:643
  2.5 21.8 %collective-permute-start.1 = (f32[2,24,768]{2,1,0:T(8,128)S(1)}, f32[2,24,768]{2,1,0:T(8,128)S(1)}, u32[]{:S(2)}, u32[]{:S(2)}) collective-permute-start(f32[2,24,768]{2,1,0:T(8,128)S(1)} %get-tuple-element.28), channel_id=1, source_target_pairs={{1,2},{2,1},{9,10},{10,9},{17,18},{18,17},{25,26},{26,25},{33,34},... | collective-permute-start | bytes 442376 | tf_op jit(solution)/shard_map/ppermute | solution.py:644
  24.5 7.1 %collective-permute-start.3 = (f32[72,128]{1,0:T(8,128)S(1)}, f32[72,128]{1,0:T(8,128)S(1)}, u32[]{:S(2)}, u32[]{:S(2)}) collective-permute-start(f32[72,128]{1,0:T(8,128)S(1)} %get-tuple-element.38), channel_id=1, source_target_pairs={{8,16},{16,8},{24,32},{32,24},{40,48},{48,40},{56,64},{64,56},{72,... | collective-permute-start | bytes 110600 | tf_op jit(solution)/shard_map/ppermute | solution.py:650
  25.1 6.5 %collective-permute-start.2 = (f32[72,128]{1,0:T(8,128)S(1)}, f32[72,128]{1,0:T(8,128)S(1)}, u32[]{:S(2)}, u32[]{:S(2)}) collective-permute-start(f32[72,128]{1,0:T(8,128)S(1)} %get-tuple-element.38), channel_id=1, source_target_pairs={{0,8},{8,0},{16,24},{24,16},{32,40},{40,32},{48,56},{56,48},{64,72... | collective-permute-start | bytes 110600 | tf_op jit(solution)/shard_map/ppermute | solution.py:649

commit v4 on v3

--- a/solution.py
+++ b/solution.py
@@ -230,61 +230,65 @@
     return pltpu.roll(jnp.where(sub == 7, below, here), 1, 0)
 
 
-def inner_kernel(
-    temp, salt, uvel, vvel, thick, land, ewid, nwid, cori,
-    temp_out, salt_out, uvel_out, vvel_out,
-    deep, ratio_e, ratio_n, span_e, span_n, inv_area, half_e, half_n,
-    coef_e, coef_n, inv_vol, move_n, flux_t, flux_s, lap, pres, slope, over, over_e,
-):
-    level = pl.program_id(0)
+def tile(t):
+    return slice(TILE * t, TILE * t + TILE)
+
+
+def turn_e(x):
+    return pltpu.roll(x, TILE - 1, 1)
+
+
+def turn_w(x):
+    return pltpu.roll(x, 1, 1)
+
+
+def around(c):
+    r = pl.multiple_of(8 * c, 8)
+    up = pl.multiple_of(8 * jnp.minimum(c + 1, CHUNKS - 1), 8)
+    down = pl.multiple_of(8 * jnp.maximum(c - 1, 0), 8)
+    return pl.ds(r, 8), pl.ds(up, 8), pl.ds(down, 8)
+
+
+def inner_metric(ewid, nwid, known, over, over_e):
+    ratio_e, ratio_n, span_e, span_n, inv_area, half_e, half_n = known
+    last = lax.broadcasted_iota(jnp.int32, (8, TILE), 1) == TILE - 1
+
+    def chunk(c, _):
+        here, above, _ = around(c)
+        east = [(ewid[here, tile(0)], nwid[here, tile(0)])]
+        east = [tuple((x, turn_e(x)) for x in east[0])]
+        for t in range(TILES):
+            (e, re), (n, rn) = east[t]
+            u = (t + 1) % TILES
+            if u:
+                east.append(tuple((x, turn_e(x)) for x in (ewid[here, tile(u)], nwid[here, tile(u)])))
+            else:
+                east.append(east[0])
+            ee = jnp.where(last, east[t + 1][0][1], re)
+            ne = jnp.where(last, east[t + 1][1][1], rn)
+            en = north_of(e, ewid[above, tile(t)])
+            nn = north_of(n, nwid[above, tile(t)])
+            ratio_e[here, tile(t)] = (n + ne) / (e + ee)
+            ratio_n[here, tile(t)] = (e + en) / (n + nn)
+            span_e[here, tile(t)] = flux_scale * (n + ne)
+            span_n[here, tile(t)] = flux_scale * (e + en)
+            inv_area[here, tile(t)] = 1.0 / (e * n)
+            half_e[here, tile(t)] = (0.5 * time_step) / e
+            half_n[here, tile(t)] = (0.5 * time_step) / n
+            over[here, tile(t)] = jnp.zeros((8, TILE), F32)
+            over_e[here, tile(t)] = jnp.zeros((8, TILE), F32)
+        return 0
+
+    lax.fori_loop(0, CHUNKS, chunk, 0)
+
+
+def inner_level(level, fields, outs, known, work, over, over_e, keep):
+    temp, salt, uvel, vvel, thick, land, ewid, nwid, cori = fields
+    ratio_e, ratio_n, span_e, span_n, inv_area, half_e, half_n = known
+    deep, coef_e, coef_n, inv_vol, move_n, flux_t, flux_s, pres, slope, lap = work
     lane = lax.broadcasted_iota(jnp.int32, (8, TILE), 1)
     first, last = lane == 0, lane == TILE - 1
     data = (temp, salt, uvel, vvel)
-
-    def tile(t):
-        return slice(TILE * t, TILE * t + TILE)
-
-    def turn_e(x):
-        return pltpu.roll(x, TILE - 1, 1)
-
-    def turn_w(x):
-        return pltpu.roll(x, 1, 1)
-
-    def around(c):
-        r = pl.multiple_of(8 * c, 8)
-        up = pl.multiple_of(8 * jnp.minimum(c + 1, CHUNKS - 1), 8)
-        down = pl.multiple_of(8 * jnp.maximum(c - 1, 0), 8)
-        return pl.ds(r, 8), pl.ds(up, 8), pl.ds(down, 8)
-
-    @pl.when(level == 0)
-    def _():
-        def chunk(c, _):
-            here, above, _ = around(c)
-            east = [(ewid[here, tile(0)], nwid[here, tile(0)])]
-            east = [tuple((x, turn_e(x)) for x in east[0])]
-            for t in range(TILES):
-                (e, re), (n, rn) = east[t]
-                u = (t + 1) % TILES
-                if u:
-                    east.append(tuple((x, turn_e(x)) for x in (ewid[here, tile(u)], nwid[here, tile(u)])))
-                else:
-                    east.append(east[0])
-                ee = jnp.where(last, east[t + 1][0][1], re)
-                ne = jnp.where(last, east[t + 1][1][1], rn)
-                en = north_of(e, ewid[above, tile(t)])
-                nn = north_of(n, nwid[above, tile(t)])
-                ratio_e[here, tile(t)] = (n + ne) / (e + ee)
-                ratio_n[here, tile(t)] = (e + en) / (n + nn)
-                span_e[here, tile(t)] = flux_scale * (n + ne)
-                span_n[here, tile(t)] = flux_scale * (e + en)
-                inv_area[here, tile(t)] = 1.0 / (e * n)
-                half_e[here, tile(t)] = (0.5 * time_step) / e
-                half_n[here, tile(t)] = (0.5 * time_step) / n
-                over[here, tile(t)] = jnp.zeros((8, TILE), F32)
-                over_e[here, tile(t)] = jnp.zeros((8, TILE), F32)
-            return 0
-
-        lax.fori_loop(0, CHUNKS, chunk, 0)
 
     for r in range(0, ROWS, 8):
         deep[r : r + 8, :] = thick[level, r : r + 8, :] * land[level, r : r + 8, :].astype(F32)
@@ -307,7 +311,8 @@
             be = (beta_salt * east[1] - alpha_temp * east[0]) * de
             before = over_e[here, tile(t)]
             pe = before + 0.5 * be
-            over_e[here, tile(t)] = before + be
+            if keep:
+                over_e[here, tile(t)] = before + be
             return ce, flux, te, east, pe
 
         end, start = turned_at(TILES - 1), turned_at(0)
@@ -346,12 +351,13 @@
             b = (beta_salt * q1 - alpha_temp * q0) * d
             before = over[here, tile(t)]
             pres[here, tile(t)] = before + 0.5 * b
-            over[here, tile(t)] = before + b
+            if keep:
+                over[here, tile(t)] = before + b
             slope[here, tile(t)] = pe - jnp.where(lane < 2, behind_pe, turned_pe)
             behind, behind_pe, turned = turned_flux, turned_pe, ahead
         return 0
 
-    lax.fori_loop(0, CHUNKS, laps, 0)
+    lax.fori_loop(0, CHUNKS, laps, 0, unroll=2)
 
     def finish(c, _):
         here, above, below = around(c)
@@ -370,7 +376,6 @@
         kept = zonal(TILES - 1, end, start)
         kept_turned = [turn_w(x) for x in kept]
         behind, turned = kept_turned, start
-        outs = (temp_out, salt_out, uvel_out, vvel_out)
         for t in range(TILES):
             if t < TILES - 1:
                 ahead = turned_at(t + 1) if t < TILES - 2 else end
@@ -406,21 +411,36 @@
             behind, turned = turned_flux, ahead
         return 0
 
-    lax.fori_loop(0, CHUNKS, finish, 0)
+    lax.fori_loop(0, CHUNKS, finish, 0, unroll=2)
+
+
+WORK = [pltpu.VMEM((ROWS, COLS), F32)] * 9 + [pltpu.VMEM((4, ROWS, COLS), F32)]
+
+
+def inner_kernel(*refs):
+    fields, outs, known, over, over_e, work = refs[:9], refs[9:13], refs[13:20], refs[20], refs[21], refs[22:]
+    level = pl.program_id(0)
+
+    @pl.when(level == 0)
+    def _():
+        inner_metric(fields[6], fields[7], known, over, over_e)
+
+    inner_level(level, fields, outs, known, work, over, over_e, True)
 
 
 def inner(arrays, coriolis):
-    plane = pltpu.VMEM((ROWS, COLS), F32)
-    return pl.pallas_call(
+    out = [pltpu.VMEM((LEVELS, ROWS, COLS), F32)] * 4 + [pltpu.VMEM((ROWS, COLS), F32)] * 9
+    done = pl.pallas_call(
         inner_kernel,
-        grid=(LEVELS,),
+        grid=(LEVELS - 1,),
         in_specs=[VMEM] * 9,
-        out_specs=[VMEM] * 4,
-        out_shape=[pltpu.VMEM((LEVELS, ROWS, COLS), F32)] * 4,
-        scratch_shapes=[plane] * 14 + [pltpu.VMEM((4, ROWS, COLS), F32)] + [plane] * 4,
+        out_specs=[VMEM] * 13,
+        out_shape=out,
+        scratch_shapes=WORK,
         compiler_params=PARAMS,
         name="inner",
     )(*[onto_chip(x) for x in (*arrays, coriolis)])
+    return done[:4], done[4:]
 
 
 def metric(e, n, lanes, rows):
@@ -475,11 +495,8 @@
     return (outs[2], outs[3], outs[0], outs[1]), over + b
 
 
-def rims_kernel(
-    temp, salt, uvel, vvel, thick, land, ewid, nwid, cori, ghosts, temp_in, salt_in, uvel_in, vvel_in,
-    temp_out, salt_out, uvel_out, vvel_out, known, spin, over,
-):
-    level = pl.program_id(0)
+def rims_level(level, fields, ghosts, outs, known, spin, over):
+    temp, salt, uvel, vvel, thick, land, ewid, nwid, cori = fields
     sub = lax.broadcasted_iota(jnp.int32, (8, COLS), 0)
     low, high = slice(0, 8), slice(ROWS - 8, ROWS)
 
@@ -516,28 +533,68 @@
     new, over[...] = patch(
         cells, d, own(wet_low, wet_high), spin[...], [known[i] for i in range(7)], over[...], lanes, rows
     )
-    ins = (temp_in, salt_in, uvel_in, vvel_in)
-    for x, old, out in zip(new, ins, (temp_out, salt_out, uvel_out, vvel_out)):
+    for x, (old, out) in zip(new, outs):
         out[level, low, :] = jnp.where(sub < 2, pltpu.roll(x[0], 6, 0), old[level, low, :])
         out[level, high, :] = jnp.where(sub >= 6, pltpu.roll(x[1], 2, 0), old[level, high, :])
 
 
-def rims(arrays, coriolis, ghosts, outs):
+def runs_late():
+    lon, lons = lax.axis_index("lon"), lax.axis_size("lon")
+    top = lax.axis_index("lat") == lax.axis_size("lat") - 1
+    late = jnp.logical_or(lon == lons - 1, lon == lons // 2)
+    return jnp.where(top, lon == 0, late)
+
+
+def last_kernel(*refs):
+    fields, known, over, over_e, outs, work = refs[:9], refs[9:16], refs[16], refs[17], refs[22:26], refs[26:]
+
+    @pl.when(jnp.logical_not(runs_late()))
+    def _():
+        inner_level(LEVELS - 1, fields, outs, known, work, over, over_e, False)
+
+
+def rims_kernel(*refs):
+    fields, known, over, over_e, ghosts = refs[:9], refs[9:16], refs[16], refs[17], refs[18]
+    outs, rim_known, spin, rim_over, work = refs[23:27], refs[27], refs[28], refs[29], refs[30:]
+    level = pl.program_id(0)
+
+    @pl.when(jnp.logical_and(runs_late(), level == 0))
+    def _():
+        inner_level(LEVELS - 1, fields, outs, known, work, over, over_e, False)
+
+    rims_level(level, fields, ghosts, list(zip(outs, outs)), rim_known, spin, rim_over)
+
+
+def last_level(arrays, coriolis, known, outs):
+    return pl.pallas_call(
+        last_kernel,
+        in_specs=[VMEM] * 22,
+        out_specs=[VMEM] * 4,
+        out_shape=[pltpu.VMEM((LEVELS, ROWS, COLS), F32)] * 4,
+        scratch_shapes=WORK,
+        input_output_aliases={18: 0, 19: 1, 20: 2, 21: 3},
+        compiler_params=PARAMS,
+        name="last_level",
+    )(*[onto_chip(x) for x in (*arrays, coriolis, *known, *outs)])
+
+
+def rims(arrays, coriolis, known, ghosts, outs):
     return pl.pallas_call(
         rims_kernel,
         grid=(LEVELS,),
-        in_specs=[VMEM] * 14,
+        in_specs=[VMEM] * 23,
         out_specs=[VMEM] * 4,
         out_shape=[pltpu.VMEM((LEVELS, ROWS, COLS), F32)] * 4,
         scratch_shapes=[
             pltpu.VMEM((7, 2, 8, COLS), F32),
             pltpu.VMEM((2, 8, COLS), F32),
             pltpu.VMEM((2, 8, COLS), F32),
-        ],
-        input_output_aliases={10: 0, 11: 1, 12: 2, 13: 3},
+        ]
+        + WORK,
+        input_output_aliases={19: 0, 20: 1, 21: 2, 22: 3},
         compiler_params=PARAMS,
         name="rims",
-    )(*[onto_chip(x) for x in (*arrays, coriolis, ghosts, *outs)])
+    )(*[onto_chip(x) for x in (*arrays, coriolis, *known, ghosts, *outs)])
 
 
 def sides_kernel(
@@ -643,12 +700,13 @@
     near = lax.ppermute(near, AXES, lat_pairs(lats, lons, 0))
     far = lax.ppermute(far, AXES, lat_pairs(lats, lons, 1))
     win, packed = windows(arrays, coriolis)
-    outs = inner(arrays, coriolis)
+    outs, known = inner(arrays, coriolis)
+    outs = last_level(arrays, coriolis, known, outs)
     near, far, packed, *outs = lax.optimization_barrier((near, far, packed, *outs))
     packed, ghosts, corner = pack_columns(packed, near, far)
+    lon_odd = lax.ppermute(packed, AXES, lon_pairs(lats, lons, 1))
     lon_even = lax.ppermute(packed, AXES, lon_pairs(lats, lons, 0))
-    lon_odd = lax.ppermute(packed, AXES, lon_pairs(lats, lons, 1))
-    outs = rims(arrays, coriolis, ghosts, outs)
+    outs = rims(arrays, coriolis, known, ghosts, outs)
     return tuple(sides(win, corner, lon_even, lon_odd, outs))
 
 

time: 35.6 us -> 31.5 us (0.88)
  waiting for transfers between devices: 3.82 us -> 0.01 us
  Pallas kernels: 22.8 us -> 20.1 us
  starting transfers between devices: 7.98 us -> 10.4 us
    ppermute x1, waiting for transfers between devices: 3.81 us -> 0.01 us  [shards(): lon_odd = lax.ppermute(packed, AXES, lon_pairs(lats, lons, 1))]
    pallas_call x2 -> x3, Pallas kernels: 15.5 us -> 12.8 us  [the longest x1 7.94 us: inner(): pl.pallas_call(inner_kernel, grid=(LEVELS - 1,), in_specs=[VMEM] * 9, out...]
    ppermute x1, starting transfers between devices: 0.57 us -> 2.98 us  [shards(): lon_odd = lax.ppermute(packed, AXES, lon_pairs(lats, lons, 1))]
  transfers between devices with their start and end apart: 4 -> 4, of which waited for: 1 -> 0; matrix products, arithmetic and copies ran while one was open for 0% -> 0% of each run, Pallas kernels for 48% -> 46%
where the time goes in v4:
time: 31.5 us; the launch traced here: 31.4 us
  Pallas kernels  20.1 us (64%)
  starting transfers between devices  10.4 us (33%)
  between operations  0.87 us (3%)
    pallas_call x1, Pallas kernels, inner(): pl.pallas_call(inner_kernel, grid=(LEVELS - 1,), in_specs=[VMEM] * 9, out...  7.94 us
    ppermute x1, starting transfers between devices, shards(): far = lax.ppermute(far, AXES, lat_pairs(lats, lons, 1))  6.91 us
    pallas_call x1, Pallas kernels, rims(): pl.pallas_call(rims_kernel, grid=(LEVELS,), in_specs=[VMEM] * 23, out_spe...  4.84 us
    pallas_call x1, Pallas kernels, sides(): pl.pallas_call(sides_kernel, grid=(LEVELS,), in_specs=[VMEM] * 8, out_spe...  3.89 us
    ppermute x1, starting transfers between devices, shards(): lon_odd = lax.ppermute(packed, AXES, lon_pairs(lats, lons, 1))  2.98 us
    pallas_call x1, Pallas kernels, pack_rows(): pl.pallas_call(rows_kernel, grid=(1,), in_specs=[spec(a, 0) for a in arra...  1.71 us
    pallas_call x1, Pallas kernels, windows(): pl.pallas_call(windows_kernel, in_specs=[VMEM] * 9, out_specs=[VMEM] * 2,...  1.52 us
  transfers between devices with their start and end apart: 4, of which 0 were waited for; matrix products, arithmetic and copies ran while one was open for 0% of the time, Pallas kernels for 46%

profile of v4, /device:TPU:38, one launch (start us, length us, event | category | flops | bytes accessed | tf_op | source)
XLA Modules:
  0.0 31.4 jit_solution(7708012235963829819)
XLA Ops:
  0.6 0.0 copy-start.7
  0.6 0.0 copy-start.6
  0.7 0.0 copy-start.5
  0.7 0.0 copy-start.4
  0.7 0.0 copy-start.3
  0.7 0.0 copy-start.2
  0.7 0.0 copy-start.1
  0.7 0.0 copy-start
  0.7 0.0 copy-start.8
  0.7 1.7 %pack_rows.1 = (f32[2,24,768]{2,1,0:T(8,128)S(1)}, f32[2,24,768]{2,1,0:T(8,128)S(1)}) custom-call(f32[4,64,768]{2,1,0:T(8,128)} %refs_0_.7, f32[4,64,768]{2,1,0:T(8,128)} %refs_1_.7, f32[4,64,768]{2,1,0:T(8,128)} %refs_2_.7, f32[4,64,768]{2,1,0:T(8,128)} %refs_3_.7, f32[4,64,768]{2,1,0:T(8,128)} %refs_4_.7, s32[4,64,768]{2,1,0:T(8,128)} %refs_5_.7, ...), custom_call_target="tpu_custom_call" | custom-call | tf_op jit(solution)/shard_map/pack_rows/pallas_call | solution.py:124
  2.4 0.1 collective-permute-start
  2.5 6.9 %collective-permute-start.1 = (f32[2,24,768]{2,1,0:T(8,128)S(1)}, f32[2,24,768]{2,1,0:T(8,128)S(1)}, u32[]{:S(2)}, u32[]{:S(2)}) collective-permute-start(f32[2,24,768]{2,1,0:T(8,128)S(1)} %get-tuple-element.41), channel_id=1, source_target_pairs={{1,2},{2,1},{9,10},{10,9},{17,18},{18,17},{25,26},{26,25},{33,34},... | collective-permute-start | bytes 442376 | tf_op jit(solution)/shard_map/ppermute | solution.py:701
  9.4 0.0 copy-done.7
  9.5 0.0 copy-done.6
  9.5 0.0 copy-done.5
  9.5 0.0 copy-done.4
  9.5 0.0 copy-done.3
  9.5 0.0 copy-done.2
  9.5 0.0 copy-done.1
  9.5 0.0 copy-done
  9.5 0.0 copy-done.8
  9.5 1.5 %windows.1 = (f32[27,64,128]{2,1,0:T(8,128)S(1)}, f32[64,128]{1,0:T(8,128)S(1)}) custom-call(f32[4,64,768]{2,1,0:T(8,128)S(1)} %copy-done, f32[4,64,768]{2,1,0:T(8,128)S(1)} %copy-done.1, f32[4,64,768]{2,1,0:T(8,128)S(1)} %copy-done.2, f32[4,64,768]{2,1,0:T(8,128)S(1)} %copy-done.3, f32[4,64,768]{2,1,0:T(8,128)S(1)} %copy-done.4, ...), custom_call_target="tpu_custom_call" | custom-call | tf_op jit(solution)/shard_map/windows/pallas_call | solution.py:172
  11.1 7.9 %inner.1 = (f32[4,64,768]{2,1,0:T(8,128)S(1)}, f32[4,64,768]{2,1,0:T(8,128)S(1)}, f32[4,64,768]{2,1,0:T(8,128)S(1)}, f32[4,64,768]{2,1,0:T(8,128)S(1)}, f32[64,7...) custom-call(f32[4,64,768]{2,1,0:T(8,128)S(1)} %copy-done, ...), custom_call_target="tpu_custom_call" | custom-call | tf_op jit(solution)/shard_map/inner/pallas_call | solution.py:433
  19.0 0.0 collective-permute-done.near
  19.1 0.0 collective-permute-done.1.far
  19.1 0.2 pack_columns.1
  19.2 3.0 %collective-permute-start.3 = (f32[72,128]{1,0:T(8,128)S(1)}, f32[72,128]{1,0:T(8,128)S(1)}, u32[]{:S(2)}, u32[]{:S(2)}) collective-permute-start(f32[72,128]{1,0:T(8,128)S(1)} %get-tuple-element.64), channel_id=1, source_target_pairs={{8,16},{16,8},{24,32},{32,24},{40,48},{48,40},{56,64},{64,56},{72,... | collective-permute-start | bytes 110600 | tf_op jit(solution)/shard_map/ppermute | solution.py:707
  22.2 0.4 %collective-permute-start.2 = (f32[72,128]{1,0:T(8,128)S(1)}, f32[72,128]{1,0:T(8,128)S(1)}, u32[]{:S(2)}, u32[]{:S(2)}) collective-permute-start(f32[72,128]{1,0:T(8,128)S(1)} %get-tuple-element.64), channel_id=1, source_target_pairs={{0,8},{8,0},{16,24},{24,16},{32,40},{40,32},{48,56},{56,48},{64,72... | collective-permute-start | bytes 110600 | tf_op jit(solution)/shard_map/ppermute | solution.py:708
  22.6 4.8 %rims.1 = (f32[4,64,768]{2,1,0:T(8,128)S(1)}, f32[4,64,768]{2,1,0:T(8,128)S(1)}, f32[4,64,768]{2,1,0:T(8,128)S(1)}, f32[4,64,768]{2,1,0:T(8,128)S(1)}) custom-call(f32[4,64,768]{2,1,0:T(8,128)S(1)} %copy-done, f32[4,64,768]{2,1,0:T(8,128)S(1)} %copy-done.1, ...), custom_call_target="tpu_custom_call", output_to_operand_aliasing={{0}: (19, {}), {1}: (20, {}), {2}: (21, {}), {3}: (22, {})} | custom-call | tf_op jit(solution)/shard_map/rims/pallas_call | solution.py:582
  27.5 0.0 collective-permute-done.3.lon_odd
  27.5 0.0 collective-permute-done.2.lon_even
  27.5 3.9 %sides.1 = (f32[4,64,768]{2,1,0:T(8,128)}, f32[4,64,768]{2,1,0:T(8,128)}, f32[4,64,768]{2,1,0:T(8,128)}, f32[4,64,768]{2,1,0:T(8,128)}) custom-call(f32[27,64,128]{2,1,0:T(8,128)S(1)} %get-tuple-element.39.win, f32[4,24,128]{2,1,0:T(8,128)S(1)} %get-tuple-element.63.corner, f32[72,128]{1,0:T(8,128)S(1)} %collective-permute-done.2.lon_even, ...), custom_call_target="tpu_custom_call" | custom-call | tf_op jit(solution)/shard_map/sides/pallas_call | solution.py:676
  (1 shorter events, 0.0 us)
Async XLA Ops:
  0.6 8.8 %copy-start.7 = (f32[64,768]{1,0:T(8,128)S(1)}, f32[64,768]{1,0:T(8,128)}, u32[]{:S(2)}) copy-start(f32[64,768]{1,0:T(8,128)} %refs_7_.7) | copy-start | bytes 589828
  0.6 8.8 %copy-start.6 = (f32[64,768]{1,0:T(8,128)S(1)}, f32[64,768]{1,0:T(8,128)}, u32[]{:S(2)}) copy-start(f32[64,768]{1,0:T(8,128)} %refs_6_.7) | copy-start | bytes 589828
  0.7 8.8 %copy-start.5 = (s32[4,64,768]{2,1,0:T(8,128)S(1)}, s32[4,64,768]{2,1,0:T(8,128)}, u32[]{:S(2)}) copy-start(s32[4,64,768]{2,1,0:T(8,128)} %refs_5_.7) | copy-start | bytes 2359300
  0.7 8.8 %copy-start.4 = (f32[4,64,768]{2,1,0:T(8,128)S(1)}, f32[4,64,768]{2,1,0:T(8,128)}, u32[]{:S(2)}) copy-start(f32[4,64,768]{2,1,0:T(8,128)} %refs_4_.7) | copy-start | bytes 2359300
  0.7 8.8 %copy-start.3 = (f32[4,64,768]{2,1,0:T(8,128)S(1)}, f32[4,64,768]{2,1,0:T(8,128)}, u32[]{:S(2)}) copy-start(f32[4,64,768]{2,1,0:T(8,128)} %refs_3_.7) | copy-start | bytes 2359300
  0.7 8.8 %copy-start.2 = (f32[4,64,768]{2,1,0:T(8,128)S(1)}, f32[4,64,768]{2,1,0:T(8,128)}, u32[]{:S(2)}) copy-start(f32[4,64,768]{2,1,0:T(8,128)} %refs_2_.7) | copy-start | bytes 2359300
  0.7 8.8 %copy-start.1 = (f32[4,64,768]{2,1,0:T(8,128)S(1)}, f32[4,64,768]{2,1,0:T(8,128)}, u32[]{:S(2)}) copy-start(f32[4,64,768]{2,1,0:T(8,128)} %refs_1_.7) | copy-start | bytes 2359300
  0.7 8.8 %copy-start = (f32[4,64,768]{2,1,0:T(8,128)S(1)}, f32[4,64,768]{2,1,0:T(8,128)}, u32[]{:S(2)}) copy-start(f32[4,64,768]{2,1,0:T(8,128)} %refs_0_.7) | copy-start | bytes 2359300
  0.7 8.8 %copy-start.8 = (f32[64,768]{1,0:T(8,128)S(1)}, f32[64,768]{1,0:T(8,128)}, u32[]{:S(2)}) copy-start(f32[64,768]{1,0:T(8,128)} %refs_8_.7) | copy-start | bytes 589828
  2.4 16.6 %collective-permute-start = (f32[2,24,768]{2,1,0:T(8,128)S(1)}, f32[2,24,768]{2,1,0:T(8,128)S(1)}, u32[]{:S(2)}, u32[]{:S(2)}) collective-permute-start(f32[2,24,768]{2,1,0:T(8,128)S(1)} %get-tuple-element.40), channel_id=1, source_target_pairs={{0,1},{1,0},{8,9},{9,8},{16,17},{17,16},{24,25},{25,24},{32,33},{3... | collective-permute-start | bytes 442376 | tf_op jit(solution)/shard_map/ppermute | solution.py:700
  2.5 16.5 %collective-permute-start.1 = (f32[2,24,768]{2,1,0:T(8,128)S(1)}, f32[2,24,768]{2,1,0:T(8,128)S(1)}, u32[]{:S(2)}, u32[]{:S(2)}) collective-permute-start(f32[2,24,768]{2,1,0:T(8,128)S(1)} %get-tuple-element.41), channel_id=1, source_target_pairs={{1,2},{2,1},{9,10},{10,9},{17,18},{18,17},{25,26},{26,25},{33,34},... | collective-permute-start | bytes 442376 | tf_op jit(solution)/shard_map/ppermute | solution.py:701
  19.2 8.2 %collective-permute-start.3 = (f32[72,128]{1,0:T(8,128)S(1)}, f32[72,128]{1,0:T(8,128)S(1)}, u32[]{:S(2)}, u32[]{:S(2)}) collective-permute-start(f32[72,128]{1,0:T(8,128)S(1)} %get-tuple-element.64), channel_id=1, source_target_pairs={{8,16},{16,8},{24,32},{32,24},{40,48},{48,40},{56,64},{64,56},{72,... | collective-permute-start | bytes 110600 | tf_op jit(solution)/shard_map/ppermute | solution.py:707
  22.2 5.3 %collective-permute-start.2 = (f32[72,128]{1,0:T(8,128)S(1)}, f32[72,128]{1,0:T(8,128)S(1)}, u32[]{:S(2)}, u32[]{:S(2)}) collective-permute-start(f32[72,128]{1,0:T(8,128)S(1)} %get-tuple-element.64), channel_id=1, source_target_pairs={{0,8},{8,0},{16,24},{24,16},{32,40},{40,32},{48,56},{56,48},{64,72... | collective-permute-start | bytes 110600 | tf_op jit(solution)/shard_map/ppermute | solution.py:708

commit v5 on v4

--- a/solution.py
+++ b/solution.py
@@ -20,7 +20,8 @@
 CHUNKS = ROWS // 8
 TALL = ROWS + 16
 FIELDS = 22
-SHOWN = FIELDS + LEVELS + 1
+KINDS = 6
+GROUP = TILE // LEVELS
 F32 = jnp.float32
 PARAMS = pltpu.CompilerParams(vmem_limit_bytes=12 * 1024 * 1024)
 AXES = ("lon", "lat")
@@ -133,38 +134,51 @@
     )(*[off_chip(x) for x in (*arrays, *arrays)])
 
 
-def packed_field():
-    def of(shape):
-        lane = lax.broadcasted_iota(jnp.int32, shape, len(shape) - 1)
-        return ((lane + 2) & (TILE - 1)) >> 1
-
-    return of
+def slot_of(shape):
+    return ((lax.broadcasted_iota(jnp.int32, shape, len(shape) - 1) + 2) & (GROUP - 1)) >> 1
+
+
+def level_of(shape):
+    return ((lax.broadcasted_iota(jnp.int32, shape, len(shape) - 1) + 8) >> 5) & (LEVELS - 1)
+
+
+def join_ends(low, high):
+    lane = lax.broadcasted_iota(jnp.int32, low.shape, len(low.shape) - 1)
+    return jnp.where(lane < 8, low, pltpu.roll(high, 16, len(low.shape) - 1))
 
 
 def windows_kernel(temp, salt, uvel, vvel, thick, land, ewid, nwid, cori, win, packed):
-    lane = lax.broadcasted_iota(jnp.int32, (ROWS, TILE), 1)
-    field = packed_field()((ROWS, TILE))
-    total = jnp.zeros((ROWS, TILE), F32)
-
-    def edge(f, cut):
-        kind, level = divmod(f, LEVELS)
+    shape = (ROWS, TILE)
+    lane = lax.broadcasted_iota(jnp.int32, shape, 1)
+    slot = slot_of(shape)
+    ends = (slice(0, TILE), slice(COLS - TILE, COLS))
+    total = jnp.zeros(shape, F32)
+
+    def spread(parts):
+        whole = parts[0]
+        for level in range(1, len(parts)):
+            whole = jnp.where(lane >= GROUP * level, pltpu.roll(parts[level], GROUP * level, 1), whole)
+        return whole
+
+    def at(kind, level, cut):
         if kind < 4:
             return (temp, salt, uvel, vvel)[kind][level, :, cut]
         if kind == 4:
             return thick[level, :, cut] * land[level, :, cut].astype(F32)
-        if f < FIELDS:
-            return (ewid, nwid)[f - 20][:, cut]
-        if f < FIELDS + LEVELS:
-            return land[f - FIELDS, :, cut].astype(F32)
+        if kind == 5:
+            return (ewid, nwid)[level][:, cut]
+        if kind == 6:
+            return land[level, :, cut].astype(F32)
         return cori[:, cut]
 
-    for f in range(SHOWN):
-        low, high = edge(f, slice(0, TILE)), edge(f, slice(COLS - TILE, COLS))
-        cells = jnp.where(lane < TILE // 4, low, pltpu.roll(high, TILE // 2, 1))
-        win[f] = cells
-        if f < FIELDS:
-            mine = jnp.logical_or(field == f, field == f + 33)
-            total = jnp.where(mine, pltpu.roll(cells, (TILE // 2 + 2 * f) % TILE, 1), total)
+    for kind in range(KINDS + 2):
+        count = (LEVELS, 2, LEVELS, 1)[max(kind - 4, 0)]
+        parts = [join_ends(*[at(kind, level, cut) for cut in ends]) for level in range(count)]
+        cells = spread(parts * LEVELS if count == 1 else parts)
+        win[kind] = cells
+        if kind < KINDS:
+            total = jnp.where(slot == 9 + kind, pltpu.roll(cells, 16 + 2 * kind, 1), total)
+            total = jnp.where(slot == kind, pltpu.roll(cells, TILE - 16 + 2 * kind, 1), total)
     packed[...] = total
 
 
@@ -173,7 +187,7 @@
         windows_kernel,
         in_specs=[VMEM] * 9,
         out_specs=[VMEM] * 2,
-        out_shape=[pltpu.VMEM((SHOWN, ROWS, TILE), F32), pltpu.VMEM((ROWS, TILE), F32)],
+        out_shape=[pltpu.VMEM((KINDS + 2, ROWS, TILE), F32), pltpu.VMEM((ROWS, TILE), F32)],
         compiler_params=PARAMS,
         name="windows",
     )(*[onto_chip(x) for x in (*arrays, coriolis)])
@@ -186,9 +200,10 @@
     row = lax.broadcasted_iota(jnp.int32, (24, COLS), 0)
     fill = jnp.logical_and(lat == 0, row >= 20)
     lane = lax.broadcasted_iota(jnp.int32, (24, TILE), 1)
-    field = packed_field()((24, TILE))
     small_row = lax.broadcasted_iota(jnp.int32, (24, TILE), 0)
-    mine = jnp.logical_or(field == small_row, field == small_row + 33)
+    mine = jnp.logical_and(lane >> 5 == small_row & (LEVELS - 1), lane & (GROUP - 1) < 16)
+    slot = slot_of((8, TILE))
+    kind = lax.broadcasted_iota(jnp.int32, (8, TILE), 0)
     for k in range(2):
         a, b = near[k], far[k]
         for side in range(2):
@@ -198,10 +213,18 @@
                 cells = jnp.where(fill, 1.0, jnp.where(odd, a, b))
             at = 2 * side + k
             ghosts[at] = cells
-            shown = jnp.where(lane < TILE // 4, cells[:, 0:TILE], pltpu.roll(cells[:, COLS - TILE : COLS], TILE // 2, 1))
+            ends = join_ends(cells[:, 0:TILE], cells[:, COLS - TILE : COLS])
+            moved = ends
+            for level in range(1, LEVELS):
+                moved = jnp.where(small_row & (LEVELS - 1) == level, pltpu.roll(ends, GROUP * level, 1), moved)
+            ends = jnp.where(mine, moved, 0.0)
+            rows = [jnp.sum(ends[LEVELS * i : LEVELS * (i + 1)], axis=0, keepdims=True) for i in range(KINDS)]
+            shown = jnp.concatenate(rows + [jnp.zeros((8 - KINDS, TILE), F32)], axis=0)
             corner[at] = shown
-            spread = pltpu.roll(shown, TILE // 2, 1, stride=2, stride_axis=0)
-            out[ROWS + at : ROWS + at + 1, :] = jnp.sum(jnp.where(mine, spread, 0.0), axis=0, keepdims=True)
+            east = pltpu.roll(shown, 16, 1, stride=2, stride_axis=0)
+            west = pltpu.roll(shown, TILE - 16, 1, stride=2, stride_axis=0)
+            sent = jnp.where(slot == kind + 9, east, jnp.where(slot == kind, west, 0.0))
+            out[ROWS + at : ROWS + at + 1, :] = jnp.sum(sent[0:KINDS], axis=0, keepdims=True)
     out[ROWS + 4 : ROWS + 8, :] = jnp.zeros((4, TILE), F32)
 
 
@@ -213,7 +236,7 @@
         out_shape=[
             pltpu.VMEM((ROWS + 8, TILE), F32),
             pltpu.VMEM((4, 24, COLS), F32),
-            pltpu.VMEM((4, 24, TILE), F32),
+            pltpu.VMEM((4, 8, TILE), F32),
         ],
         compiler_params=PARAMS,
         name="pack_columns",
@@ -456,7 +479,7 @@
     )
 
 
-def patch(cells, d, wet, cori, known, over, lanes, rows):
+def patch(cells, d, wet, cori, known, overhead, lanes, rows):
     ratio_e, ratio_n, span_e, span_n, inv_area, half_e, half_n = known
     temp, salt, uvel, vvel = cells
     de, dn = lanes(d, 1), rows(d, 1)
@@ -465,7 +488,7 @@
     cs = rows(cn, -1)
     iv = inv_area / jnp.maximum(d, thin_floor)
     b = (beta_salt * salt - alpha_temp * temp) * d
-    p = over + 0.5 * b
+    p = overhead(b) + 0.5 * b
     ge = (lanes(p, 1) - lanes(p, -1)) * half_e
     gn = (rows(p, 1) - rows(p, -1)) * half_n
     outs = []
@@ -492,7 +515,7 @@
         if f == 3:
             change = change - time_step * cori * uvel - gn
         outs.append(wet * change)
-    return (outs[2], outs[3], outs[0], outs[1]), over + b
+    return outs[2], outs[3], outs[0], outs[1]
 
 
 def rims_level(level, fields, ghosts, outs, known, spin, over):
@@ -530,8 +553,14 @@
     ]
     wet_low, wet_high = land[level, low, :].astype(F32), land[level, high, :].astype(F32)
     d = strips(4 * LEVELS + level, thick[level, low, :] * wet_low, thick[level, high, :] * wet_high)
-    new, over[...] = patch(
-        cells, d, own(wet_low, wet_high), spin[...], [known[i] for i in range(7)], over[...], lanes, rows
+
+    def overhead(b):
+        before = over[...]
+        over[...] = before + b
+        return before
+
+    new = patch(
+        cells, d, own(wet_low, wet_high), spin[...], [known[i] for i in range(7)], overhead, lanes, rows
     )
     for x, (old, out) in zip(new, outs):
         out[level, low, :] = jnp.where(sub < 2, pltpu.roll(x[0], 6, 0), old[level, low, :])
@@ -600,23 +629,25 @@
 def sides_kernel(
     win, corner, lon_even, lon_odd, temp_in, salt_in, uvel_in, vvel_in,
     temp_out, salt_out, uvel_out, vvel_out,
-    side, known, over, edges, mid_sem, low_sem, high_sem,
+    side, edges, mid_sem, low_sem, high_sem,
 ):
-    level = pl.program_id(0)
     ins, outs = (temp_in, salt_in, uvel_in, vvel_in), (temp_out, salt_out, uvel_out, vvel_out)
-    lane = lax.broadcasted_iota(jnp.int32, (TALL, TILE), 1)
-    field = packed_field()((TALL, TILE))
-    ghost_lane = jnp.logical_or(field == 0, field == 33)
+    shape = (TALL, TILE)
+    level, slot = level_of(shape), slot_of(shape)
+    ghost_lane = jnp.logical_or(slot == 0, slot == 9)
     middle = pl.ds(TILE, COLS - 2 * TILE)
 
-    def mid_copy(i):
+    def middle_copy(i):
         return pltpu.make_async_copy(ins[i].at[:, :, middle], outs[i].at[:, :, middle], mid_sem.at[i])
 
-    def edge_copies(i, at):
-        return (
-            pltpu.make_async_copy(edges.at[0, i, at], outs[i].at[at, :, pl.ds(0, TILE)], low_sem.at[i, at]),
-            pltpu.make_async_copy(edges.at[1, i, at], outs[i].at[at, :, pl.ds(COLS - TILE, TILE)], high_sem.at[i, at]),
-        )
+    def low_copy(i):
+        return pltpu.make_async_copy(edges.at[0, i], outs[i].at[:, :, pl.ds(0, TILE)], low_sem.at[i])
+
+    def high_copy(i):
+        return pltpu.make_async_copy(edges.at[1, i], outs[i].at[:, :, pl.ds(COLS - TILE, TILE)], high_sem.at[i])
+
+    for i in range(4):
+        middle_copy(i).start()
 
     def lanes(x, by):
         return pltpu.roll(x, TILE - 1 if by > 0 else 1, 1)
@@ -628,65 +659,63 @@
         pad = jnp.zeros((6, TILE), F32)
         return jnp.concatenate([pad, south, body, north, pad], axis=0)
 
-    def extended(f):
-        shift = (TILE - 2 * f) & (TILE - 1)
-        base = tall(
-            win[f],
-            jnp.concatenate([corner[k, pl.ds(f, 1), :] for k in (0, 1)], axis=0),
-            jnp.concatenate([corner[k, pl.ds(f, 1), :] for k in (2, 3)], axis=0),
-        )
-        return jnp.where(ghost_lane, pltpu.roll(side[...], shift, 1), base)
-
-    @pl.when(level == 0)
-    def _():
-        for i in range(4):
-            mid_copy(i).start()
-        odd = lax.axis_index("lon") % 2 == 1
-        a, b = lon_even[...], lon_odd[...]
-        got = jnp.where(packed_field()((ROWS + 8, TILE)) >= 33, jnp.where(odd, b, a), jnp.where(odd, a, b))
-        side[...] = tall(got[0:ROWS], got[ROWS : ROWS + 2], got[ROWS + 2 : ROWS + 4])
-        e, n = extended(20), extended(21)
-        for i, x in enumerate(metric(e, n, lanes, rows)):
-            known[i] = x
-        over[...] = jnp.zeros((TALL, TILE), F32)
-
-    cells = [extended(LEVELS * kind + level) for kind in range(4)]
-    d = extended(4 * LEVELS + level)
+    odd = lax.axis_index("lon") % 2 == 1
+    a, b = lon_even[...], lon_odd[...]
+    got = jnp.where(slot_of((ROWS + 8, TILE)) >= 9, jnp.where(odd, b, a), jnp.where(odd, a, b))
+    side[...] = tall(got[0:ROWS], got[ROWS : ROWS + 2], got[ROWS + 2 : ROWS + 4])
+
+    def extended(kind):
+        ends = [jnp.concatenate([corner[k, kind : kind + 1, :] for k in pair], axis=0) for pair in ((0, 1), (2, 3))]
+        came = side[...]
+        if kind:
+            came = pltpu.roll(came, TILE - 2 * kind, 1)
+        return jnp.where(ghost_lane, came, tall(win[kind], *ends))
+
+    def everywhere(x):
+        return jnp.where(level < 2, x, pltpu.roll(x, 2 * GROUP, 1))
+
+    pair = extended(5)
+    e = everywhere(jnp.where(level == 0, pair, pltpu.roll(pair, GROUP, 1)))
+    n = everywhere(jnp.where(level == 0, pltpu.roll(pair, TILE - GROUP, 1), pair))
+
+    def overhead(b):
+        total = jnp.where(level > 0, pltpu.roll(b, GROUP, 1), 0.0)
+        for up in (2, 3):
+            total = total + jnp.where(level >= up, pltpu.roll(b, GROUP * up, 1), 0.0)
+        return total
+
+    cells = [extended(kind) for kind in range(4)]
     blank = jnp.zeros((2, TILE), F32)
-    wet, spin = tall(win[FIELDS + level], blank, blank), tall(win[FIELDS + LEVELS], blank, blank)
-    new, over[...] = patch(cells, d, wet, spin, [known[i] for i in range(7)], over[...], lanes, rows)
-    own = lax.broadcasted_iota(jnp.int32, (ROWS, TILE), 1)
+    wet, spin = tall(win[KINDS], blank, blank), tall(win[KINDS + 1], blank, blank)
+    new = patch(cells, extended(4), wet, spin, metric(e, n, lanes, rows), overhead, lanes, rows)
+    lane = lax.broadcasted_iota(jnp.int32, (ROWS, TILE), 1)
     for i, x in enumerate(new):
         x = x[8 : 8 + ROWS]
-        edges[0, i, level] = jnp.where(own < 2, x, ins[i][level, :, 0:TILE])
-        edges[1, i, level] = jnp.where(own >= TILE - 2, pltpu.roll(x, TILE // 2, 1), ins[i][level, :, COLS - TILE : COLS])
-        for copy in edge_copies(i, level):
-            copy.start()
-
-    @pl.when(level == LEVELS - 1)
-    def _():
-        for i in range(4):
-            mid_copy(i).wait()
-            for at in range(LEVELS):
-                for copy in edge_copies(i, at):
-                    copy.wait()
+        x = jnp.where(lane & (GROUP - 1) < 8, x, pltpu.roll(x, TILE - 16, 1))
+        for at in range(LEVELS):
+            own = pltpu.roll(x, TILE - GROUP * at, 1) if at else x
+            edges[0, i, at] = jnp.where(lane < 2, own, ins[i][at, :, 0:TILE])
+            edges[1, i, at] = jnp.where(lane >= TILE - 2, own, ins[i][at, :, COLS - TILE : COLS])
+        low_copy(i).start()
+        high_copy(i).start()
+    for i in range(4):
+        middle_copy(i).wait()
+        low_copy(i).wait()
+        high_copy(i).wait()
 
 
 def sides(win, corner, lon_even, lon_odd, outs):
     return pl.pallas_call(
         sides_kernel,
-        grid=(LEVELS,),
         in_specs=[VMEM] * 8,
         out_specs=[pl.BlockSpec(memory_space=pltpu.HBM)] * 4,
         out_shape=[jax.ShapeDtypeStruct((LEVELS, ROWS, COLS), F32)] * 4,
         scratch_shapes=[
             pltpu.VMEM((TALL, TILE), F32),
-            pltpu.VMEM((7, TALL, TILE), F32),
-            pltpu.VMEM((TALL, TILE), F32),
             pltpu.VMEM((2, 4, LEVELS, ROWS, TILE), F32),
             pltpu.SemaphoreType.DMA((4,)),
-            pltpu.SemaphoreType.DMA((4, LEVELS)),
-            pltpu.SemaphoreType.DMA((4, LEVELS)),
+            pltpu.SemaphoreType.DMA((4,)),
+            pltpu.SemaphoreType.DMA((4,)),
         ],
         compiler_params=PARAMS,
         name="sides",

time: 31.5 us -> 29.6 us (0.940)
  Pallas kernels: 20.1 us -> 18.2 us
    pallas_call x1, Pallas kernels: 3.89 us -> 2.18 us  [sides(): pl.pallas_call(sides_kernel, in_specs=[VMEM] * 8, out_specs=[pl.BlockSpec...]
    pallas_call x1, Pallas kernels: 1.52 us -> 1.17 us  [windows(): pl.pallas_call(windows_kernel, in_specs=[VMEM] * 9, out_specs=[VMEM] * 2,...]
  transfers between devices with their start and end apart: 4 -> 4, of which waited for: 0 -> 0; matrix products, arithmetic and copies ran while one was open for 0% -> 0% of each run, Pallas kernels for 46% -> 47%
where the time goes in v5:
time: 29.6 us; the launch traced here: 29.5 us
  Pallas kernels  18.2 us (61%)
  starting transfers between devices  10.4 us (35%)
  between operations  0.87 us (3%)
    pallas_call x1, Pallas kernels, inner(): pl.pallas_call(inner_kernel, grid=(LEVELS - 1,), in_specs=[VMEM] * 9, out...  7.95 us
    ppermute x1, starting transfers between devices, shards(): far = lax.ppermute(far, AXES, lat_pairs(lats, lons, 1))  6.91 us
    pallas_call x1, Pallas kernels, rims(): pl.pallas_call(rims_kernel, grid=(LEVELS,), in_specs=[VMEM] * 23, out_spe...  4.85 us
    ppermute x1, starting transfers between devices, shards(): lon_odd = lax.ppermute(packed, AXES, lon_pairs(lats, lons, 1))  2.98 us
    pallas_call x1, Pallas kernels, sides(): pl.pallas_call(sides_kernel, in_specs=[VMEM] * 8, out_specs=[pl.BlockSpec...  2.18 us
    pallas_call x1, Pallas kernels, pack_rows(): pl.pallas_call(rows_kernel, grid=(1,), in_specs=[spec(a, 0) for a in arra...  1.71 us
    pallas_call x1, Pallas kernels, windows(): pl.pallas_call(windows_kernel, in_specs=[VMEM] * 9, out_specs=[VMEM] * 2,...  1.17 us
  transfers between devices with their start and end apart: 4, of which 0 were waited for; matrix products, arithmetic and copies ran while one was open for 0% of the time, Pallas kernels for 47%

profile of v5, /device:TPU:38, one launch (start us, length us, event | category | flops | bytes accessed | tf_op | source)
XLA Modules:
  0.0 29.5 jit_solution(5864856294723789593)
XLA Ops:
  0.6 0.0 copy-start.7
  0.6 0.0 copy-start.6
  0.7 0.0 copy-start.5
  0.7 0.0 copy-start.4
  0.7 0.0 copy-start.3
  0.7 0.0 copy-start.2
  0.7 0.0 copy-start.1
  0.7 0.0 copy-start
  0.7 0.0 copy-start.8
  0.7 1.7 %pack_rows.1 = (f32[2,24,768]{2,1,0:T(8,128)S(1)}, f32[2,24,768]{2,1,0:T(8,128)S(1)}) custom-call(f32[4,64,768]{2,1,0:T(8,128)} %refs_0_.7, f32[4,64,768]{2,1,0:T(8,128)} %refs_1_.7, f32[4,64,768]{2,1,0:T(8,128)} %refs_2_.7, f32[4,64,768]{2,1,0:T(8,128)} %refs_3_.7, f32[4,64,768]{2,1,0:T(8,128)} %refs_4_.7, s32[4,64,768]{2,1,0:T(8,128)} %refs_5_.7, ...), custom_call_target="tpu_custom_call" | custom-call | tf_op jit(solution)/shard_map/pack_rows/pallas_call | solution.py:125
  2.4 0.1 collective-permute-start
  2.5 6.9 %collective-permute-start.1 = (f32[2,24,768]{2,1,0:T(8,128)S(1)}, f32[2,24,768]{2,1,0:T(8,128)S(1)}, u32[]{:S(2)}, u32[]{:S(2)}) collective-permute-start(f32[2,24,768]{2,1,0:T(8,128)S(1)} %get-tuple-element.41), channel_id=1, source_target_pairs={{1,2},{2,1},{9,10},{10,9},{17,18},{18,17},{25,26},{26,25},{33,34},... | collective-permute-start | bytes 442376 | tf_op jit(solution)/shard_map/ppermute | solution.py:730
  9.4 0.0 copy-done.7
  9.5 0.0 copy-done.6
  9.5 0.0 copy-done.5
  9.5 0.0 copy-done.4
  9.5 0.0 copy-done.3
  9.5 0.0 copy-done.2
  9.5 0.0 copy-done.1
  9.5 0.0 copy-done
  9.5 0.0 copy-done.8
  9.5 1.2 %windows.1 = (f32[8,64,128]{2,1,0:T(8,128)S(1)}, f32[64,128]{1,0:T(8,128)S(1)}) custom-call(f32[4,64,768]{2,1,0:T(8,128)S(1)} %copy-done, f32[4,64,768]{2,1,0:T(8,128)S(1)} %copy-done.1, f32[4,64,768]{2,1,0:T(8,128)S(1)} %copy-done.2, f32[4,64,768]{2,1,0:T(8,128)S(1)} %copy-done.3, f32[4,64,768]{2,1,0:T(8,128)S(1)} %copy-done.4, ...), custom_call_target="tpu_custom_call" | custom-call | tf_op jit(solution)/shard_map/windows/pallas_call | solution.py:186
  10.7 8.0 %inner.1 = (f32[4,64,768]{2,1,0:T(8,128)S(1)}, f32[4,64,768]{2,1,0:T(8,128)S(1)}, f32[4,64,768]{2,1,0:T(8,128)S(1)}, f32[4,64,768]{2,1,0:T(8,128)S(1)}, f32[64,7...) custom-call(f32[4,64,768]{2,1,0:T(8,128)S(1)} %copy-done, ...), custom_call_target="tpu_custom_call" | custom-call | tf_op jit(solution)/shard_map/inner/pallas_call | solution.py:456
  18.7 0.0 collective-permute-done.near
  18.7 0.0 collective-permute-done.1.far
  18.7 0.3 pack_columns.1
  19.0 3.0 %collective-permute-start.3 = (f32[72,128]{1,0:T(8,128)S(1)}, f32[72,128]{1,0:T(8,128)S(1)}, u32[]{:S(2)}, u32[]{:S(2)}) collective-permute-start(f32[72,128]{1,0:T(8,128)S(1)} %get-tuple-element.64), channel_id=1, source_target_pairs={{8,16},{16,8},{24,32},{32,24},{40,48},{48,40},{56,64},{64,56},{72,... | collective-permute-start | bytes 110600 | tf_op jit(solution)/shard_map/ppermute | solution.py:736
  22.0 0.4 %collective-permute-start.2 = (f32[72,128]{1,0:T(8,128)S(1)}, f32[72,128]{1,0:T(8,128)S(1)}, u32[]{:S(2)}, u32[]{:S(2)}) collective-permute-start(f32[72,128]{1,0:T(8,128)S(1)} %get-tuple-element.64), channel_id=1, source_target_pairs={{0,8},{8,0},{16,24},{24,16},{32,40},{40,32},{48,56},{56,48},{64,72... | collective-permute-start | bytes 110600 | tf_op jit(solution)/shard_map/ppermute | solution.py:737
  22.4 4.9 %rims.1 = (f32[4,64,768]{2,1,0:T(8,128)S(1)}, f32[4,64,768]{2,1,0:T(8,128)S(1)}, f32[4,64,768]{2,1,0:T(8,128)S(1)}, f32[4,64,768]{2,1,0:T(8,128)S(1)}) custom-call(f32[4,64,768]{2,1,0:T(8,128)S(1)} %copy-done, f32[4,64,768]{2,1,0:T(8,128)S(1)} %copy-done.1, ...), custom_call_target="tpu_custom_call", output_to_operand_aliasing={{0}: (19, {}), {1}: (20, {}), {2}: (21, {}), {3}: (22, {})} | custom-call | tf_op jit(solution)/shard_map/rims/pallas_call | solution.py:611
  27.3 0.0 collective-permute-done.3.lon_odd
  27.3 0.0 collective-permute-done.2.lon_even
  27.3 2.2 %sides.1 = (f32[4,64,768]{2,1,0:T(8,128)}, f32[4,64,768]{2,1,0:T(8,128)}, f32[4,64,768]{2,1,0:T(8,128)}, f32[4,64,768]{2,1,0:T(8,128)}) custom-call(f32[8,64,128]{2,1,0:T(8,128)S(1)} %get-tuple-element.39.win, f32[4,8,128]{2,1,0:T(8,128)S(1)} %get-tuple-element.63.corner, f32[72,128]{1,0:T(8,128)S(1)} %collective-permute-done.2.lon_even, ...), custom_call_target="tpu_custom_call" | custom-call | tf_op jit(solution)/shard_map/sides/pallas_call | solution.py:708
  (1 shorter events, 0.0 us)
Async XLA Ops:
  0.6 8.8 %copy-start.7 = (f32[64,768]{1,0:T(8,128)S(1)}, f32[64,768]{1,0:T(8,128)}, u32[]{:S(2)}) copy-start(f32[64,768]{1,0:T(8,128)} %refs_7_.7) | copy-start | bytes 589828
  0.6 8.8 %copy-start.6 = (f32[64,768]{1,0:T(8,128)S(1)}, f32[64,768]{1,0:T(8,128)}, u32[]{:S(2)}) copy-start(f32[64,768]{1,0:T(8,128)} %refs_6_.7) | copy-start | bytes 589828
  0.7 8.8 %copy-start.5 = (s32[4,64,768]{2,1,0:T(8,128)S(1)}, s32[4,64,768]{2,1,0:T(8,128)}, u32[]{:S(2)}) copy-start(s32[4,64,768]{2,1,0:T(8,128)} %refs_5_.7) | copy-start | bytes 2359300
  0.7 8.8 %copy-start.4 = (f32[4,64,768]{2,1,0:T(8,128)S(1)}, f32[4,64,768]{2,1,0:T(8,128)}, u32[]{:S(2)}) copy-start(f32[4,64,768]{2,1,0:T(8,128)} %refs_4_.7) | copy-start | bytes 2359300
  0.7 8.8 %copy-start.3 = (f32[4,64,768]{2,1,0:T(8,128)S(1)}, f32[4,64,768]{2,1,0:T(8,128)}, u32[]{:S(2)}) copy-start(f32[4,64,768]{2,1,0:T(8,128)} %refs_3_.7) | copy-start | bytes 2359300
  0.7 8.8 %copy-start.2 = (f32[4,64,768]{2,1,0:T(8,128)S(1)}, f32[4,64,768]{2,1,0:T(8,128)}, u32[]{:S(2)}) copy-start(f32[4,64,768]{2,1,0:T(8,128)} %refs_2_.7) | copy-start | bytes 2359300
  0.7 8.8 %copy-start.1 = (f32[4,64,768]{2,1,0:T(8,128)S(1)}, f32[4,64,768]{2,1,0:T(8,128)}, u32[]{:S(2)}) copy-start(f32[4,64,768]{2,1,0:T(8,128)} %refs_1_.7) | copy-start | bytes 2359300
  0.7 8.8 %copy-start = (f32[4,64,768]{2,1,0:T(8,128)S(1)}, f32[4,64,768]{2,1,0:T(8,128)}, u32[]{:S(2)}) copy-start(f32[4,64,768]{2,1,0:T(8,128)} %refs_0_.7) | copy-start | bytes 2359300
  0.7 8.8 %copy-start.8 = (f32[64,768]{1,0:T(8,128)S(1)}, f32[64,768]{1,0:T(8,128)}, u32[]{:S(2)}) copy-start(f32[64,768]{1,0:T(8,128)} %refs_8_.7) | copy-start | bytes 589828
  2.4 16.3 %collective-permute-start = (f32[2,24,768]{2,1,0:T(8,128)S(1)}, f32[2,24,768]{2,1,0:T(8,128)S(1)}, u32[]{:S(2)}, u32[]{:S(2)}) collective-permute-start(f32[2,24,768]{2,1,0:T(8,128)S(1)} %get-tuple-element.40), channel_id=1, source_target_pairs={{0,1},{1,0},{8,9},{9,8},{16,17},{17,16},{24,25},{25,24},{32,33},{3... | collective-permute-start | bytes 442376 | tf_op jit(solution)/shard_map/ppermute | solution.py:729
  2.5 16.2 %collective-permute-start.1 = (f32[2,24,768]{2,1,0:T(8,128)S(1)}, f32[2,24,768]{2,1,0:T(8,128)S(1)}, u32[]{:S(2)}, u32[]{:S(2)}) collective-permute-start(f32[2,24,768]{2,1,0:T(8,128)S(1)} %get-tuple-element.41), channel_id=1, source_target_pairs={{1,2},{2,1},{9,10},{10,9},{17,18},{18,17},{25,26},{26,25},{33,34},... | collective-permute-start | bytes 442376 | tf_op jit(solution)/shard_map/ppermute | solution.py:730
  19.0 8.3 %collective-permute-start.3 = (f32[72,128]{1,0:T(8,128)S(1)}, f32[72,128]{1,0:T(8,128)S(1)}, u32[]{:S(2)}, u32[]{:S(2)}) collective-permute-start(f32[72,128]{1,0:T(8,128)S(1)} %get-tuple-element.64), channel_id=1, source_target_pairs={{8,16},{16,8},{24,32},{32,24},{40,48},{48,40},{56,64},{64,56},{72,... | collective-permute-start | bytes 110600 | tf_op jit(solution)/shard_map/ppermute | solution.py:736
  22.0 5.3 %collective-permute-start.2 = (f32[72,128]{1,0:T(8,128)S(1)}, f32[72,128]{1,0:T(8,128)S(1)}, u32[]{:S(2)}, u32[]{:S(2)}) collective-permute-start(f32[72,128]{1,0:T(8,128)S(1)} %get-tuple-element.64), channel_id=1, source_target_pairs={{0,8},{8,0},{16,24},{24,16},{32,40},{40,32},{48,56},{56,48},{64,72... | collective-permute-start | bytes 110600 | tf_op jit(solution)/shard_map/ppermute | solution.py:737

commit v6 on v5

--- a/solution.py
+++ b/solution.py
@@ -20,6 +20,7 @@
 CHUNKS = ROWS // 8
 TALL = ROWS + 16
 FIELDS = 22
+AHEAD = 2
 KINDS = 6
 GROUP = TILE // LEVELS
 F32 = jnp.float32
@@ -302,7 +303,7 @@
             over_e[here, tile(t)] = jnp.zeros((8, TILE), F32)
         return 0
 
-    lax.fori_loop(0, CHUNKS, chunk, 0)
+    lax.fori_loop(0, CHUNKS, chunk, 0, unroll=2)
 
 
 def inner_level(level, fields, outs, known, work, over, over_e, keep):
@@ -448,14 +449,16 @@
     def _():
         inner_metric(fields[6], fields[7], known, over, over_e)
 
-    inner_level(level, fields, outs, known, work, over, over_e, True)
+    @pl.when(jnp.logical_or(level < AHEAD, near_fold()))
+    def _():
+        inner_level(level, fields, outs, known, work, over, over_e, True)
 
 
 def inner(arrays, coriolis):
     out = [pltpu.VMEM((LEVELS, ROWS, COLS), F32)] * 4 + [pltpu.VMEM((ROWS, COLS), F32)] * 9
     done = pl.pallas_call(
         inner_kernel,
-        grid=(LEVELS - 1,),
+        grid=(AHEAD + 1,),
         in_specs=[VMEM] * 9,
         out_specs=[VMEM] * 13,
         out_shape=out,
@@ -567,44 +570,55 @@
         out[level, high, :] = jnp.where(sub >= 6, pltpu.roll(x[1], 2, 0), old[level, high, :])
 
 
-def runs_late():
-    lon, lons = lax.axis_index("lon"), lax.axis_size("lon")
-    top = lax.axis_index("lat") == lax.axis_size("lat") - 1
-    late = jnp.logical_or(lon == lons - 1, lon == lons // 2)
-    return jnp.where(top, lon == 0, late)
-
-
-def last_kernel(*refs):
-    fields, known, over, over_e, outs, work = refs[:9], refs[9:16], refs[16], refs[17], refs[22:26], refs[26:]
-
-    @pl.when(jnp.logical_not(runs_late()))
+def near_fold():
+    return lax.axis_index("lat") >= lax.axis_size("lat") - 2
+
+
+def runs_early():
+    return jnp.logical_and(lax.axis_index("lon") == 0, lax.axis_index("lat") < lax.axis_size("lat") - 1)
+
+
+def middle_kernel(*refs):
+    fields, known, outs, over, over_e, work = refs[:9], refs[9:16], refs[22:26], refs[26], refs[27], refs[28:]
+
+    @pl.when(runs_early())
     def _():
-        inner_level(LEVELS - 1, fields, outs, known, work, over, over_e, False)
+        level = AHEAD + near_fold().astype(jnp.int32)
+        inner_level(level, fields, outs, known, work, over, over_e, True)
 
 
 def rims_kernel(*refs):
-    fields, known, over, over_e, ghosts = refs[:9], refs[9:16], refs[16], refs[17], refs[18]
-    outs, rim_known, spin, rim_over, work = refs[23:27], refs[27], refs[28], refs[29], refs[30:]
+    fields, known, ghosts, outs, over, over_e = refs[:9], refs[9:16], refs[18], refs[23:27], refs[27], refs[28]
+    rim_known, spin, rim_over, work = refs[29], refs[30], refs[31], refs[32:]
     level = pl.program_id(0)
 
-    @pl.when(jnp.logical_and(runs_late(), level == 0))
+    @pl.when(level == 0)
     def _():
-        inner_level(LEVELS - 1, fields, outs, known, work, over, over_e, False)
+        def one(at, _):
+            inner_level(at, fields, outs, known, work, over, over_e, True)
+            return 0
+
+        done = AHEAD + runs_early().astype(jnp.int32) + near_fold().astype(jnp.int32)
+        lax.fori_loop(done, LEVELS, one, 0)
 
     rims_level(level, fields, ghosts, list(zip(outs, outs)), rim_known, spin, rim_over)
 
 
-def last_level(arrays, coriolis, known, outs):
-    return pl.pallas_call(
-        last_kernel,
+WHOLE = [pltpu.VMEM((LEVELS, ROWS, COLS), F32)] * 4 + [pltpu.VMEM((ROWS, COLS), F32)] * 2
+
+
+def middle(arrays, coriolis, known, outs):
+    done = pl.pallas_call(
+        middle_kernel,
         in_specs=[VMEM] * 22,
-        out_specs=[VMEM] * 4,
-        out_shape=[pltpu.VMEM((LEVELS, ROWS, COLS), F32)] * 4,
+        out_specs=[VMEM] * 6,
+        out_shape=WHOLE,
         scratch_shapes=WORK,
-        input_output_aliases={18: 0, 19: 1, 20: 2, 21: 3},
+        input_output_aliases={16: 4, 17: 5, 18: 0, 19: 1, 20: 2, 21: 3},
         compiler_params=PARAMS,
-        name="last_level",
+        name="middle",
     )(*[onto_chip(x) for x in (*arrays, coriolis, *known, *outs)])
+    return done[:4], (*known[:7], *done[4:])
 
 
 def rims(arrays, coriolis, known, ghosts, outs):
@@ -612,22 +626,22 @@
         rims_kernel,
         grid=(LEVELS,),
         in_specs=[VMEM] * 23,
-        out_specs=[VMEM] * 4,
-        out_shape=[pltpu.VMEM((LEVELS, ROWS, COLS), F32)] * 4,
+        out_specs=[VMEM] * 6,
+        out_shape=WHOLE,
         scratch_shapes=[
             pltpu.VMEM((7, 2, 8, COLS), F32),
             pltpu.VMEM((2, 8, COLS), F32),
             pltpu.VMEM((2, 8, COLS), F32),
         ]
         + WORK,
-        input_output_aliases={19: 0, 20: 1, 21: 2, 22: 3},
+        input_output_aliases={16: 4, 17: 5, 19: 0, 20: 1, 21: 2, 22: 3},
         compiler_params=PARAMS,
         name="rims",
-    )(*[onto_chip(x) for x in (*arrays, coriolis, *known, ghosts, *outs)])
+    )(*[onto_chip(x) for x in (*arrays, coriolis, *known, ghosts, *outs)])[:4]
 
 
 def sides_kernel(
-    win, corner, lon_even, lon_odd, temp_in, salt_in, uvel_in, vvel_in,
+    win, corner, lon_odd, lon_even, temp_in, salt_in, uvel_in, vvel_in,
     temp_out, salt_out, uvel_out, vvel_out,
     side, edges, mid_sem, low_sem, high_sem,
 ):
@@ -719,7 +733,7 @@
         ],
         compiler_params=PARAMS,
         name="sides",
-    )(*[onto_chip(x) for x in (win, corner, lon_even, lon_odd, *outs)])
+    )(*[onto_chip(x) for x in (win, corner, lon_odd, lon_even, *outs)])
 
 
 def shards(temp, salt, uvel, vvel, thick, land, east_width, north_width, coriolis):
@@ -730,9 +744,10 @@
     far = lax.ppermute(far, AXES, lat_pairs(lats, lons, 1))
     win, packed = windows(arrays, coriolis)
     outs, known = inner(arrays, coriolis)
-    outs = last_level(arrays, coriolis, known, outs)
     near, far, packed, *outs = lax.optimization_barrier((near, far, packed, *outs))
     packed, ghosts, corner = pack_columns(packed, near, far)
+    outs, known = middle(arrays, coriolis, known, outs)
+    packed, *outs = lax.optimization_barrier((packed, *outs))
     lon_odd = lax.ppermute(packed, AXES, lon_pairs(lats, lons, 1))
     lon_even = lax.ppermute(packed, AXES, lon_pairs(lats, lons, 0))
     outs = rims(arrays, coriolis, known, ghosts, outs)

time: 29.6 us -> 28.9 us (0.976)
  starting transfers between devices: 10.4 us -> 8.51 us
  waiting for transfers between devices: 0.01 us -> 1.58 us
  Pallas kernels: 18.2 us -> 17.8 us
    ppermute x1, starting transfers between devices: 2.98 us -> 0.62 us  [shards(): lon_odd = lax.ppermute(packed, AXES, lon_pairs(lats, lons, 1))]
    ppermute x1, waiting for transfers between devices: 0.01 us -> 1.57 us  [shards(): lon_odd = lax.ppermute(packed, AXES, lon_pairs(lats, lons, 1))]
    ppermute x1, starting transfers between devices: 0.42 us -> 0.9 us  [shards(): lon_even = lax.ppermute(packed, AXES, lon_pairs(lats, lons, 0))]
  transfers between devices with their start and end apart: 4 -> 4, of which waited for: 0 -> 1; matrix products, arithmetic and copies ran while one was open for 0% -> 0% of each run, Pallas kernels for 47% -> 47%
where the time goes in v6:
time: 28.9 us; the launch traced here: 28.8 us
  Pallas kernels  17.8 us (62%)
  starting transfers between devices  8.51 us (29%)
  waiting for transfers between devices  1.58 us (5%)
  between operations  0.86 us (3%)
    pallas_call x1, Pallas kernels, inner(): pl.pallas_call(inner_kernel, grid=(AHEAD + 1,), in_specs=[VMEM] * 9, out_...  7.69 us
    ppermute x1, starting transfers between devices, shards(): far = lax.ppermute(far, AXES, lat_pairs(lats, lons, 1))  6.91 us
    pallas_call x1, Pallas kernels, rims(): pl.pallas_call(rims_kernel, grid=(LEVELS,), in_specs=[VMEM] * 23, out_spe...  4.79 us
    pallas_call x1, Pallas kernels, sides(): pl.pallas_call(sides_kernel, in_specs=[VMEM] * 8, out_specs=[pl.BlockSpec...  2.17 us
    pallas_call x1, Pallas kernels, pack_rows(): pl.pallas_call(rows_kernel, grid=(1,), in_specs=[spec(a, 0) for a in arra...  1.71 us
    ppermute x1, waiting for transfers between devices, shards(): lon_odd = lax.ppermute(packed, AXES, lon_pairs(lats, lons, 1))  1.57 us
    pallas_call x1, Pallas kernels, windows(): pl.pallas_call(windows_kernel, in_specs=[VMEM] * 9, out_specs=[VMEM] * 2,...  1.17 us
    ppermute x1, starting transfers between devices, shards(): lon_even = lax.ppermute(packed, AXES, lon_pairs(lats, lons, 0))  0.9 us
  transfers between devices with their start and end apart: 4, of which 1 were waited for; matrix products, arithmetic and copies ran while one was open for 0% of the time, Pallas kernels for 47%

profile of v6, /device:TPU:38, one launch (start us, length us, event | category | flops | bytes accessed | tf_op | source)
XLA Modules:
  0.0 28.8 jit_solution(1035296597424327697)
XLA Ops:
  0.6 0.0 copy-start.7
  0.6 0.0 copy-start.6
  0.7 0.0 copy-start.5
  0.7 0.0 copy-start.4
  0.7 0.0 copy-start.3
  0.7 0.0 copy-start.2
  0.7 0.0 copy-start.1
  0.7 0.0 copy-start
  0.7 0.0 copy-start.8
  0.7 1.7 %pack_rows.1 = (f32[2,24,768]{2,1,0:T(8,128)S(1)}, f32[2,24,768]{2,1,0:T(8,128)S(1)}) custom-call(f32[4,64,768]{2,1,0:T(8,128)} %refs_0_.7, f32[4,64,768]{2,1,0:T(8,128)} %refs_1_.7, f32[4,64,768]{2,1,0:T(8,128)} %refs_2_.7, f32[4,64,768]{2,1,0:T(8,128)} %refs_3_.7, f32[4,64,768]{2,1,0:T(8,128)} %refs_4_.7, s32[4,64,768]{2,1,0:T(8,128)} %refs_5_.7, ...), custom_call_target="tpu_custom_call" | custom-call | tf_op jit(solution)/shard_map/pack_rows/pallas_call | solution.py:126
  2.4 0.1 collective-permute-start
  2.5 6.9 %collective-permute-start.1 = (f32[2,24,768]{2,1,0:T(8,128)S(1)}, f32[2,24,768]{2,1,0:T(8,128)S(1)}, u32[]{:S(2)}, u32[]{:S(2)}) collective-permute-start(f32[2,24,768]{2,1,0:T(8,128)S(1)} %get-tuple-element.48), channel_id=1, source_target_pairs={{1,2},{2,1},{9,10},{10,9},{17,18},{18,17},{25,26},{26,25},{33,34},... | collective-permute-start | bytes 442376 | tf_op jit(solution)/shard_map/ppermute | solution.py:744
  9.4 0.0 copy-done.7
  9.5 0.0 copy-done.6
  9.5 0.0 copy-done.5
  9.5 0.0 copy-done.4
  9.5 0.0 copy-done.3
  9.5 0.0 copy-done.2
  9.5 0.0 copy-done.1
  9.5 0.0 copy-done
  9.5 0.0 copy-done.8
  9.5 1.2 %windows.1 = (f32[8,64,128]{2,1,0:T(8,128)S(1)}, f32[64,128]{1,0:T(8,128)S(1)}) custom-call(f32[4,64,768]{2,1,0:T(8,128)S(1)} %copy-done, f32[4,64,768]{2,1,0:T(8,128)S(1)} %copy-done.1, f32[4,64,768]{2,1,0:T(8,128)S(1)} %copy-done.2, f32[4,64,768]{2,1,0:T(8,128)S(1)} %copy-done.3, f32[4,64,768]{2,1,0:T(8,128)S(1)} %copy-done.4, ...), custom_call_target="tpu_custom_call" | custom-call | tf_op jit(solution)/shard_map/windows/pallas_call | solution.py:187
  10.7 7.7 %inner.1 = (f32[4,64,768]{2,1,0:T(8,128)S(1)}, f32[4,64,768]{2,1,0:T(8,128)S(1)}, f32[4,64,768]{2,1,0:T(8,128)S(1)}, f32[4,64,768]{2,1,0:T(8,128)S(1)}, f32[64,7...) custom-call(f32[4,64,768]{2,1,0:T(8,128)S(1)} %copy-done, ...), custom_call_target="tpu_custom_call" | custom-call | tf_op jit(solution)/shard_map/inner/pallas_call | solution.py:459
  18.4 0.0 collective-permute-done.near
  18.4 0.0 collective-permute-done.1.far
  18.4 0.3 pack_columns.1
  18.8 0.9 %collective-permute-start.3 = (f32[72,128]{1,0:T(8,128)S(1)}, f32[72,128]{1,0:T(8,128)S(1)}, u32[]{:S(2)}, u32[]{:S(2)}) collective-permute-start(f32[72,128]{1,0:T(8,128)S(1)} %get-tuple-element.76), channel_id=1, source_target_pairs={{0,8},{8,0},{16,24},{24,16},{32,40},{40,32},{48,56},{56,48},{64,72... | collective-permute-start | bytes 110600 | tf_op jit(solution)/shard_map/ppermute | solution.py:752
  19.7 0.6 %collective-permute-start.2 = (f32[72,128]{1,0:T(8,128)S(1)}, f32[72,128]{1,0:T(8,128)S(1)}, u32[]{:S(2)}, u32[]{:S(2)}) collective-permute-start(f32[72,128]{1,0:T(8,128)S(1)} %get-tuple-element.76), channel_id=1, source_target_pairs={{8,16},{16,8},{24,32},{32,24},{40,48},{48,40},{56,64},{64,56},{72,... | collective-permute-start | bytes 110600 | tf_op jit(solution)/shard_map/ppermute | solution.py:751
  20.3 4.8 %rims.1 = (f32[4,64,768]{2,1,0:T(8,128)S(1)}, f32[4,64,768]{2,1,0:T(8,128)S(1)}, f32[4,64,768]{2,1,0:T(8,128)S(1)}, f32[4,64,768]{2,1,0:T(8,128)S(1)}, f32[64,768]{1,0:T(8,128)S(1)}, /*index=5*/f32[64,768]{1,0:T(8,128)S(1)}) custom-call(f32[4,64,768]{2,1,0:T(8,128)S(1)} %copy-done, ...), custom_call_target="tpu_custom_call", output_to_operand_aliasing={{4}: (16, {}), {5}: (17, {}), {0}: (19, {}), {1}: (20, {}),... | custom-call | tf_op jit(solution)/shard_map/rims/pallas_call | solution.py:625
  25.1 0.0 collective-permute-done.3.lon_even
  25.1 1.6 %collective-permute-done.2.lon_odd = f32[72,128]{1,0:T(8,128)S(1)} collective-permute-done((f32[72,128]{1,0:T(8,128)S(1)}, f32[72,128]{1,0:T(8,128)S(1)}, u32[]{:S(2)}, u32[]{:S(2)}) %collective-permute-start.2) | collective-permute-done | bytes 36896 | tf_op jit(solution)/shard_map/ppermute | solution.py:751
  26.6 2.2 %sides.1 = (f32[4,64,768]{2,1,0:T(8,128)}, f32[4,64,768]{2,1,0:T(8,128)}, f32[4,64,768]{2,1,0:T(8,128)}, f32[4,64,768]{2,1,0:T(8,128)}) custom-call(f32[8,64,128]{2,1,0:T(8,128)S(1)} %get-tuple-element.46.win, f32[4,8,128]{2,1,0:T(8,128)S(1)} %get-tuple-element.57.corner, f32[72,128]{1,0:T(8,128)S(1)} %collective-permute-done.2.lon_odd, ...), custom_call_target="tpu_custom_call" | custom-call | tf_op jit(solution)/shard_map/sides/pallas_call | solution.py:722
  (1 shorter events, 0.0 us)
Async XLA Ops:
  0.6 8.8 %copy-start.7 = (f32[64,768]{1,0:T(8,128)S(1)}, f32[64,768]{1,0:T(8,128)}, u32[]{:S(2)}) copy-start(f32[64,768]{1,0:T(8,128)} %refs_7_.7) | copy-start | bytes 589828
  0.6 8.8 %copy-start.6 = (f32[64,768]{1,0:T(8,128)S(1)}, f32[64,768]{1,0:T(8,128)}, u32[]{:S(2)}) copy-start(f32[64,768]{1,0:T(8,128)} %refs_6_.7) | copy-start | bytes 589828
  0.7 8.8 %copy-start.5 = (s32[4,64,768]{2,1,0:T(8,128)S(1)}, s32[4,64,768]{2,1,0:T(8,128)}, u32[]{:S(2)}) copy-start(s32[4,64,768]{2,1,0:T(8,128)} %refs_5_.7) | copy-start | bytes 2359300
  0.7 8.8 %copy-start.4 = (f32[4,64,768]{2,1,0:T(8,128)S(1)}, f32[4,64,768]{2,1,0:T(8,128)}, u32[]{:S(2)}) copy-start(f32[4,64,768]{2,1,0:T(8,128)} %refs_4_.7) | copy-start | bytes 2359300
  0.7 8.8 %copy-start.3 = (f32[4,64,768]{2,1,0:T(8,128)S(1)}, f32[4,64,768]{2,1,0:T(8,128)}, u32[]{:S(2)}) copy-start(f32[4,64,768]{2,1,0:T(8,128)} %refs_3_.7) | copy-start | bytes 2359300
  0.7 8.8 %copy-start.2 = (f32[4,64,768]{2,1,0:T(8,128)S(1)}, f32[4,64,768]{2,1,0:T(8,128)}, u32[]{:S(2)}) copy-start(f32[4,64,768]{2,1,0:T(8,128)} %refs_2_.7) | copy-start | bytes 2359300
  0.7 8.8 %copy-start.1 = (f32[4,64,768]{2,1,0:T(8,128)S(1)}, f32[4,64,768]{2,1,0:T(8,128)}, u32[]{:S(2)}) copy-start(f32[4,64,768]{2,1,0:T(8,128)} %refs_1_.7) | copy-start | bytes 2359300
  0.7 8.8 %copy-start = (f32[4,64,768]{2,1,0:T(8,128)S(1)}, f32[4,64,768]{2,1,0:T(8,128)}, u32[]{:S(2)}) copy-start(f32[4,64,768]{2,1,0:T(8,128)} %refs_0_.7) | copy-start | bytes 2359300
  0.7 8.8 %copy-start.8 = (f32[64,768]{1,0:T(8,128)S(1)}, f32[64,768]{1,0:T(8,128)}, u32[]{:S(2)}) copy-start(f32[64,768]{1,0:T(8,128)} %refs_8_.7) | copy-start | bytes 589828
  2.4 16.0 %collective-permute-start = (f32[2,24,768]{2,1,0:T(8,128)S(1)}, f32[2,24,768]{2,1,0:T(8,128)S(1)}, u32[]{:S(2)}, u32[]{:S(2)}) collective-permute-start(f32[2,24,768]{2,1,0:T(8,128)S(1)} %get-tuple-element.47), channel_id=1, source_target_pairs={{0,1},{1,0},{8,9},{9,8},{16,17},{17,16},{24,25},{25,24},{32,33},{3... | collective-permute-start | bytes 442376 | tf_op jit(solution)/shard_map/ppermute | solution.py:743
  2.5 15.9 %collective-permute-start.1 = (f32[2,24,768]{2,1,0:T(8,128)S(1)}, f32[2,24,768]{2,1,0:T(8,128)S(1)}, u32[]{:S(2)}, u32[]{:S(2)}) collective-permute-start(f32[2,24,768]{2,1,0:T(8,128)S(1)} %get-tuple-element.48), channel_id=1, source_target_pairs={{1,2},{2,1},{9,10},{10,9},{17,18},{18,17},{25,26},{26,25},{33,34},... | collective-permute-start | bytes 442376 | tf_op jit(solution)/shard_map/ppermute | solution.py:744
  18.8 6.3 %collective-permute-start.3 = (f32[72,128]{1,0:T(8,128)S(1)}, f32[72,128]{1,0:T(8,128)S(1)}, u32[]{:S(2)}, u32[]{:S(2)}) collective-permute-start(f32[72,128]{1,0:T(8,128)S(1)} %get-tuple-element.76), channel_id=1, source_target_pairs={{0,8},{8,0},{16,24},{24,16},{32,40},{40,32},{48,56},{56,48},{64,72... | collective-permute-start | bytes 110600 | tf_op jit(solution)/shard_map/ppermute | solution.py:752
  19.7 7.0 %collective-permute-start.2 = (f32[72,128]{1,0:T(8,128)S(1)}, f32[72,128]{1,0:T(8,128)S(1)}, u32[]{:S(2)}, u32[]{:S(2)}) collective-permute-start(f32[72,128]{1,0:T(8,128)S(1)} %get-tuple-element.76), channel_id=1, source_target_pairs={{8,16},{16,8},{24,32},{32,24},{40,48},{48,40},{56,64},{64,56},{72,... | collective-permute-start | bytes 110600 | tf_op jit(solution)/shard_map/ppermute | solution.py:751

commit v7 on v6

--- a/solution.py
+++ b/solution.py
@@ -575,7 +575,7 @@
 
 
 def runs_early():
-    return jnp.logical_and(lax.axis_index("lon") == 0, lax.axis_index("lat") < lax.axis_size("lat") - 1)
+    return jnp.logical_and(lax.axis_index("lon") < 2, lax.axis_index("lat") < lax.axis_size("lat") - 1)
 
 
 def middle_kernel(*refs):
@@ -641,7 +641,7 @@
 
 
 def sides_kernel(
-    win, corner, lon_odd, lon_even, temp_in, salt_in, uvel_in, vvel_in,
+    win, corner, lon_even, lon_odd, temp_in, salt_in, uvel_in, vvel_in,
     temp_out, salt_out, uvel_out, vvel_out,
     side, edges, mid_sem, low_sem, high_sem,
 ):
@@ -733,7 +733,7 @@
         ],
         compiler_params=PARAMS,
         name="sides",
-    )(*[onto_chip(x) for x in (win, corner, lon_odd, lon_even, *outs)])
+    )(*[onto_chip(x) for x in (win, corner, lon_even, lon_odd, *outs)])
 
 
 def shards(temp, salt, uvel, vvel, thick, land, east_width, north_width, coriolis):

time: 28.9 us -> 28.1 us (0.972)
  starting transfers between devices: 8.51 us -> 7.99 us
  waiting for transfers between devices: 1.58 us -> 1.29 us
    ppermute x1, starting transfers between devices: 0.9 us -> 0.01 us  [shards(): lon_even = lax.ppermute(packed, AXES, lon_pairs(lats, lons, 0))]
    ppermute x1, starting transfers between devices: 0.62 us -> 1 us  [shards(): lon_odd = lax.ppermute(packed, AXES, lon_pairs(lats, lons, 1))]
  transfers between devices with their start and end apart: 4 -> 4, of which waited for: 1 -> 1; matrix products, arithmetic and copies ran while one was open for 0% -> 0% of each run, Pallas kernels for 47% -> 49%
where the time goes in v7:
time: 28.1 us; the launch traced here: 28 us
  Pallas kernels  17.8 us (63%)
  starting transfers between devices  7.99 us (28%)
  waiting for transfers between devices  1.29 us (5%)
  between operations  0.86 us (3%)
    pallas_call x1, Pallas kernels, inner(): pl.pallas_call(inner_kernel, grid=(AHEAD + 1,), in_specs=[VMEM] * 9, out_...  7.69 us
    ppermute x1, starting transfers between devices, shards(): far = lax.ppermute(far, AXES, lat_pairs(lats, lons, 1))  6.91 us
    pallas_call x1, Pallas kernels, rims(): pl.pallas_call(rims_kernel, grid=(LEVELS,), in_specs=[VMEM] * 23, out_spe...  4.79 us
    pallas_call x1, Pallas kernels, sides(): pl.pallas_call(sides_kernel, in_specs=[VMEM] * 8, out_specs=[pl.BlockSpec...  2.18 us
    pallas_call x1, Pallas kernels, pack_rows(): pl.pallas_call(rows_kernel, grid=(1,), in_specs=[spec(a, 0) for a in arra...  1.71 us
    ppermute x1, waiting for transfers between devices, shards(): lon_odd = lax.ppermute(packed, AXES, lon_pairs(lats, lons, 1))  1.28 us
    pallas_call x1, Pallas kernels, windows(): pl.pallas_call(windows_kernel, in_specs=[VMEM] * 9, out_specs=[VMEM] * 2,...  1.17 us
    ppermute x1, starting transfers between devices, shards(): lon_odd = lax.ppermute(packed, AXES, lon_pairs(lats, lons, 1))  1 us
  transfers between devices with their start and end apart: 4, of which 1 were waited for; matrix products, arithmetic and copies ran while one was open for 0% of the time, Pallas kernels for 49%

profile of v7, /device:TPU:38, one launch (start us, length us, event | category | flops | bytes accessed | tf_op | source)
XLA Modules:
  0.0 28.0 jit_solution(2759096796389411265)
XLA Ops:
  0.6 0.0 copy-start.7
  0.6 0.0 copy-start.6
  0.7 0.0 copy-start.5
  0.7 0.0 copy-start.4
  0.7 0.0 copy-start.3
  0.7 0.0 copy-start.2
  0.7 0.0 copy-start.1
  0.7 0.0 copy-start
  0.7 0.0 copy-start.8
  0.7 1.7 %pack_rows.1 = (f32[2,24,768]{2,1,0:T(8,128)S(1)}, f32[2,24,768]{2,1,0:T(8,128)S(1)}) custom-call(f32[4,64,768]{2,1,0:T(8,128)} %refs_0_.7, f32[4,64,768]{2,1,0:T(8,128)} %refs_1_.7, f32[4,64,768]{2,1,0:T(8,128)} %refs_2_.7, f32[4,64,768]{2,1,0:T(8,128)} %refs_3_.7, f32[4,64,768]{2,1,0:T(8,128)} %refs_4_.7, s32[4,64,768]{2,1,0:T(8,128)} %refs_5_.7, ...), custom_call_target="tpu_custom_call" | custom-call | tf_op jit(solution)/shard_map/pack_rows/pallas_call | solution.py:126
  2.4 0.1 collective-permute-start
  2.5 6.9 %collective-permute-start.1 = (f32[2,24,768]{2,1,0:T(8,128)S(1)}, f32[2,24,768]{2,1,0:T(8,128)S(1)}, u32[]{:S(2)}, u32[]{:S(2)}) collective-permute-start(f32[2,24,768]{2,1,0:T(8,128)S(1)} %get-tuple-element.48), channel_id=1, source_target_pairs={{1,2},{2,1},{9,10},{10,9},{17,18},{18,17},{25,26},{26,25},{33,34},... | collective-permute-start | bytes 442376 | tf_op jit(solution)/shard_map/ppermute | solution.py:744
  9.4 0.0 copy-done.7
  9.5 0.0 copy-done.6
  9.5 0.0 copy-done.5
  9.5 0.0 copy-done.4
  9.5 0.0 copy-done.3
  9.5 0.0 copy-done.2
  9.5 0.0 copy-done.1
  9.5 0.0 copy-done
  9.5 0.0 copy-done.8
  9.5 1.2 %windows.1 = (f32[8,64,128]{2,1,0:T(8,128)S(1)}, f32[64,128]{1,0:T(8,128)S(1)}) custom-call(f32[4,64,768]{2,1,0:T(8,128)S(1)} %copy-done, f32[4,64,768]{2,1,0:T(8,128)S(1)} %copy-done.1, f32[4,64,768]{2,1,0:T(8,128)S(1)} %copy-done.2, f32[4,64,768]{2,1,0:T(8,128)S(1)} %copy-done.3, f32[4,64,768]{2,1,0:T(8,128)S(1)} %copy-done.4, ...), custom_call_target="tpu_custom_call" | custom-call | tf_op jit(solution)/shard_map/windows/pallas_call | solution.py:187
  10.7 7.7 %inner.1 = (f32[4,64,768]{2,1,0:T(8,128)S(1)}, f32[4,64,768]{2,1,0:T(8,128)S(1)}, f32[4,64,768]{2,1,0:T(8,128)S(1)}, f32[4,64,768]{2,1,0:T(8,128)S(1)}, f32[64,7...) custom-call(f32[4,64,768]{2,1,0:T(8,128)S(1)} %copy-done, ...), custom_call_target="tpu_custom_call" | custom-call | tf_op jit(solution)/shard_map/inner/pallas_call | solution.py:459
  18.4 0.0 collective-permute-done.near
  18.4 0.0 collective-permute-done.1.far
  18.4 0.3 %pack_columns.1 = (f32[72,128]{1,0:T(8,128)S(1)}, f32[4,24,768]{2,1,0:T(8,128)S(1)}, f32[4,8,128]{2,1,0:T(8,128)S(1)}) custom-call(f32[64,128]{1,0:T(8,128)S(1)} %get-tuple-element.54.packed, f32[2,24,768]{2,1,0:T(8,128)S(1)} %collective-permute-done.near, f32[2,24,768]{2,1,0:T(8,128)S(1)} %collective-permute-done.1.far), custom_call_target="tpu_custom_call" | custom-call | tf_op jit(solution)/shard_map/pack_columns/pallas_call | solution.py:233
  18.8 1.0 %collective-permute-start.3 = (f32[72,128]{1,0:T(8,128)S(1)}, f32[72,128]{1,0:T(8,128)S(1)}, u32[]{:S(2)}, u32[]{:S(2)}) collective-permute-start(f32[72,128]{1,0:T(8,128)S(1)} %get-tuple-element.76), channel_id=1, source_target_pairs={{8,16},{16,8},{24,32},{32,24},{40,48},{48,40},{56,64},{64,56},{72,... | collective-permute-start | bytes 110600 | tf_op jit(solution)/shard_map/ppermute | solution.py:751
  19.8 0.0 collective-permute-start.2
  19.8 4.8 %rims.1 = (f32[4,64,768]{2,1,0:T(8,128)S(1)}, f32[4,64,768]{2,1,0:T(8,128)S(1)}, f32[4,64,768]{2,1,0:T(8,128)S(1)}, f32[4,64,768]{2,1,0:T(8,128)S(1)}, f32[64,768]{1,0:T(8,128)S(1)}, /*index=5*/f32[64,768]{1,0:T(8,128)S(1)}) custom-call(f32[4,64,768]{2,1,0:T(8,128)S(1)} %copy-done, ...), custom_call_target="tpu_custom_call", output_to_operand_aliasing={{4}: (16, {}), {5}: (17, {}), {0}: (19, {}), {1}: (20, {}),... | custom-call | tf_op jit(solution)/shard_map/rims/pallas_call | solution.py:625
  24.6 1.3 %collective-permute-done.3.lon_odd = f32[72,128]{1,0:T(8,128)S(1)} collective-permute-done((f32[72,128]{1,0:T(8,128)S(1)}, f32[72,128]{1,0:T(8,128)S(1)}, u32[]{:S(2)}, u32[]{:S(2)}) %collective-permute-start.3) | collective-permute-done | bytes 36896 | tf_op jit(solution)/shard_map/ppermute | solution.py:751
  25.8 0.0 collective-permute-done.2.lon_even
  25.8 2.2 %sides.1 = (f32[4,64,768]{2,1,0:T(8,128)}, f32[4,64,768]{2,1,0:T(8,128)}, f32[4,64,768]{2,1,0:T(8,128)}, f32[4,64,768]{2,1,0:T(8,128)}) custom-call(f32[8,64,128]{2,1,0:T(8,128)S(1)} %get-tuple-element.46.win, f32[4,8,128]{2,1,0:T(8,128)S(1)} %get-tuple-element.57.corner, f32[72,128]{1,0:T(8,128)S(1)} %collective-permute-done.2.lon_even, ...), custom_call_target="tpu_custom_call" | custom-call | tf_op jit(solution)/shard_map/sides/pallas_call | solution.py:722
  (1 shorter events, 0.0 us)
Async XLA Ops:
  0.6 8.8 %copy-start.7 = (f32[64,768]{1,0:T(8,128)S(1)}, f32[64,768]{1,0:T(8,128)}, u32[]{:S(2)}) copy-start(f32[64,768]{1,0:T(8,128)} %refs_7_.7) | copy-start | bytes 589828
  0.6 8.8 %copy-start.6 = (f32[64,768]{1,0:T(8,128)S(1)}, f32[64,768]{1,0:T(8,128)}, u32[]{:S(2)}) copy-start(f32[64,768]{1,0:T(8,128)} %refs_6_.7) | copy-start | bytes 589828
  0.7 8.8 %copy-start.5 = (s32[4,64,768]{2,1,0:T(8,128)S(1)}, s32[4,64,768]{2,1,0:T(8,128)}, u32[]{:S(2)}) copy-start(s32[4,64,768]{2,1,0:T(8,128)} %refs_5_.7) | copy-start | bytes 2359300
  0.7 8.8 %copy-start.4 = (f32[4,64,768]{2,1,0:T(8,128)S(1)}, f32[4,64,768]{2,1,0:T(8,128)}, u32[]{:S(2)}) copy-start(f32[4,64,768]{2,1,0:T(8,128)} %refs_4_.7) | copy-start | bytes 2359300
  0.7 8.8 %copy-start.3 = (f32[4,64,768]{2,1,0:T(8,128)S(1)}, f32[4,64,768]{2,1,0:T(8,128)}, u32[]{:S(2)}) copy-start(f32[4,64,768]{2,1,0:T(8,128)} %refs_3_.7) | copy-start | bytes 2359300
  0.7 8.8 %copy-start.2 = (f32[4,64,768]{2,1,0:T(8,128)S(1)}, f32[4,64,768]{2,1,0:T(8,128)}, u32[]{:S(2)}) copy-start(f32[4,64,768]{2,1,0:T(8,128)} %refs_2_.7) | copy-start | bytes 2359300
  0.7 8.8 %copy-start.1 = (f32[4,64,768]{2,1,0:T(8,128)S(1)}, f32[4,64,768]{2,1,0:T(8,128)}, u32[]{:S(2)}) copy-start(f32[4,64,768]{2,1,0:T(8,128)} %refs_1_.7) | copy-start | bytes 2359300
  0.7 8.8 %copy-start = (f32[4,64,768]{2,1,0:T(8,128)S(1)}, f32[4,64,768]{2,1,0:T(8,128)}, u32[]{:S(2)}) copy-start(f32[4,64,768]{2,1,0:T(8,128)} %refs_0_.7) | copy-start | bytes 2359300
  0.7 8.8 %copy-start.8 = (f32[64,768]{1,0:T(8,128)S(1)}, f32[64,768]{1,0:T(8,128)}, u32[]{:S(2)}) copy-start(f32[64,768]{1,0:T(8,128)} %refs_8_.7) | copy-start | bytes 589828
  2.4 16.0 %collective-permute-start = (f32[2,24,768]{2,1,0:T(8,128)S(1)}, f32[2,24,768]{2,1,0:T(8,128)S(1)}, u32[]{:S(2)}, u32[]{:S(2)}) collective-permute-start(f32[2,24,768]{2,1,0:T(8,128)S(1)} %get-tuple-element.47), channel_id=1, source_target_pairs={{0,1},{1,0},{8,9},{9,8},{16,17},{17,16},{24,25},{25,24},{32,33},{3... | collective-permute-start | bytes 442376 | tf_op jit(solution)/shard_map/ppermute | solution.py:743
  2.5 15.9 %collective-permute-start.1 = (f32[2,24,768]{2,1,0:T(8,128)S(1)}, f32[2,24,768]{2,1,0:T(8,128)S(1)}, u32[]{:S(2)}, u32[]{:S(2)}) collective-permute-start(f32[2,24,768]{2,1,0:T(8,128)S(1)} %get-tuple-element.48), channel_id=1, source_target_pairs={{1,2},{2,1},{9,10},{10,9},{17,18},{18,17},{25,26},{26,25},{33,34},... | collective-permute-start | bytes 442376 | tf_op jit(solution)/shard_map/ppermute | solution.py:744
  18.8 7.1 %collective-permute-start.3 = (f32[72,128]{1,0:T(8,128)S(1)}, f32[72,128]{1,0:T(8,128)S(1)}, u32[]{:S(2)}, u32[]{:S(2)}) collective-permute-start(f32[72,128]{1,0:T(8,128)S(1)} %get-tuple-element.76), channel_id=1, source_target_pairs={{8,16},{16,8},{24,32},{32,24},{40,48},{48,40},{56,64},{64,56},{72,... | collective-permute-start | bytes 110600 | tf_op jit(solution)/shard_map/ppermute | solution.py:751
  19.8 6.1 %collective-permute-start.2 = (f32[72,128]{1,0:T(8,128)S(1)}, f32[72,128]{1,0:T(8,128)S(1)}, u32[]{:S(2)}, u32[]{:S(2)}) collective-permute-start(f32[72,128]{1,0:T(8,128)S(1)} %get-tuple-element.76), channel_id=1, source_target_pairs={{0,8},{8,0},{16,24},{24,16},{32,40},{40,32},{48,56},{56,48},{64,72... | collective-permute-start | bytes 110600 | tf_op jit(solution)/shard_map/ppermute | solution.py:752

commit v8 on v7

--- a/solution.py
+++ b/solution.py
@@ -148,38 +148,34 @@
     return jnp.where(lane < 8, low, pltpu.roll(high, 16, len(low.shape) - 1))
 
 
+def spread(parts):
+    lane = lax.broadcasted_iota(jnp.int32, (ROWS, TILE), 1)
+    whole = parts[0]
+    for level in range(1, len(parts)):
+        whole = jnp.where(lane >= GROUP * level, pltpu.roll(parts[level], GROUP * level, 1), whole)
+    return whole
+
+
 def windows_kernel(temp, salt, uvel, vvel, thick, land, ewid, nwid, cori, win, packed):
     shape = (ROWS, TILE)
-    lane = lax.broadcasted_iota(jnp.int32, shape, 1)
     slot = slot_of(shape)
     ends = (slice(0, TILE), slice(COLS - TILE, COLS))
     total = jnp.zeros(shape, F32)
-
-    def spread(parts):
-        whole = parts[0]
-        for level in range(1, len(parts)):
-            whole = jnp.where(lane >= GROUP * level, pltpu.roll(parts[level], GROUP * level, 1), whole)
-        return whole
 
     def at(kind, level, cut):
         if kind < 4:
             return (temp, salt, uvel, vvel)[kind][level, :, cut]
         if kind == 4:
             return thick[level, :, cut] * land[level, :, cut].astype(F32)
-        if kind == 5:
-            return (ewid, nwid)[level][:, cut]
-        if kind == 6:
-            return land[level, :, cut].astype(F32)
-        return cori[:, cut]
-
-    for kind in range(KINDS + 2):
-        count = (LEVELS, 2, LEVELS, 1)[max(kind - 4, 0)]
+        return (ewid, nwid)[level][:, cut]
+
+    for kind in range(KINDS):
+        count = 2 if kind == 5 else LEVELS
         parts = [join_ends(*[at(kind, level, cut) for cut in ends]) for level in range(count)]
-        cells = spread(parts * LEVELS if count == 1 else parts)
+        cells = spread(parts)
         win[kind] = cells
-        if kind < KINDS:
-            total = jnp.where(slot == 9 + kind, pltpu.roll(cells, 16 + 2 * kind, 1), total)
-            total = jnp.where(slot == kind, pltpu.roll(cells, TILE - 16 + 2 * kind, 1), total)
+        total = jnp.where(slot == 9 + kind, pltpu.roll(cells, 16 + 2 * kind, 1), total)
+        total = jnp.where(slot == kind, pltpu.roll(cells, TILE - 16 + 2 * kind, 1), total)
     packed[...] = total
 
 
@@ -188,7 +184,7 @@
         windows_kernel,
         in_specs=[VMEM] * 9,
         out_specs=[VMEM] * 2,
-        out_shape=[pltpu.VMEM((KINDS + 2, ROWS, TILE), F32), pltpu.VMEM((ROWS, TILE), F32)],
+        out_shape=[pltpu.VMEM((KINDS, ROWS, TILE), F32), pltpu.VMEM((ROWS, TILE), F32)],
         compiler_params=PARAMS,
         name="windows",
     )(*[onto_chip(x) for x in (*arrays, coriolis)])
@@ -589,11 +585,15 @@
 
 def rims_kernel(*refs):
     fields, known, ghosts, outs, over, over_e = refs[:9], refs[9:16], refs[18], refs[23:27], refs[27], refs[28]
-    rim_known, spin, rim_over, work = refs[29], refs[30], refs[31], refs[32:]
+    still, rim_known, spin, rim_over, work = refs[29], refs[30], refs[31], refs[32], refs[33:]
     level = pl.program_id(0)
 
     @pl.when(level == 0)
     def _():
+        ends = (slice(0, TILE), slice(COLS - TILE, COLS))
+        still[0] = spread([join_ends(*[fields[5][at, :, cut].astype(F32) for cut in ends]) for at in range(LEVELS)])
+        still[1] = spread([join_ends(*[fields[8][:, cut] for cut in ends])] * LEVELS)
+
         def one(at, _):
             inner_level(at, fields, outs, known, work, over, over_e, True)
             return 0
@@ -622,12 +622,12 @@
 
 
 def rims(arrays, coriolis, known, ghosts, outs):
-    return pl.pallas_call(
+    done = pl.pallas_call(
         rims_kernel,
         grid=(LEVELS,),
         in_specs=[VMEM] * 23,
-        out_specs=[VMEM] * 6,
-        out_shape=WHOLE,
+        out_specs=[VMEM] * 7,
+        out_shape=WHOLE + [pltpu.VMEM((2, ROWS, TILE), F32)],
         scratch_shapes=[
             pltpu.VMEM((7, 2, 8, COLS), F32),
             pltpu.VMEM((2, 8, COLS), F32),
@@ -637,11 +637,12 @@
         input_output_aliases={16: 4, 17: 5, 19: 0, 20: 1, 21: 2, 22: 3},
         compiler_params=PARAMS,
         name="rims",
-    )(*[onto_chip(x) for x in (*arrays, coriolis, *known, ghosts, *outs)])[:4]
+    )(*[onto_chip(x) for x in (*arrays, coriolis, *known, ghosts, *outs)])
+    return done[:4], done[6]
 
 
 def sides_kernel(
-    win, corner, lon_even, lon_odd, temp_in, salt_in, uvel_in, vvel_in,
+    win, still, corner, lon_even, lon_odd, temp_in, salt_in, uvel_in, vvel_in,
     temp_out, salt_out, uvel_out, vvel_out,
     side, edges, mid_sem, low_sem, high_sem,
 ):
@@ -700,7 +701,7 @@
 
     cells = [extended(kind) for kind in range(4)]
     blank = jnp.zeros((2, TILE), F32)
-    wet, spin = tall(win[KINDS], blank, blank), tall(win[KINDS + 1], blank, blank)
+    wet, spin = tall(still[0], blank, blank), tall(still[1], blank, blank)
     new = patch(cells, extended(4), wet, spin, metric(e, n, lanes, rows), overhead, lanes, rows)
     lane = lax.broadcasted_iota(jnp.int32, (ROWS, TILE), 1)
     for i, x in enumerate(new):
@@ -718,10 +719,10 @@
         high_copy(i).wait()
 
 
-def sides(win, corner, lon_even, lon_odd, outs):
+def sides(win, still, corner, lon_even, lon_odd, outs):
     return pl.pallas_call(
         sides_kernel,
-        in_specs=[VMEM] * 8,
+        in_specs=[VMEM] * 9,
         out_specs=[pl.BlockSpec(memory_space=pltpu.HBM)] * 4,
         out_shape=[jax.ShapeDtypeStruct((LEVELS, ROWS, COLS), F32)] * 4,
         scratch_shapes=[
@@ -733,7 +734,7 @@
         ],
         compiler_params=PARAMS,
         name="sides",
-    )(*[onto_chip(x) for x in (win, corner, lon_even, lon_odd, *outs)])
+    )(*[onto_chip(x) for x in (win, still, corner, lon_even, lon_odd, *outs)])
 
 
 def shards(temp, salt, uvel, vvel, thick, land, east_width, north_width, coriolis):
@@ -750,8 +751,8 @@
     packed, *outs = lax.optimization_barrier((packed, *outs))
     lon_odd = lax.ppermute(packed, AXES, lon_pairs(lats, lons, 1))
     lon_even = lax.ppermute(packed, AXES, lon_pairs(lats, lons, 0))
-    outs = rims(arrays, coriolis, known, ghosts, outs)
-    return tuple(sides(win, corner, lon_even, lon_odd, outs))
+    outs, still = rims(arrays, coriolis, known, ghosts, outs)
+    return tuple(sides(win, still, corner, lon_even, lon_odd, outs))
 
 
 def solution(mesh):

time: 28.1 us -> 27.9 us (level)
  waiting for transfers between devices: 1.29 us -> 0.82 us
    ppermute x1, waiting for transfers between devices: 1.28 us -> 0.81 us  [shards(): lon_odd = lax.ppermute(packed, AXES, lon_pairs(lats, lons, 1))]
where the time goes in v8:
time: 27.9 us; the launch traced here: 27.7 us
  Pallas kernels  17.7 us (63%)
  starting transfers between devices  8.27 us (30%)
  between operations  0.86 us (3%)
  waiting for transfers between devices  0.82 us (3%)
    pallas_call x1, Pallas kernels, inner(): pl.pallas_call(inner_kernel, grid=(AHEAD + 1,), in_specs=[VMEM] * 9, out_...  7.69 us
    ppermute x1, starting transfers between devices, shards(): far = lax.ppermute(far, AXES, lat_pairs(lats, lons, 1))  6.91 us
    pallas_call x1, Pallas kernels, rims(): pl.pallas_call(rims_kernel, grid=(LEVELS,), in_specs=[VMEM] * 23, out_spe...  4.98 us
    pallas_call x1, Pallas kernels, sides(): pl.pallas_call(sides_kernel, in_specs=[VMEM] * 9, out_specs=[pl.BlockSpec...  2.18 us
    pallas_call x1, Pallas kernels, pack_rows(): pl.pallas_call(rows_kernel, grid=(1,), in_specs=[spec(a, 0) for a in arra...  1.71 us
    ppermute x1, starting transfers between devices, shards(): lon_odd = lax.ppermute(packed, AXES, lon_pairs(lats, lons, 1))  1.28 us
    pallas_call x1, Pallas kernels, windows(): pl.pallas_call(windows_kernel, in_specs=[VMEM] * 9, out_specs=[VMEM] * 2,...  0.89 us
    ppermute x1, waiting for transfers between devices, shards(): lon_odd = lax.ppermute(packed, AXES, lon_pairs(lats, lons, 1))  0.81 us
  transfers between devices with their start and end apart: 4, of which 1 were waited for; matrix products, arithmetic and copies ran while one was open for 0% of the time, Pallas kernels for 49%

profile of v8, /device:TPU:38, one launch (start us, length us, event | category | flops | bytes accessed | tf_op | source)
XLA Modules:
  0.0 27.7 jit_solution(7817434294695015464)
XLA Ops:
  0.6 0.0 copy-start.7
  0.6 0.0 copy-start.6
  0.7 0.0 copy-start.5
  0.7 0.0 copy-start.4
  0.7 0.0 copy-start.3
  0.7 0.0 copy-start.2
  0.7 0.0 copy-start.1
  0.7 0.0 copy-start
  0.7 0.0 copy-start.8
  0.7 1.7 %pack_rows.1 = (f32[2,24,768]{2,1,0:T(8,128)S(1)}, f32[2,24,768]{2,1,0:T(8,128)S(1)}) custom-call(f32[4,64,768]{2,1,0:T(8,128)} %refs_0_.7, f32[4,64,768]{2,1,0:T(8,128)} %refs_1_.7, f32[4,64,768]{2,1,0:T(8,128)} %refs_2_.7, f32[4,64,768]{2,1,0:T(8,128)} %refs_3_.7, f32[4,64,768]{2,1,0:T(8,128)} %refs_4_.7, s32[4,64,768]{2,1,0:T(8,128)} %refs_5_.7, ...), custom_call_target="tpu_custom_call" | custom-call | tf_op jit(solution)/shard_map/pack_rows/pallas_call | solution.py:126
  2.4 0.1 collective-permute-start
  2.5 6.9 %collective-permute-start.1 = (f32[2,24,768]{2,1,0:T(8,128)S(1)}, f32[2,24,768]{2,1,0:T(8,128)S(1)}, u32[]{:S(2)}, u32[]{:S(2)}) collective-permute-start(f32[2,24,768]{2,1,0:T(8,128)S(1)} %get-tuple-element.58), channel_id=1, source_target_pairs={{1,2},{2,1},{9,10},{10,9},{17,18},{18,17},{25,26},{26,25},{33,34},... | collective-permute-start | bytes 442376 | tf_op jit(solution)/shard_map/ppermute | solution.py:745
  9.4 0.0 copy-done.7
  9.5 0.0 copy-done.6
  9.5 0.0 copy-done.5
  9.5 0.0 copy-done.4
  9.5 0.0 copy-done.3
  9.5 0.0 copy-done.2
  9.5 0.0 copy-done.1
  9.5 0.0 copy-done
  9.5 0.0 copy-done.8
  9.5 0.9 %windows.1 = (f32[6,64,128]{2,1,0:T(8,128)S(1)}, f32[64,128]{1,0:T(8,128)S(1)}) custom-call(f32[4,64,768]{2,1,0:T(8,128)S(1)} %copy-done, f32[4,64,768]{2,1,0:T(8,128)S(1)} %copy-done.1, f32[4,64,768]{2,1,0:T(8,128)S(1)} %copy-done.2, f32[4,64,768]{2,1,0:T(8,128)S(1)} %copy-done.3, f32[4,64,768]{2,1,0:T(8,128)S(1)} %copy-done.4, ...), custom_call_target="tpu_custom_call" | custom-call | tf_op jit(solution)/shard_map/windows/pallas_call | solution.py:183
  10.4 7.7 %inner.1 = (f32[4,64,768]{2,1,0:T(8,128)S(1)}, f32[4,64,768]{2,1,0:T(8,128)S(1)}, f32[4,64,768]{2,1,0:T(8,128)S(1)}, f32[4,64,768]{2,1,0:T(8,128)S(1)}, f32[64,7...) custom-call(f32[4,64,768]{2,1,0:T(8,128)S(1)} %copy-done, ...), custom_call_target="tpu_custom_call" | custom-call | tf_op jit(solution)/shard_map/inner/pallas_call | solution.py:455
  18.1 0.0 collective-permute-done.near
  18.1 0.0 collective-permute-done.1.far
  18.2 0.3 %pack_columns.1 = (f32[72,128]{1,0:T(8,128)S(1)}, f32[4,24,768]{2,1,0:T(8,128)S(1)}, f32[4,8,128]{2,1,0:T(8,128)S(1)}) custom-call(f32[64,128]{1,0:T(8,128)S(1)} %get-tuple-element.70.packed, f32[2,24,768]{2,1,0:T(8,128)S(1)} %collective-permute-done.near, f32[2,24,768]{2,1,0:T(8,128)S(1)} %collective-permute-done.1.far), custom_call_target="tpu_custom_call" | custom-call | tf_op jit(solution)/shard_map/pack_columns/pallas_call | solution.py:229
  18.5 1.3 %collective-permute-start.3 = (f32[72,128]{1,0:T(8,128)S(1)}, f32[72,128]{1,0:T(8,128)S(1)}, u32[]{:S(2)}, u32[]{:S(2)}) collective-permute-start(f32[72,128]{1,0:T(8,128)S(1)} %get-tuple-element.85), channel_id=1, source_target_pairs={{8,16},{16,8},{24,32},{32,24},{40,48},{48,40},{56,64},{64,56},{72,... | collective-permute-start | bytes 110600 | tf_op jit(solution)/shard_map/ppermute | solution.py:752
  19.8 0.0 collective-permute-start.2
  19.8 5.0 %rims.1 = (f32[4,64,768]{2,1,0:T(8,128)S(1)}, f32[4,64,768]{2,1,0:T(8,128)S(1)}, f32[4,64,768]{2,1,0:T(8,128)S(1)}, f32[4,64,768]{2,1,0:T(8,128)S(1)}, f32[64,76...) custom-call(f32[4,64,768]{2,1,0:T(8,128)S(1)} %copy-done, ...), custom_call_target="tpu_custom_call", output_to_operand_aliasing={{4}: (16, {}), {5}: (17, {}), {0}: (19, {}), {1}: (20, {}),... | custom-call | tf_op jit(solution)/shard_map/rims/pallas_call | solution.py:625
  24.7 0.8 %collective-permute-done.3.lon_odd = f32[72,128]{1,0:T(8,128)S(1)} collective-permute-done((f32[72,128]{1,0:T(8,128)S(1)}, f32[72,128]{1,0:T(8,128)S(1)}, u32[]{:S(2)}, u32[]{:S(2)}) %collective-permute-start.3) | collective-permute-done | bytes 36896 | tf_op jit(solution)/shard_map/ppermute | solution.py:752
  25.5 0.0 collective-permute-done.2.lon_even
  25.6 2.2 %sides.1 = (f32[4,64,768]{2,1,0:T(8,128)}, f32[4,64,768]{2,1,0:T(8,128)}, f32[4,64,768]{2,1,0:T(8,128)}, f32[4,64,768]{2,1,0:T(8,128)}) custom-call(f32[6,64,128]{2,1,0:T(8,128)S(1)} %get-tuple-element.47.win, f32[2,64,128]{2,1,0:T(8,128)S(1)} %get-tuple-element.83.still, f32[4,8,128]{2,1,0:T(8,128)S(1)} %get-tuple-element.84.corner, ...), custom_call_target="tpu_custom_call" | custom-call | tf_op jit(solution)/shard_map/sides/pallas_call | solution.py:723
  (1 shorter events, 0.0 us)
Async XLA Ops:
  0.6 8.8 %copy-start.7 = (f32[64,768]{1,0:T(8,128)S(1)}, f32[64,768]{1,0:T(8,128)}, u32[]{:S(2)}) copy-start(f32[64,768]{1,0:T(8,128)} %refs_7_.7) | copy-start | bytes 589828
  0.6 8.8 %copy-start.6 = (f32[64,768]{1,0:T(8,128)S(1)}, f32[64,768]{1,0:T(8,128)}, u32[]{:S(2)}) copy-start(f32[64,768]{1,0:T(8,128)} %refs_6_.7) | copy-start | bytes 589828
  0.7 8.8 %copy-start.5 = (s32[4,64,768]{2,1,0:T(8,128)S(1)}, s32[4,64,768]{2,1,0:T(8,128)}, u32[]{:S(2)}) copy-start(s32[4,64,768]{2,1,0:T(8,128)} %refs_5_.7) | copy-start | bytes 2359300
  0.7 8.8 %copy-start.4 = (f32[4,64,768]{2,1,0:T(8,128)S(1)}, f32[4,64,768]{2,1,0:T(8,128)}, u32[]{:S(2)}) copy-start(f32[4,64,768]{2,1,0:T(8,128)} %refs_4_.7) | copy-start | bytes 2359300
  0.7 8.8 %copy-start.3 = (f32[4,64,768]{2,1,0:T(8,128)S(1)}, f32[4,64,768]{2,1,0:T(8,128)}, u32[]{:S(2)}) copy-start(f32[4,64,768]{2,1,0:T(8,128)} %refs_3_.7) | copy-start | bytes 2359300
  0.7 8.8 %copy-start.2 = (f32[4,64,768]{2,1,0:T(8,128)S(1)}, f32[4,64,768]{2,1,0:T(8,128)}, u32[]{:S(2)}) copy-start(f32[4,64,768]{2,1,0:T(8,128)} %refs_2_.7) | copy-start | bytes 2359300
  0.7 8.8 %copy-start.1 = (f32[4,64,768]{2,1,0:T(8,128)S(1)}, f32[4,64,768]{2,1,0:T(8,128)}, u32[]{:S(2)}) copy-start(f32[4,64,768]{2,1,0:T(8,128)} %refs_1_.7) | copy-start | bytes 2359300
  0.7 8.8 %copy-start = (f32[4,64,768]{2,1,0:T(8,128)S(1)}, f32[4,64,768]{2,1,0:T(8,128)}, u32[]{:S(2)}) copy-start(f32[4,64,768]{2,1,0:T(8,128)} %refs_0_.7) | copy-start | bytes 2359300
  0.7 8.8 %copy-start.8 = (f32[64,768]{1,0:T(8,128)S(1)}, f32[64,768]{1,0:T(8,128)}, u32[]{:S(2)}) copy-start(f32[64,768]{1,0:T(8,128)} %refs_8_.7) | copy-start | bytes 589828
  2.4 15.7 %collective-permute-start = (f32[2,24,768]{2,1,0:T(8,128)S(1)}, f32[2,24,768]{2,1,0:T(8,128)S(1)}, u32[]{:S(2)}, u32[]{:S(2)}) collective-permute-start(f32[2,24,768]{2,1,0:T(8,128)S(1)} %get-tuple-element.57), channel_id=1, source_target_pairs={{0,1},{1,0},{8,9},{9,8},{16,17},{17,16},{24,25},{25,24},{32,33},{3... | collective-permute-start | bytes 442376 | tf_op jit(solution)/shard_map/ppermute | solution.py:744
  2.5 15.6 %collective-permute-start.1 = (f32[2,24,768]{2,1,0:T(8,128)S(1)}, f32[2,24,768]{2,1,0:T(8,128)S(1)}, u32[]{:S(2)}, u32[]{:S(2)}) collective-permute-start(f32[2,24,768]{2,1,0:T(8,128)S(1)} %get-tuple-element.58), channel_id=1, source_target_pairs={{1,2},{2,1},{9,10},{10,9},{17,18},{18,17},{25,26},{26,25},{33,34},... | collective-permute-start | bytes 442376 | tf_op jit(solution)/shard_map/ppermute | solution.py:745
  18.5 7.1 %collective-permute-start.3 = (f32[72,128]{1,0:T(8,128)S(1)}, f32[72,128]{1,0:T(8,128)S(1)}, u32[]{:S(2)}, u32[]{:S(2)}) collective-permute-start(f32[72,128]{1,0:T(8,128)S(1)} %get-tuple-element.85), channel_id=1, source_target_pairs={{8,16},{16,8},{24,32},{32,24},{40,48},{48,40},{56,64},{64,56},{72,... | collective-permute-start | bytes 110600 | tf_op jit(solution)/shard_map/ppermute | solution.py:752
  19.8 5.8 %collective-permute-start.2 = (f32[72,128]{1,0:T(8,128)S(1)}, f32[72,128]{1,0:T(8,128)S(1)}, u32[]{:S(2)}, u32[]{:S(2)}) collective-permute-start(f32[72,128]{1,0:T(8,128)S(1)} %get-tuple-element.85), channel_id=1, source_target_pairs={{0,8},{8,0},{16,24},{24,16},{32,40},{40,32},{48,56},{56,48},{64,72... | collective-permute-start | bytes 110600 | tf_op jit(solution)/shard_map/ppermute | solution.py:753
